TPU v7x, 768 devices: a whole 4x8x12 slice. The times are simulated.
768 devices in a mesh: sx: 24 (over y_lo, z), sy: 32 (over x, y_hi, core).
Axes of the slice: x: 4, y: 8 (y_hi: 4, y_lo: 2; y = y_hi * 2 + y_lo), z: 12, core: 2. Of those that a mesh axis runs over, the one named last changes fastest.
Arguments:
- right_side: float32 [768, 512, 128], P('sx', 'sy'), may hold values from -48 to 48
- class_map: int32 [384, 256, 32], P('sx', 'sy'), may hold values from 0 to 7
- conductivity_table: float32 [8], replicated, may hold values from 0.2 to 5
- velocity: float32 [3, 768, 512, 128], P(None, 'sx', 'sy'), may hold values from -6 to 6
Outputs:
- potential: float32 [768, 512, 128], P('sx', 'sy')
- velocity_next: float32 [3, 768, 512, 128], P(None, ('sx', 'sy'))
All inputs are finite; a program needn't handle non-finite values.
Results may differ from a plain program's by a relative error of at most 0.0003.
Values sent between devices are 32-bit elements; how exact they have to be, the bound alone decides.
No kernel may reach another device: no remote copies, remote signals or barrier semaphores. Data moves between devices by JAX's collectives and lax.ppermute only.
A program may use at most 32 MiB of HBM per device.

v0:
```python
import jax
import jax.numpy as jnp
from jax import lax
from jax.sharding import PartitionSpec as P

MARGIN = 4
SWEEPS = 5
CLASSES = 8


axial_ratio = 0.0625
coupling = 0.25
highest = lax.Precision.HIGHEST


def with_halo(shard, sides, width):
    for axis, dim in sides:
        peers, length = (lax.axis_size(axis), shard.shape[dim])
        up = [(i, (i + 1) % peers) for i in range(peers - 1)]
        down = [(j, i) for i, j in up]
        last = lax.slice_in_dim(shard, length - width, length, axis=dim)
        initial = lax.slice_in_dim(shard, 0, width, axis=dim)
        before = lax.ppermute(last, axis, up)
        after = lax.ppermute(initial, axis, down)
        shard = jnp.concatenate([before, shard, after], axis=dim)
    return shard


def spatial_pad(grid_field):
    return jnp.pad(grid_field, ((1, 1), (1, 1), (1, 1)))


def axial_pad(grid_field):
    return jnp.pad(grid_field, ((0, 0), (0, 0), (1, 1)))


def coefficients(cond_padded):
    centre = cond_padded[1:-1, 1:-1, 1:-1]
    face_terms = (
        0.5 * (centre + cond_padded[2:, 1:-1, 1:-1]),
        0.5 * (centre + cond_padded[:-2, 1:-1, 1:-1]),
        0.5 * (centre + cond_padded[1:-1, 2:, 1:-1]),
        0.5 * (centre + cond_padded[1:-1, :-2, 1:-1]),
        axial_ratio * 0.5 * (centre + cond_padded[1:-1, 1:-1, 2:]),
        axial_ratio * 0.5 * (centre + cond_padded[1:-1, 1:-1, :-2]),
    )
    diagonal = (
        face_terms[0]
        + face_terms[1]
        + face_terms[2]
        + face_terms[3]
        + face_terms[4]
        + face_terms[5]
    )
    return (face_terms, diagonal)


def apply_operator(face_terms, diagonal, padded):
    centre = padded[1:-1, 1:-1, 1:-1]
    beside = face_terms[0] * padded[2:, 1:-1, 1:-1] + face_terms[1] * padded[:-2, 1:-1, 1:-1]
    beside = (
        beside + face_terms[2] * padded[1:-1, 2:, 1:-1] + face_terms[3] * padded[1:-1, :-2, 1:-1]
    )
    beside = (
        beside + face_terms[4] * padded[1:-1, 1:-1, 2:] + face_terms[5] * padded[1:-1, 1:-1, :-2]
    )
    return diagonal * centre - beside


def margin(grid_field):
    return with_halo(grid_field, (("sx", 0), ("sy", 1)), MARGIN)


def faces_of(grid_field):
    return with_halo(grid_field, (("sx", 0), ("sy", 1)), 1)


def global_sums(partial_terms):
    return lax.psum(jnp.stack(partial_terms), ("sx", "sy"))


def sine_table(lines_count):
    positions = jnp.arange(lines_count, dtype=jnp.int32) + 1
    phase_index = positions[:, None] * positions[None, :] % (2 * (lines_count + 1))
    return jnp.sqrt(2.0 / (lines_count + 1)) * jnp.sin(
        jnp.pi * phase_index.astype(jnp.float32) / (lines_count + 1)
    )


def diffusion_gain(lines_count, cells_side):
    positions = (jnp.arange(lines_count, dtype=jnp.int32) + 1).astype(jnp.float32)
    half_sine = jnp.sin(0.5 * jnp.pi * positions / (lines_count + 1))
    stiffness = 8.0 * cells_side * cells_side * half_sine * half_sine
    return (1.0 - stiffness) / (1.0 + stiffness)


def per_device(right_side, class_map, conductivity_table, velocity):
    cells_x, cells_y, cells_z = right_side.shape
    picked = (class_map[..., None] == jnp.arange(CLASSES, dtype=jnp.int32)).astype(jnp.float32)
    block_values = jnp.sum(picked * conductivity_table, axis=-1)
    conductivity = jnp.repeat(jnp.repeat(jnp.repeat(block_values, 2, axis=0), 2, axis=1), 4, axis=2)
    cond_wide = margin(conductivity)
    local_faces, local_diagonal = coefficients(spatial_pad(cond_wide))
    inside = (cond_wide > 0.0).astype(jnp.float32)
    inverse = inside / (local_diagonal + (1.0 - inside))
    near_cells = cond_wide[MARGIN - 1 : MARGIN + cells_x + 1, MARGIN - 1 : MARGIN + cells_y + 1, :]
    own_faces, own_diagonal = coefficients(axial_pad(near_cells))

    def operate(padded_plane):
        return apply_operator(own_faces, own_diagonal, axial_pad(padded_plane))

    def precondition(residual):
        region = margin(residual)
        update = region * inverse
        for sweep_index in range(SWEEPS - 1):
            update = (
                update
                + (region - apply_operator(local_faces, local_diagonal, spatial_pad(update)))
                * inverse
            )
        return update[MARGIN : MARGIN + cells_x, MARGIN : MARGIN + cells_y, :]

    residual = right_side
    first_dir = precondition(residual)
    first_wide = faces_of(first_dir)
    image_one = operate(first_wide)
    totals = global_sums([jnp.sum(residual * image_one), jnp.sum(image_one * image_one)])
    weight_one = totals[1]
    alpha_one = totals[0] / weight_one
    residual = residual - alpha_one * image_one
    second_dir = precondition(residual)
    second_wide = faces_of(second_dir)
    image_two = operate(second_wide)
    beta_two = global_sums([jnp.sum(image_two * image_one)])[0] / weight_one
    image_two = image_two - beta_two * image_one
    totals = global_sums([jnp.sum(residual * image_two), jnp.sum(image_two * image_two)])
    alpha_two = totals[0] / totals[1]
    second_dir = second_dir - beta_two * first_dir
    potential = alpha_one * first_dir
    potential = potential + alpha_two * second_dir
    potential_wide = faces_of(potential)
    grad_x = 0.5 * (potential_wide[2:, 1:-1, :] - potential_wide[:-2, 1:-1, :])
    grad_y = 0.5 * (potential_wide[1:-1, 2:, :] - potential_wide[1:-1, :-2, :])
    lines_count = cells_y * lax.axis_size("sy")
    sine_rows = sine_table(lines_count)
    line_gain = diffusion_gain(lines_count, cells_y)[:, None]
    force_x = conductivity * (-grad_y - velocity[0])
    force_y = conductivity * (grad_x - velocity[1])
    moved_velocity = jnp.stack(
        [velocity[0] + coupling * force_x, velocity[1] + coupling * force_y, velocity[2]]
    )
    sine_coeffs = jnp.matmul(
        sine_rows,
        lax.all_to_all(moved_velocity, "sy", split_axis=1, concat_axis=2, tiled=True),
        precision=highest,
    )
    velocity_next = jnp.matmul(sine_rows, sine_coeffs * line_gain, precision=highest)
    return (potential, velocity_next)


def solution(mesh):
    return jax.shard_map(
        per_device,
        mesh=mesh,
        in_specs=(P("sx", "sy", None), P("sx", "sy", None), P(), P(None, "sx", "sy", None)),
        out_specs=(P("sx", "sy", None), P(None, ("sx", "sy"), None, None)),
        check_vma=False,
    )
```

profile of v0, /device:TPU:1, one launch (start us, length us, event | category | flops | bytes accessed | tf_op | source)
XLA Modules:
  0.0 509.7 jit_solution(5255281795072225022)
XLA Ops:
  0.6 1.1 select_reduce_fusion
  2.1 1.3 collective-permute-start
  3.6 5.5 %collective-permute-start.1 = (f32[4,16,128]{2,1,0:T(8,128)S(1)}, f32[4,16,128]{2,1,0:T(8,128)S(1)}, u32[]{:S(2)}, u32[]{:S(2)}) collective-permute-start(f32[4,16,128]{2,1,0:T(8,128)S(1)} %copy.248), channel_id=1, source_target_pairs={{0,32},{32,64},{64,96},{96,128},{128,160},{160,192},{192,224},{224... | collective-permute-start | bytes 98312 | tf_op jit(solution)/shard_map/ppermute | solution.py:23
  9.1 4.0 collective-permute-start.4
  13.1 1.3 collective-permute-start.5
  15.3 9.4 %collective-permute-start.2 = (f32[40,4,128]{2,1,0:T(4,128)S(1)}, f32[40,4,128]{2,1,0:T(4,128)S(1)}, u32[]{:S(2)}, u32[]{:S(2)}) collective-permute-start(f32[40,4,128]{2,1,0:T(4,128)S(1)} %get-tuple-element.40), channel_id=1, source_target_pairs={{1,0},{2,1},{3,2},{4,3},{5,4},{6,5},{7,6},{8,7},{9,8},{10,9},{11,1... | collective-permute-start | bytes 245768 | tf_op jit(solution)/shard_map/ppermute | solution.py:24
  24.8 1.9 collective-permute-start.3
  26.8 1.9 collective-permute-start.6
  28.7 2.4 collective-permute-start.7
  31.3 4.1 collective-permute-done.7
  35.4 1.6 fusion.213
  39.4 1.3 collective-permute-start.8
  40.7 4.9 collective-permute-start.9
  46.4 2.1 collective-permute-start.10
  48.5 4.5 collective-permute-start.11
  53.1 0.8 collective-permute-done.11
  54.4 1.9 multiply_reduce_fusion.4
  56.3 2.0 pad_maximum_fusion.51
  58.3 125.3 %psum.21 = f32[2]{0:T(128)} all-reduce(f32[2]{0:T(128)} %pad_maximum_fusion.51), channel_id=1, replica_groups=mesh['sx'=24,'sy'=32] {'sx','sy'}, use_global_device_ids=true, to_apply=%region_3.4 | all-reduce | flops 2 | bytes 16 | tf_op jit(solution)/shard_map/psum | solution.py:79
  183.6 1.4 fusion.231
  186.3 1.1 multiply_subtract_fusion.1
  187.4 3.1 collective-permute-start.12
  190.5 1.3 collective-permute-start.13
  191.8 3.3 collective-permute-done.13
  195.2 1.9 collective-permute-start.14
  197.2 3.4 collective-permute-start.15
  200.6 3.3 collective-permute-done.15
  206.2 1.4 collective-permute-start.16
  207.6 4.0 collective-permute-start.17
  212.4 1.9 collective-permute-start.18
  214.3 4.5 collective-permute-start.19
  218.9 0.8 collective-permute-done.19
  220.2 1.1 multiply_reduce_fusion.2
  221.4 118.5 %psum.22 = f32[1]{0:T(128)} all-reduce(f32[1]{0:T(128)} %bitcast.12), channel_id=1, replica_groups=mesh['sx'=24,'sy'=32] {'sx','sy'}, use_global_device_ids=true, to_apply=%region_5.6 | all-reduce | flops 1 | bytes 8 | tf_op jit(solution)/shard_map/psum | solution.py:79
  342.0 1.3 pad_maximum_fusion.52
  343.3 105.5 %psum.23 = f32[2]{0:T(128)S(1)} all-reduce(f32[2]{0:T(128)S(1)} %pad_maximum_fusion.52), channel_id=1, replica_groups=mesh['sx'=24,'sy'=32] {'sx','sy'}, use_global_device_ids=true, to_apply=%region_8.9 | all-reduce | flops 2 | bytes 16 | tf_op jit(solution)/shard_map/psum | solution.py:79
  450.7 1.1 multiply_add_fusion
  451.8 2.8 collective-permute-start.20
  454.7 1.3 collective-permute-start.21
  456.0 3.1 collective-permute-done.21
  459.1 4.0 collective-permute-start.22
  463.1 2.6 collective-permute-start.23
  465.7 0.8 collective-permute-done.23
  466.8 0.9 copy.258
  467.8 7.4 %all-to-all-start = ((f32[3,32,16,128]{3,2,0,1:T(8,128)}), f32[3,32,16,128]{3,2,0,1:T(8,128)S(1)}, u32[]{:S(2)}, u32[]{:S(2)}) async-start(f32[3,32,16,128]{3,2,0,1:T(8,128)} %copy.258), calls=%async_computation | async-start | bytes 1572864 | tf_op jit(solution)/shard_map/all_to_all | solution.py:154
  475.2 20.8 %all-to-all-done = f32[3,32,16,128]{3,2,0,1:T(8,128)S(1)} async-done(((f32[3,32,16,128]{3,2,0,1:T(8,128)}), f32[3,32,16,128]{3,2,0,1:T(8,128)S(1)}, u32[]{:S(2)}, u32[]{:S(2)}) %all-to-all-start) | async-done | bytes 786464 | tf_op jit(solution)/shard_map/all_to_all | solution.py:154
  496.1 5.8 %fusion.1 = f32[3,512,128]{2,1,0:T(8,128)S(1)} fusion(f32[3,512,128]{2,1,0:T(8,128)S(1)} %bitcast.52, s32[512]{0:T(512)S(1)} %iota_add_fusion, f32[512]{0:T(512)S(1)} %add_divide_fusion), kind=kOutput, calls=%fused_computation.58 | convolution fusion | flops 1210777600 | bytes 1576960 | tf_op jit(solution)/shard_map/dot_general | solution.py:152
  502.0 7.8 %convolution_bitcast_fusion = f32[3,1,512,128]{3,2,1,0:T(8,128)} fusion(f32[3,512,128]{2,1,0:T(8,128)S(1)} %fusion.1, s32[512]{0:T(512)S(1)} %iota_add_fusion), kind=kOutput, calls=%fused_computation.55 | convolution fusion | flops 1210580992 | bytes 1574912 | tf_op jit(solution)/shard_map/dot_general | solution.py:157
  (111 shorter events, 10.4 us)
Async XLA Ops:
  0.6 8.5 %copy-start.8 = (f32[32,16,128]{2,1,0:T(8,128)S(1)}, f32[32,16,128]{2,1,0:T(8,128)}, u32[]{:S(2)}) copy-start(f32[32,16,128]{2,1,0:T(8,128)} %param.4) | copy-start | bytes 786436
  2.1 13.2 %collective-permute-start = (f32[4,16,128]{2,1,0:T(8,128)S(1)}, f32[4,16,128]{2,1,0:T(8,128)S(1)}, u32[]{:S(2)}, u32[]{:S(2)}) collective-permute-start(f32[4,16,128]{2,1,0:T(8,128)S(1)} %copy.244), channel_id=1, source_target_pairs={{32,0},{64,32},{96,64},{128,96},{160,128},{192,160},{224,192},{256... | collective-permute-start | bytes 98312 | tf_op jit(solution)/shard_map/ppermute | solution.py:24
  3.6 11.6 %collective-permute-start.1 = (f32[4,16,128]{2,1,0:T(8,128)S(1)}, f32[4,16,128]{2,1,0:T(8,128)S(1)}, u32[]{:S(2)}, u32[]{:S(2)}) collective-permute-start(f32[4,16,128]{2,1,0:T(8,128)S(1)} %copy.248), channel_id=1, source_target_pairs={{0,32},{32,64},{64,96},{96,128},{128,160},{160,192},{192,224},{224... | collective-permute-start | bytes 98312 | tf_op jit(solution)/shard_map/ppermute | solution.py:23
  9.1 17.6 %collective-permute-start.4 = (f32[4,16,128]{2,1,0:T(8,128)S(1)}, f32[4,16,128]{2,1,0:T(8,128)S(1)}, u32[]{:S(2)}, u32[]{:S(2)}) collective-permute-start(f32[4,16,128]{2,1,0:T(8,128)S(1)} %get-tuple-element.54), channel_id=1, source_target_pairs={{0,32},{32,64},{64,96},{96,128},{128,160},{160,192},{192,224},{224... | collective-permute-start | bytes 98312 | tf_op jit(solution)/shard_map/ppermute | solution.py:23
  13.1 13.6 %collective-permute-start.5 = (f32[4,16,128]{2,1,0:T(8,128)S(1)}, f32[4,16,128]{2,1,0:T(8,128)S(1)}, u32[]{:S(2)}, u32[]{:S(2)}) collective-permute-start(f32[4,16,128]{2,1,0:T(8,128)S(1)} %get-tuple-element.53), channel_id=1, source_target_pairs={{32,0},{64,32},{96,64},{128,96},{160,128},{192,160},{224,192},{256... | collective-permute-start | bytes 98312 | tf_op jit(solution)/shard_map/ppermute | solution.py:24
  15.2 16.0 %copy-start.2 = (f32[32,16,128]{2,1,0:T(8,128)}, f32[32,16,128]{2,1,0:T(8,128)S(1)}, u32[]{:S(2)}) copy-start(f32[32,16,128]{2,1,0:T(8,128)S(1)} %copy.246) | copy-start | bytes 786436
  15.3 16.0 %copy-start.17 = (f32[4,16,128]{2,1,0:T(8,128)}, f32[4,16,128]{2,1,0:T(8,128)S(1)}, u32[]{:S(2)}) copy-start(f32[4,16,128]{2,1,0:T(8,128)S(1)} %collective-permute-done.1) | copy-start | bytes 98308
  15.3 15.8 %collective-permute-start.2 = (f32[40,4,128]{2,1,0:T(4,128)S(1)}, f32[40,4,128]{2,1,0:T(4,128)S(1)}, u32[]{:S(2)}, u32[]{:S(2)}) collective-permute-start(f32[40,4,128]{2,1,0:T(4,128)S(1)} %get-tuple-element.40), channel_id=1, source_target_pairs={{1,0},{2,1},{3,2},{4,3},{5,4},{6,5},{7,6},{8,7},{9,8},{10,9},{11,1... | collective-permute-start | bytes 245768 | tf_op jit(solution)/shard_map/ppermute | solution.py:24
  24.8 6.4 %collective-permute-start.3 = (f32[40,4,128]{2,1,0:T(4,128)S(1)}, f32[40,4,128]{2,1,0:T(4,128)S(1)}, u32[]{:S(2)}, u32[]{:S(2)}) collective-permute-start(f32[40,4,128]{2,1,0:T(4,128)S(1)} %get-tuple-element.39), channel_id=1, source_target_pairs={{0,1},{1,2},{2,3},{3,4},{4,5},{5,6},{6,7},{7,8},{8,9},{9,10},{10,1... | collective-permute-start | bytes 245768 | tf_op jit(solution)/shard_map/ppermute | solution.py:23
  26.8 4.5 collective-permute-start.6
  28.7 6.7 %collective-permute-start.7 = (f32[40,4,128]{2,1,0:T(4,128)S(1)}, f32[40,4,128]{2,1,0:T(4,128)S(1)}, u32[]{:S(2)}, u32[]{:S(2)}) collective-permute-start(f32[40,4,128]{2,1,0:T(4,128)S(1)} %get-tuple-element.42), channel_id=1, source_target_pairs={{1,0},{2,1},{3,2},{4,3},{5,4},{6,5},{7,6},{8,7},{9,8},{10,9},{11,1... | collective-permute-start | bytes 245768 | tf_op jit(solution)/shard_map/ppermute | solution.py:24
  31.2 23.1 %copy-start.14 = (f32[40,4,128]{2,1,0:T(4,128)}, f32[40,4,128]{2,1,0:T(4,128)S(1)}, u32[]{:S(2)}) copy-start(f32[40,4,128]{2,1,0:T(4,128)S(1)} %collective-permute-done.3) | copy-start | bytes 245764
  39.3 15.0 %copy-start.11 = (f32[40,24,128]{2,1,0:T(8,128)}, f32[40,24,128]{2,1,0:T(8,128)S(1)}, u32[]{:S(2)}) copy-start(f32[40,24,128]{2,1,0:T(8,128)S(1)} %fusion.92) | copy-start | bytes 1474564
  39.4 6.2 %collective-permute-start.8 = (f32[1,16,128]{2,1,0:T(8,128)S(1)}, f32[1,16,128]{2,1,0:T(8,128)S(1)}, u32[]{:S(2)}, u32[]{:S(2)}) collective-permute-start(f32[1,16,128]{2,1,0:T(8,128)S(1)} %get-tuple-element.36), channel_id=1, source_target_pairs={{32,0},{64,32},{96,64},{128,96},{160,128},{192,160},{224,192},{256... | collective-permute-start | bytes 24584 | tf_op jit(solution)/shard_map/ppermute | solution.py:24
  40.7 5.7 %collective-permute-start.9 = (f32[1,16,128]{2,1,0:T(8,128)S(1)}, f32[1,16,128]{2,1,0:T(8,128)S(1)}, u32[]{:S(2)}, u32[]{:S(2)}) collective-permute-start(f32[1,16,128]{2,1,0:T(8,128)S(1)} %get-tuple-element.35), channel_id=1, source_target_pairs={{0,32},{32,64},{64,96},{96,128},{128,160},{160,192},{192,224},{224... | collective-permute-start | bytes 24584 | tf_op jit(solution)/shard_map/ppermute | solution.py:23
  46.4 8.0 %copy-start.3 = (f32[32,16,128]{2,1,0:T(8,128)S(1)}, f32[32,16,128]{2,1,0:T(8,128)}, u32[]{:S(2)}) copy-start(f32[32,16,128]{2,1,0:T(8,128)} %copy-done.2) | copy-start | bytes 786436
  46.4 8.0 %copy-start.9 = (f32[32,16,128]{2,1,0:T(8,128)S(1)}, f32[32,16,128]{2,1,0:T(8,128)}, u32[]{:S(2)}) copy-start(f32[32,16,128]{2,1,0:T(8,128)} %param.4) | copy-start | bytes 786436
  46.4 8.0 %copy-start.18 = (f32[4,16,128]{2,1,0:T(8,128)S(1)}, f32[4,16,128]{2,1,0:T(8,128)}, u32[]{:S(2)}) copy-start(f32[4,16,128]{2,1,0:T(8,128)} %copy-done.17) | copy-start | bytes 98308
  46.4 6.7 %collective-permute-start.10 = (f32[34,1,128]{2,1,0:T(1,128)S(1)}, f32[34,1,128]{2,1,0:T(1,128)S(1)}, u32[]{:S(2)}, u32[]{:S(2)}) collective-permute-start(f32[34,1,128]{2,1,0:T(1,128)S(1)} %get-tuple-element.48), channel_id=1, source_target_pairs={{1,0},{2,1},{3,2},{4,3},{5,4},{6,5},{7,6},{8,7},{9,8},{10,9},{11,1... | collective-permute-start | bytes 52232 | tf_op jit(solution)/shard_map/ppermute | solution.py:24
  48.5 5.4 %collective-permute-start.11 = (f32[34,1,128]{2,1,0:T(1,128)S(1)}, f32[34,1,128]{2,1,0:T(1,128)S(1)}, u32[]{:S(2)}, u32[]{:S(2)}) collective-permute-start(f32[34,1,128]{2,1,0:T(1,128)S(1)} %get-tuple-element.47), channel_id=1, source_target_pairs={{0,1},{1,2},{2,3},{3,4},{4,5},{5,6},{6,7},{7,8},{8,9},{9,10},{10,1... | collective-permute-start | bytes 52232 | tf_op jit(solution)/shard_map/ppermute | solution.py:23
  53.1 3.2 copy-start.6
  187.4 18.2 %copy-start = (f32[32,16,128]{2,1,0:T(8,128)}, f32[32,16,128]{2,1,0:T(8,128)S(1)}, u32[]{:S(2)}) copy-start(f32[32,16,128]{2,1,0:T(8,128)S(1)} %multiply_subtract_fusion.1) | copy-start | bytes 786436
  187.4 4.4 collective-permute-start.12
  190.5 4.7 collective-permute-start.13
  195.2 5.3 %collective-permute-start.14 = (f32[40,4,128]{2,1,0:T(4,128)S(1)}, f32[40,4,128]{2,1,0:T(4,128)S(1)}, u32[]{:S(2)}, u32[]{:S(2)}) collective-permute-start(f32[40,4,128]{2,1,0:T(4,128)S(1)} %get-tuple-element.37), channel_id=1, source_target_pairs={{0,1},{1,2},{2,3},{3,4},{4,5},{5,6},{6,7},{7,8},{8,9},{9,10},{10,1... | collective-permute-start | bytes 245768 | tf_op jit(solution)/shard_map/ppermute | solution.py:23
  197.2 6.7 %collective-permute-start.15 = (f32[40,4,128]{2,1,0:T(4,128)S(1)}, f32[40,4,128]{2,1,0:T(4,128)S(1)}, u32[]{:S(2)}, u32[]{:S(2)}) collective-permute-start(f32[40,4,128]{2,1,0:T(4,128)S(1)} %get-tuple-element.38), channel_id=1, source_target_pairs={{1,0},{2,1},{3,2},{4,3},{5,4},{6,5},{7,6},{8,7},{9,8},{10,9},{11,1... | collective-permute-start | bytes 245768 | tf_op jit(solution)/shard_map/ppermute | solution.py:24
  206.1 15.3 %copy-start.13 = (f32[40,24,128]{2,1,0:T(8,128)}, f32[40,24,128]{2,1,0:T(8,128)S(1)}, u32[]{:S(2)}) copy-start(f32[40,24,128]{2,1,0:T(8,128)S(1)} %fusion.152) | copy-start | bytes 1474564
  206.1 14.1 %copy-start.4 = (f32[32,16,128]{2,1,0:T(8,128)S(1)}, f32[32,16,128]{2,1,0:T(8,128)}, u32[]{:S(2)}) copy-start(f32[32,16,128]{2,1,0:T(8,128)} %copy-done.2) | copy-start | bytes 786436
  206.1 14.1 %copy-start.5 = (f32[32,16,128]{2,1,0:T(8,128)S(1)}, f32[32,16,128]{2,1,0:T(8,128)}, u32[]{:S(2)}) copy-start(f32[32,16,128]{2,1,0:T(8,128)} %get-tuple-element.22) | copy-start | bytes 786436
  206.1 14.1 %copy-start.7 = (f32[34,18,128]{2,1,0:T(8,128)S(1)}, f32[34,18,128]{2,1,0:T(8,128)}, u32[]{:S(2)}) copy-start(f32[34,18,128]{2,1,0:T(8,128)} %copy-done.6) | copy-start | bytes 940036
  206.1 14.1 %copy-start.15 = (f32[40,4,128]{2,1,0:T(4,128)S(1)}, f32[40,4,128]{2,1,0:T(4,128)}, u32[]{:S(2)}) copy-start(f32[40,4,128]{2,1,0:T(4,128)} %copy-done.14) | copy-start | bytes 245764
  206.1 14.1 %copy-start.19 = (f32[4,16,128]{2,1,0:T(8,128)S(1)}, f32[4,16,128]{2,1,0:T(8,128)}, u32[]{:S(2)}) copy-start(f32[4,16,128]{2,1,0:T(8,128)} %copy-done.17) | copy-start | bytes 98308
  206.2 5.5 %collective-permute-start.16 = (f32[1,16,128]{2,1,0:T(8,128)S(1)}, f32[1,16,128]{2,1,0:T(8,128)S(1)}, u32[]{:S(2)}, u32[]{:S(2)}) collective-permute-start(f32[1,16,128]{2,1,0:T(8,128)S(1)} %get-tuple-element.34), channel_id=1, source_target_pairs={{32,0},{64,32},{96,64},{128,96},{160,128},{192,160},{224,192},{256... | collective-permute-start | bytes 24584 | tf_op jit(solution)/shard_map/ppermute | solution.py:24
  207.6 4.8 collective-permute-start.17
  212.4 6.5 %collective-permute-start.18 = (f32[34,1,128]{2,1,0:T(1,128)S(1)}, f32[34,1,128]{2,1,0:T(1,128)S(1)}, u32[]{:S(2)}, u32[]{:S(2)}) collective-permute-start(f32[34,1,128]{2,1,0:T(1,128)S(1)} %get-tuple-element.46), channel_id=1, source_target_pairs={{1,0},{2,1},{3,2},{4,3},{5,4},{6,5},{7,6},{8,7},{9,8},{10,9},{11,1... | collective-permute-start | bytes 52232 | tf_op jit(solution)/shard_map/ppermute | solution.py:24
  214.3 5.4 %collective-permute-start.19 = (f32[34,1,128]{2,1,0:T(1,128)S(1)}, f32[34,1,128]{2,1,0:T(1,128)S(1)}, u32[]{:S(2)}, u32[]{:S(2)}) collective-permute-start(f32[34,1,128]{2,1,0:T(1,128)S(1)} %get-tuple-element.45), channel_id=1, source_target_pairs={{0,1},{1,2},{2,3},{3,4},{4,5},{5,6},{6,7},{7,8},{8,9},{9,10},{10,1... | collective-permute-start | bytes 52232 | tf_op jit(solution)/shard_map/ppermute | solution.py:23
  220.2 121.0 %copy-start.1 = (f32[32,16,128]{2,1,0:T(8,128)S(1)}, f32[32,16,128]{2,1,0:T(8,128)}, u32[]{:S(2)}) copy-start(f32[32,16,128]{2,1,0:T(8,128)} %copy-done) | copy-start | bytes 786436
  220.2 230.5 %copy-start.12 = (f32[40,24,128]{2,1,0:T(8,128)S(1)}, f32[40,24,128]{2,1,0:T(8,128)}, u32[]{:S(2)}) copy-start(f32[40,24,128]{2,1,0:T(8,128)} %copy-done.11) | copy-start | bytes 1474564
  341.2 125.4 %copy-start.16 = (f32[3,32,16,128]{3,2,1,0:T(8,128)S(1)}, f32[3,32,16,128]{3,2,1,0:T(8,128)}, u32[]{:S(2)}) copy-start(f32[3,32,16,128]{3,2,1,0:T(8,128)} %param.7) | copy-start | bytes 2359300
  451.8 15.0 %copy-start.10 = (f32[32,16,128]{2,1,0:T(8,128)}, f32[32,16,128]{2,1,0:T(8,128)S(1)}, u32[]{:S(2)}) copy-start(f32[32,16,128]{2,1,0:T(8,128)S(1)} %multiply_add_fusion) | copy-start | bytes 786436
  451.8 4.1 collective-permute-start.20
  454.7 4.4 collective-permute-start.21
  459.1 6.6 %collective-permute-start.22 = (f32[34,1,128]{2,1,0:T(1,128)S(1)}, f32[34,1,128]{2,1,0:T(1,128)S(1)}, u32[]{:S(2)}, u32[]{:S(2)}) collective-permute-start(f32[34,1,128]{2,1,0:T(1,128)S(1)} %get-tuple-element.43), channel_id=1, source_target_pairs={{1,0},{2,1},{3,2},{4,3},{5,4},{6,5},{7,6},{8,7},{9,8},{10,9},{11,1... | collective-permute-start | bytes 52232 | tf_op jit(solution)/shard_map/ppermute | solution.py:24
  463.1 3.7 slice-start
  463.1 3.4 collective-permute-start.23
  467.8 28.3 %all-to-all-start = ((f32[3,32,16,128]{3,2,0,1:T(8,128)}), f32[3,32,16,128]{3,2,0,1:T(8,128)S(1)}, u32[]{:S(2)}, u32[]{:S(2)}) async-start(f32[3,32,16,128]{3,2,0,1:T(8,128)} %copy.258), calls=%async_computation | async-start | bytes 1572864 | tf_op jit(solution)/shard_map/all_to_all | solution.py:154
where the time goes:
time: 514 us; the launch traced here: 510 us
  blocking collectives  349 us (68%)
  starting transfers between devices  80.2 us (16%)
  waiting for transfers between devices  38.6 us (8%)
  other arithmetic  17.9 us (3%)
  matrix products  13.6 us (3%)
  between operations  5.55 us (1%)
    psum x3, blocking collectives, global_sums(): return lax.psum(jnp.stack(partial_terms), ('sx', 'sy'))  349 us
    ppermute x12, starting transfers between devices, with_halo(): before = lax.ppermute(last, axis, up)  41.7 us
    ppermute x12, starting transfers between devices, with_halo(): after = lax.ppermute(initial, axis, down)  31.1 us
    all_to_all x1, waiting for transfers between devices, per_device(): lax.all_to_all(moved_velocity, 'sy', split_axis=1, concat_axis=2, tiled=T...  20.8 us
    ppermute x12, waiting for transfers between devices, with_halo(): after = lax.ppermute(initial, axis, down)  13.8 us
  transfers between devices with their start and end apart: 25, of which 10 were waited for; matrix products, arithmetic and copies ran while one was open for 0% of the time, Pallas kernels for 0%

commit v1 on v0

v1 whole, which is shorter than its diff:
```python
import functools

import jax
import jax.numpy as jnp
import numpy as np
from jax import lax
from jax.experimental import pallas as pl
from jax.experimental.pallas import tpu as pltpu
from jax.sharding import PartitionSpec as P

CX, CY, NZ = 32, 16, 128
CLASSES = 8
PAD = 12
REACH = 10
WX, WY = CX + 2 * PAD, CY + 2 * PAD
EX = 68
EY = 56
AXIAL = 1.0 / 16.0
COUPLING = 0.25
f32 = jnp.float32
bf16 = jnp.bfloat16


def rows_of_lines(table):
    return table.reshape(CX, NZ)


def lay_out(row):
    return jnp.concatenate([row[0:16], row[8:32], row[24:40]], axis=0)


def gather_owned(row, low):
    return jnp.concatenate(
        [
            row[0:8],
            jnp.where(low, row[8:16], row[16:24]),
            row[24:32],
            jnp.where(low, row[32:40], row[40:48]),
            row[48:56],
        ],
        axis=0,
    )


def up_y(v):
    return pltpu.roll(v, v.shape[0] - 1, 0)


def down_y(v):
    return pltpu.roll(v, 1, 0)


def up_z(v):
    return pltpu.roll(v, v.shape[1] - 1, 1)


def down_z(v):
    return pltpu.roll(v, 1, 1)


def operator_row(s_ref, v_ref, xw, first, last):
    sl = slice(first, last)
    s, v = s_ref[xw, sl, :], v_ref[xw, sl, :]
    lane = lax.broadcasted_iota(jnp.int32, s.shape, 1)
    not_top, not_bottom = lane < NZ - 1, lane > 0
    total = (s + s_ref[xw + 1, sl, :]) * (v - v_ref[xw + 1, sl, :])
    total = total + (s + s_ref[xw - 1, sl, :]) * (v - v_ref[xw - 1, sl, :])
    total = total + (s + up_y(s)) * (v - up_y(v))
    total = total + (s + down_y(s)) * (v - down_y(v))
    axial = (s + jnp.where(not_top, up_z(s), 0.0)) * (v - jnp.where(not_top, up_z(v), 0.0))
    axial = axial + (s + jnp.where(not_bottom, down_z(s), 0.0)) * (
        v - jnp.where(not_bottom, down_z(v), 0.0)
    )
    return 0.5 * total + (0.5 * AXIAL) * axial


def loop(start, stop, body):
    def step(i, carry):
        body(i)
        return carry

    lax.fori_loop(start, stop, step, 0)


def krylov_kernel(
    copies,
    own_ref,
    cond_ref,
    yl_ref,
    yr_ref,
    xl_ref,
    xr_ref,
    spread_ref,
    d1_out,
    e_out,
    s_out,
    sums_out,
    sr,
    sa,
    sw,
    rw,
    d1w,
    i1w,
    ew,
    cxp,
    cxm,
    cyp,
    cym,
    czp,
    czm,
    inv,
    t0,
    ta,
    tb,
):
    sr[0, PAD : PAD + CX, :] = yl_ref[CX : CX + 2, :, :].reshape(CX, NZ)
    sr[1, PAD : PAD + CX, :] = cond_ref[...]
    sr[2, PAD : PAD + CX, :] = yr_ref[CX : CX + 2, :, :].reshape(CX, NZ)
    left_rows = xl_ref[3 * REACH : 3 * REACH + 3, :, :].reshape(48, NZ)
    right_rows = xr_ref[3 * REACH : 3 * REACH + 3, :, :].reshape(48, NZ)
    for k, src in enumerate((1, 0, 2)):
        sr[src, 0:PAD, :] = left_rows[PAD * k : PAD * k + PAD, :]
        sr[src, PAD + CX : WX, :] = right_rows[PAD * k : PAD * k + PAD, :]

    sub = lax.broadcasted_iota(jnp.int32, (8, NZ), 0)
    lane8 = lax.broadcasted_iota(jnp.int32, (8, NZ), 1)
    low8 = sub < 4
    pick = lane8 // 32 == (sub // 2 + 2) % 4

    def spread_rows(cx):
        def wide_row(part, half):
            return jnp.broadcast_to(sr[part, pl.ds(2 * cx + half, 1), :], (8, NZ))

        pairs = (
            (wide_row(0, 0), wide_row(0, 1)),
            (wide_row(0, 1), wide_row(1, 0)),
            (wide_row(1, 0), wide_row(1, 1)),
            (wide_row(1, 1), wide_row(2, 0)),
            (wide_row(2, 0), wide_row(2, 1)),
        )
        for t, (a, b) in enumerate(pairs):
            sa[cx, 8 * t : 8 * t + 8, :] = jnp.where(pick, jnp.where(low8, a, b), 0.0)

    loop(0, WX // 2, spread_rows)
    spread = spread_ref[...]

    def spread_cells(c):
        rest = sa[pl.ds(7 * c, 7), :, :].reshape(7 * WY, NZ)
        out = jnp.zeros((7 * WY, NZ), f32)
        for _ in range(3):
            part = rest.astype(bf16)
            rest = rest - part.astype(f32)
            out = out + jnp.dot(part, spread, preferred_element_type=f32)
        out = out.reshape(7, WY, NZ)
        for k in range(7):
            sw[14 * c + 2 * k, :, :] = out[k]
            sw[14 * c + 2 * k + 1, :, :] = out[k]

    loop(0, 4, spread_cells)

    rw[PAD : PAD + CX, 0:PAD, :] = yl_ref[0:CX, CY - PAD : CY, :]
    rw[PAD : PAD + CX, PAD : PAD + CY, :] = own_ref[...]
    rw[PAD : PAD + CX, PAD + CY : WY, :] = yr_ref[0:CX, 0:PAD, :]
    for ref, at in ((xl_ref, PAD - REACH), (xr_ref, PAD + CX)):
        rw[at : at + REACH, PAD : PAD + CY, :] = ref[0:REACH, :, :]
        rw[at : at + REACH, 0:PAD, :] = ref[REACH : 2 * REACH, CY - PAD : CY, :]
        rw[at : at + REACH, PAD + CY : WY, :] = ref[2 * REACH : 3 * REACH, 0:PAD, :]

    def coefficient_row(e, xw, cut_up=False, cut_down=False):
        s5 = sw[xw]
        lane = lax.broadcasted_iota(jnp.int32, (WY, NZ), 1)
        place = lax.broadcasted_iota(jnp.int32, (EY, NZ), 0)
        zp = AXIAL * (s5 + jnp.where(lane < NZ - 1, up_z(s5), 0.0))
        zm = AXIAL * (s5 + jnp.where(lane > 0, down_z(s5), 0.0))
        axial = lay_out(zp + zm)
        s = lay_out(s5)
        yp = s + jnp.where((place == 15) | (place == 39), 0.0, lay_out(up_y(s5)))
        ym = s + jnp.where((place == 16) | (place == 40), 0.0, lay_out(down_y(s5)))
        xp = s if cut_up else s + lay_out(sw[xw + 1])
        xm = s if cut_down else s + lay_out(sw[xw - 1])
        inverse = jnp.where(s > 0.0, 1.0 / (xp + xm + yp + ym + axial), 0.0)
        cxp[e] = xp * inverse
        cxm[e] = xm * inverse
        cyp[e] = yp * inverse
        cym[e] = ym * inverse
        czp[e] = lay_out(jnp.where(lane < NZ - 1, zp, 0.0)) * inverse
        czm[e] = lay_out(jnp.where(lane > 0, zm, 0.0)) * inverse
        inverse = inverse + inverse
        inv[e] = inverse
        t0[e] = lay_out(rw[xw]) * inverse

    loop(0, 13, lambda e: coefficient_row(e, e + 2))
    coefficient_row(13, 15, cut_up=True)
    coefficient_row(14, 8, cut_down=True)
    loop(15, 53, lambda e: coefficient_row(e, e - 6))
    coefficient_row(53, 47, cut_up=True)
    coefficient_row(54, 40, cut_down=True)
    loop(55, EX, lambda e: coefficient_row(e, e - 14))

    low = lax.broadcasted_iota(jnp.int32, (8, NZ), 0) < 4

    def swept(src, e):
        t = src[e]
        a = t0[e] + cxp[e] * src[e + 1]
        b = cyp[e] * up_y(t) + cym[e] * down_y(t)
        c = czp[e] * up_z(t) + czm[e] * down_z(t)
        return (a + cxm[e] * src[e - 1]) + (b + c)

    def sweep(src, dst, ranges):
        for start, stop, _ in ranges:

            def row(e):
                dst[e] = swept(src, e)

            loop(start, stop, row)

    def last_sweep(src, dst, ranges):
        for start, stop, shift in ranges:

            def row(e, shift=shift):
                dst[e + shift] = gather_owned(swept(src, e), low)

            loop(start, stop, row)

    def ranges(k, skip):
        return (
            (skip + k, 14 - k, 2),
            (14 + k, 54 - k, -6),
            (54 + k, EX - skip - k, -14),
        )

    def precondition(dst, skip):
        sweep(t0, ta, ranges(1, skip))
        sweep(ta, tb, ranges(2, skip))
        sweep(tb, ta, ranges(3, skip))
        last_sweep(ta, dst, ranges(4, skip))

    precondition(d1w, 0)

    def image_row(xw):
        i1w[xw] = operator_row(sw, d1w, xw, 0, WY)

    loop(PAD - 5, PAD + CX + 5, image_row)

    for start, stop, shift in ranges(0, 5):

        def start_row(e, shift=shift):
            t0[e] = lay_out(i1w[e + shift]) * inv[e]

        loop(start, stop, start_row)
    precondition(ew, 5)

    place = lax.broadcasted_iota(jnp.int32, (24, NZ), 0)
    owned = (place >= 4) & (place < 20)

    def products(i, sums):
        xw = i + PAD
        j = jnp.where(owned, operator_row(sw, ew, xw, 8, 32), 0.0)
        i1 = jnp.where(owned, i1w[xw, 8:32, :], 0.0)
        r = rw[xw, 8:32, :]

        def fold(v):
            return v[0:8] + v[8:16] + v[16:24]

        terms = (r * i1, i1 * i1, i1 * j, r * j, j * j)
        return tuple(acc + fold(t) for acc, t in zip(sums, terms))

    zero = jnp.zeros((8, NZ), f32)
    sums = lax.fori_loop(0, CX, products, (zero,) * 5)
    block = zero
    for k, acc in enumerate(sums):
        block = jnp.where(sub == k, jnp.sum(acc, axis=0, keepdims=True), block)
    for k in range(copies):
        sums_out[k] = block
    d1_out[...] = d1w[PAD - 1 : PAD + CX + 1, 8:32, :]
    e_out[...] = ew[PAD - 1 : PAD + CX + 1, 8:32, :]
    s_out[...] = sw[PAD : PAD + CX, 8:32, :]


def krylov(copies, own, cond_rows, yl, yr, xl, xr):
    lane = np.arange(NZ)
    spread = jnp.asarray((lane[:, None] % 32 == lane[None, :] // 4).astype(np.float32), bf16)
    wide = pltpu.VMEM((WX, WY, NZ), f32)
    laid = pltpu.VMEM((EX, EY, NZ), f32)
    return pl.pallas_call(
        functools.partial(krylov_kernel, copies),
        out_shape=(
            jax.ShapeDtypeStruct((CX + 2, 24, NZ), f32),
            jax.ShapeDtypeStruct((CX + 2, 24, NZ), f32),
            jax.ShapeDtypeStruct((CX, 24, NZ), f32),
            jax.ShapeDtypeStruct((copies, 8, NZ), f32),
        ),
        scratch_shapes=[
            pltpu.VMEM((3, WX, NZ), f32),
            pltpu.VMEM((WX // 2, WY, NZ), f32),
            wide,
            wide,
            wide,
            wide,
            wide,
        ]
        + [laid] * 10,
        compiler_params=pltpu.CompilerParams(vmem_limit_bytes=48 << 20),
        name="krylov",
    )(own, cond_rows, yl, yr, xl, xr, spread)


def partial_kernel(copies, parts_ref, out_ref):
    total = jnp.sum(parts_ref[...], axis=0)
    for k in range(copies):
        out_ref[k] = total


def partial_sums(parts, copies):
    return pl.pallas_call(
        functools.partial(partial_kernel, copies),
        out_shape=jax.ShapeDtypeStruct((copies, 8, NZ), f32),
        name="partial_sums",
    )(parts)


def velocity_kernel(parts_ref, d1_ref, e_ref, s_ref, v_ref, pot_ref, moved_ref):
    lanes = jnp.sum(jnp.sum(parts_ref[...], axis=0), axis=1, keepdims=True)
    a, b, c, d, g = (lanes[k : k + 1, 0:1] for k in range(5))
    ratio = c / b
    second = (d - ratio * a) / (g - ratio * c)
    first = a / b - ratio * second
    p1 = jnp.broadcast_to(first, (24, NZ))
    p2 = jnp.broadcast_to(second, (24, NZ))

    def row(i, before_here):
        before, here = before_here
        after = p1 * d1_ref[i + 2] + p2 * e_ref[i + 2]
        factor = COUPLING * s_ref[i]
        grad_x = 0.5 * (after - before)
        grad_y = 0.5 * (up_y(here) - down_y(here))
        pot_ref[i] = here[4:20]
        vx, vy = v_ref[0, i], v_ref[1, i]
        force_y = (factor * grad_x)[4:20]
        force_x = (factor * grad_y)[4:20]
        factor = factor[4:20]
        moved_ref[i, 0] = vx - force_x - factor * vx
        moved_ref[i, 1] = vy + force_y - factor * vy
        moved_ref[i, 2] = v_ref[2, i]
        return here, after

    lax.fori_loop(
        0, CX, row, (p1 * d1_ref[0] + p2 * e_ref[0], p1 * d1_ref[1] + p2 * e_ref[1])
    )


def velocity_step(parts, d1, e, cond, velocity):
    return pl.pallas_call(
        velocity_kernel,
        out_shape=(
            jax.ShapeDtypeStruct((CX, CY, NZ), f32),
            jax.ShapeDtypeStruct((CX, 3, CY, NZ), f32),
        ),
        compiler_params=pltpu.CompilerParams(vmem_limit_bytes=32 << 20),
        name="velocity_step",
    )(parts, d1, e, cond, velocity)


def diffusion_matrix(lines_count, cells_side):
    k = np.arange(lines_count) + 1
    phase = (k[:, None] * k[None, :]) % (2 * (lines_count + 1))
    sine = np.sqrt(2.0 / (lines_count + 1)) * np.sin(np.pi * phase / (lines_count + 1))
    half = np.sin(0.5 * np.pi * k / (lines_count + 1))
    gain = 2.0 / (1.0 + 8.0 * cells_side * cells_side * half * half)
    return (sine * gain) @ sine


def diffusion_kernel(high_ref, low_ref, x_ref, out_ref):
    high, low = high_ref[...], low_ref[...]
    for i in range(x_ref.shape[1]):
        for c in range(3):
            x = x_ref[:, i, c, :, :].reshape(high.shape[0], NZ)
            big = x.astype(bf16)
            small = (x - big.astype(f32)).astype(bf16)
            total = jnp.dot(high, small, preferred_element_type=f32)
            total = total + jnp.dot(low, big, preferred_element_type=f32)
            total = total + jnp.dot(high, big, preferred_element_type=f32)
            out_ref[c, i] = total - x


def diffuse(lines, cells_side):
    sources, count = lines.shape[0], lines.shape[1]
    length = sources * cells_side
    matrix = diffusion_matrix(length, cells_side).astype(np.float32)
    high = matrix.astype(bf16)
    low = (matrix - high.astype(np.float32)).astype(bf16)
    return pl.pallas_call(
        diffusion_kernel,
        out_shape=jax.ShapeDtypeStruct((3, count, length, NZ), f32),
        compiler_params=pltpu.CompilerParams(vmem_limit_bytes=32 << 20),
        name="diffuse",
    )(jnp.asarray(high), jnp.asarray(low), lines)


def per_device(right_side, class_map, conductivity_table, velocity):
    nx, ny = lax.axis_size("sx"), lax.axis_size("sy")

    def up(peers):
        return [(i, i + 1) for i in range(peers - 1)]

    def down(peers):
        return [(i + 1, i) for i in range(peers - 1)]

    classes = rows_of_lines(class_map)
    cond_rows = jnp.zeros((CX, NZ), f32)
    for k in range(CLASSES):
        cond_rows = jnp.where(classes == k, conductivity_table[k], cond_rows)
    message = jnp.concatenate([right_side, cond_rows.reshape(2, CY, NZ)], axis=0)
    yl = lax.ppermute(message, "sy", up(ny))
    yr = lax.ppermute(message, "sy", down(ny))

    def strip(at, cond_at):
        rows = [m[at : at + REACH] for m in (right_side, yl, yr)]
        cond = [cond_rows] + [m[CX : CX + 2].reshape(CX, NZ) for m in (yl, yr)]
        cond = [c[cond_at : cond_at + PAD] for c in cond] + [jnp.zeros((12, NZ), f32)]
        return jnp.concatenate(rows + [jnp.concatenate(cond, 0).reshape(3, CY, NZ)], axis=0)

    xl = lax.ppermute(strip(CX - REACH, CX - PAD), "sx", up(nx))
    xr = lax.ppermute(strip(0, 0), "sx", down(nx))
    d1, e, cond, sums = krylov(ny, right_side, cond_rows, yl, yr, xl, xr)
    sums = lax.all_to_all(sums, "sy", split_axis=0, concat_axis=0, tiled=True)
    sums = partial_sums(sums, nx)
    sums = lax.all_to_all(sums, "sx", split_axis=0, concat_axis=0, tiled=True)
    potential, moved = velocity_step(sums, d1, e, cond, velocity)
    lines = lax.all_to_all(
        moved.reshape(ny, CX // ny, 3, CY, NZ), "sy", split_axis=0, concat_axis=0, tiled=True
    )
    return potential, diffuse(lines, CY)


def solution(mesh):
    return jax.shard_map(
        per_device,
        mesh=mesh,
        in_specs=(P("sx", "sy", None), P("sx", "sy", None), P(), P(None, "sx", "sy", None)),
        out_specs=(P("sx", "sy", None), P(None, ("sx", "sy"), None, None)),
        check_vma=False,
    )
```

time: 514 us -> 167 us (0.32)
  blocking collectives: 349 us -> 75.2 us
  starting transfers between devices: 80.2 us -> 16.9 us
  Pallas kernels: 0 us -> 53.7 us
  waiting for transfers between devices: 38.6 us -> 10.8 us
  matrix products: 13.6 us -> 0 us
  other arithmetic: 17.9 us -> 6.02 us
    psum x3 -> x0, blocking collectives: 349 us -> none  [global_sums(): return lax.psum(jnp.stack(partial_terms), ('sx', 'sy'))]
    all_to_all x0 -> x3, blocking collectives: none -> 75.2 us  [the longest x1 27.8 us: per_device(): lax.all_to_all(moved.reshape(ny, CX // ny, 3, CY, NZ), 'sy', split_axis=0...]
    ppermute x24 -> x4, starting transfers between devices: 72.8 us -> 16.9 us  [the longest x1 12.4 us: per_device(): yr = lax.ppermute(message, 'sy', down(ny))]
    pallas_call x0 -> x4, Pallas kernels: none -> 53.7 us  [the longest x1 48.4 us: krylov(): pl.pallas_call(functools.partial(krylov_kernel, copies), out_shape=(jax.S...]
    all_to_all x1 -> x0, waiting for transfers between devices: 20.8 us -> none  [per_device(): lax.all_to_all(moved_velocity, 'sy', split_axis=1, concat_axis=2, tiled=T...]
    dot_general x2 -> x0, matrix products: 13.6 us -> none  [the longest x1 7.8 us: per_device(): jnp.matmul(sine_rows, sine_coeffs * line_gain, precision=highest)]
    all_to_all x1 -> x0, starting transfers between devices: 7.42 us -> none  [per_device(): lax.all_to_all(moved_velocity, 'sy', split_axis=1, concat_axis=2, tiled=T...]
    ppermute x24 -> x4, waiting for transfers between devices: 17.8 us -> 10.8 us  [the longest x1 4.95 us: per_device(): yl = lax.ppermute(message, 'sy', up(ny))]
  transfers between devices with their start and end apart: 25 -> 4, of which waited for: 10 -> 3; matrix products, arithmetic and copies ran while one was open for 0% -> 0% of each run, Pallas kernels for 0% -> 0%
where the time goes in v1:
time: 167 us
  blocking collectives  75.2 us (45%)
  Pallas kernels  53.7 us (32%)
  starting transfers between devices  16.9 us (10%)
  waiting for transfers between devices  10.8 us (6%)
  other arithmetic  6.02 us (4%)
  local copies, waits for them, and re-layouts  3.13 us (2%)
    pallas_call x1, Pallas kernels, krylov(): pl.pallas_call(functools.partial(krylov_kernel, copies), out_shape=(jax.S...  48.4 us
    all_to_all x1, blocking collectives, per_device(): lax.all_to_all(moved.reshape(ny, CX // ny, 3, CY, NZ), 'sy', split_axis=0...  27.8 us
    all_to_all x1, blocking collectives, per_device(): sums = lax.all_to_all(sums, 'sx', split_axis=0, concat_axis=0, tiled=True)  25.9 us
    all_to_all x1, blocking collectives, per_device(): sums = lax.all_to_all(sums, 'sy', split_axis=0, concat_axis=0, tiled=True)  21.5 us
    ppermute x1, starting transfers between devices, per_device(): yr = lax.ppermute(message, 'sy', down(ny))  12.4 us
    select_n x1, other arithmetic, per_device(): cond_rows = jnp.where(classes == k, conductivity_table[k], cond_rows)  5.9 us
    ppermute x1, waiting for transfers between devices, per_device(): yl = lax.ppermute(message, 'sy', up(ny))  4.95 us
    ppermute x1, waiting for transfers between devices, per_device(): xr = lax.ppermute(strip(0, 0), 'sx', down(nx))  3.87 us
  transfers between devices with their start and end apart: 4, of which 3 were waited for; matrix products, arithmetic and copies ran while one was open for 0% of the time, Pallas kernels for 0%

profile of v1, /device:TPU:1, one launch (start us, length us, event | category | flops | bytes accessed | tf_op | source)
XLA Modules:
  0.0 166.6 jit_solution(10697072222188594516)
XLA Ops:
  0.6 1.6 fusion.6
  2.3 5.9 %select_select_fusion = f32[16,8,32]{2,1,0:T(8,128)S(1)} fusion(s32[16,8,32]{2,1,0:T(8,128)} %param.8, f32[]{:T(128)} %bitcast, f32[]{:T(128)} %bitcast.1, f32[]{:T(128)} %bitcast.2, f32[]{:T(128)} %bitcast.3, f32[]{:T(128)} %bitcast.4, f32[]{:T(128)} %bitcast.7, f32[]{:T(128)} %bitcast.6, f32[]{:T(128)} %bitcast.5), kind=kLoop, calls=%fused_computation.2 | loop fusion | flops 65536 | bytes 32800 | tf_op jit(solution)/shard_map/jit(_where)/select_n | solution.py:412
  8.2 0.1 reshape.94
  8.2 0.0 copy-start
  8.3 1.0 constant_dynamic-update-slice_fusion.1
  9.3 12.4 %collective-permute-start.1 = (f32[34,16,128]{2,1,0:T(8,128)S(1)}, f32[34,16,128]{2,1,0:T(8,128)S(1)}, u32[]{:S(2)}, u32[]{:S(2)}) collective-permute-start(f32[34,16,128]{2,1,0:T(8,128)S(1)} %constant_dynamic-update-slice_fusion), channel_id=1, source_target_pairs={{1,0},{2,1},{3,2},{4,3},{5,4},{6,5},{7,6},{8,7},{9,8},{10,9},{11,1... | collective-permute-start | bytes 835592 | tf_op jit(solution)/shard_map/ppermute | solution.py:415
  21.7 1.9 %collective-permute-start = (f32[34,16,128]{2,1,0:T(8,128)S(1)}, f32[34,16,128]{2,1,0:T(8,128)S(1)}, u32[]{:S(2)}, u32[]{:S(2)}) collective-permute-start(f32[34,16,128]{2,1,0:T(8,128)S(1)} %constant_dynamic-update-slice_fusion), channel_id=1, source_target_pairs={{0,1},{1,2},{2,3},{3,4},{4,5},{5,6},{6,7},{7,8},{8,9},{9,10},{10,1... | collective-permute-start | bytes 835592 | tf_op jit(solution)/shard_map/ppermute | solution.py:414
  23.7 0.1 reshape.96
  23.8 0.1 reshape.95
  23.8 0.1 pad.15.clone
  23.9 0.0 copy-done
  23.9 0.0 collective-permute-done.1.yr_ref
  23.9 5.0 %collective-permute-done.yl_ref = f32[34,16,128]{2,1,0:T(8,128)S(1)} collective-permute-done((f32[34,16,128]{2,1,0:T(8,128)S(1)}, f32[34,16,128]{2,1,0:T(8,128)S(1)}, u32[]{:S(2)}, u32[]{:S(2)}) %collective-permute-start) | collective-permute-done | bytes 278560 | tf_op jit(solution)/shard_map/ppermute | solution.py:414
  28.9 0.1 maximum_maximum_fusion.1
  29.1 1.3 collective-permute-start.2
  30.4 0.0 copy-start.4
  30.4 1.3 collective-permute-start.3
  31.7 0.1 reshape.92.cond_ref
  31.8 0.0 copy-start.1
  31.8 1.9 %collective-permute-done.2.xl_ref = f32[33,16,128]{2,1,0:T(8,128)S(1)} collective-permute-done((f32[33,16,128]{2,1,0:T(8,128)S(1)}, f32[33,16,128]{2,1,0:T(8,128)S(1)}, u32[]{:S(2)}, u32[]{:S(2)}) %collective-permute-start.2) | collective-permute-done | bytes 270368 | tf_op jit(solution)/shard_map/ppermute | solution.py:423
  33.7 3.9 %collective-permute-done.3.xr_ref = f32[33,16,128]{2,1,0:T(8,128)S(1)} collective-permute-done((f32[33,16,128]{2,1,0:T(8,128)S(1)}, f32[33,16,128]{2,1,0:T(8,128)S(1)}, u32[]{:S(2)}, u32[]{:S(2)}) %collective-permute-start.3) | collective-permute-done | bytes 270368 | tf_op jit(solution)/shard_map/ppermute | solution.py:424
  37.6 0.0 copy-done.4
  37.6 48.4 %krylov.1 = (f32[34,24,128]{2,1,0:T(8,128)S(1)}, f32[34,24,128]{2,1,0:T(8,128)S(1)}, f32[32,24,128]{2,1,0:T(8,128)S(1)}, f32[32,8,128]{2,1,0:T(8,128)S(1)}) custom-call(f32[32,16,128]{2,1,0:T(8,128)S(1)} %copy-done, f32[32,128]{1,0:T(8,128)S(1)} %reshape.92.cond_ref, f32[34,16,128]{2,1,0:T(8,128)S(1)} %collective-permute-done.yl_ref, ...), custom_call_target="tpu_custom_call" | custom-call | tf_op jit(solution)/shard_map/krylov/pallas_call | solution.py:285
  86.0 21.5 %all_to_all.15.parts_ref = f32[32,8,128]{2,1,0:T(8,128)} all-to-all(f32[32,8,128]{2,1,0:T(8,128)S(1)} %get-tuple-element.8), channel_id=1, replica_groups=mesh['sx'=24,'sy'=32] {'sy'}, dimensions={0} | all-to-all | bytes 262144 | tf_op jit(solution)/shard_map/all_to_all | solution.py:426
  107.5 1.6 partial_sums.1
  109.1 25.9 %all_to_all.16.parts_ref = f32[24,8,128]{2,1,0:T(8,128)S(1)} all-to-all(f32[24,8,128]{2,1,0:T(8,128)} %partial_sums.1), channel_id=1, replica_groups=mesh['sx'=24,'sy'=32] {'sx'}, dimensions={0} | all-to-all | bytes 196608 | tf_op jit(solution)/shard_map/all_to_all | solution.py:428
  135.1 0.0 copy-done.1
  135.1 1.5 velocity_step.1
  136.5 0.0 copy-start.2
  136.5 0.0 copy-start.3
  136.5 27.8 %all_to_all.17.x_ref = f32[32,1,3,16,128]{4,3,2,1,0:T(8,128)S(1)} all-to-all(f32[32,1,3,16,128]{4,3,2,1,0:T(8,128)S(1)} %bitcast.13), channel_id=1, replica_groups=mesh['sx'=24,'sy'=32] {'sy'}, dimensions={0} | all-to-all | bytes 1572864 | tf_op jit(solution)/shard_map/all_to_all | solution.py:430
  164.3 0.0 copy-done.2
  164.3 0.0 copy-done.3
  164.3 2.3 %diffuse.1 = f32[3,1,512,128]{3,2,1,0:T(8,128)} custom-call(bf16[512,512]{1,0:T(8,128)(2,1)S(1)} %copy-done.3, bf16[512,512]{1,0:T(8,128)(2,1)S(1)} %copy-done.2, f32[32,1,3,16,128]{4,3,2,1,0:T(8,128)S(1)} %all_to_all.17.x_ref), custom_call_target="tpu_custom_call" | custom-call | tf_op jit(solution)/shard_map/diffuse/pallas_call | solution.py:392
  (11 shorter events, 0.1 us)
Async XLA Ops:
  8.2 15.7 %copy-start = (f32[32,16,128]{2,1,0:T(8,128)S(1)}, f32[32,16,128]{2,1,0:T(8,128)}, u32[]{:S(2)}) copy-start(f32[32,16,128]{2,1,0:T(8,128)} %own_ref.1) | copy-start | bytes 786436
  9.3 14.6 %collective-permute-start.1 = (f32[34,16,128]{2,1,0:T(8,128)S(1)}, f32[34,16,128]{2,1,0:T(8,128)S(1)}, u32[]{:S(2)}, u32[]{:S(2)}) collective-permute-start(f32[34,16,128]{2,1,0:T(8,128)S(1)} %constant_dynamic-update-slice_fusion), channel_id=1, source_target_pairs={{1,0},{2,1},{3,2},{4,3},{5,4},{6,5},{7,6},{8,7},{9,8},{10,9},{11,1... | collective-permute-start | bytes 835592 | tf_op jit(solution)/shard_map/ppermute | solution.py:415
  21.7 7.2 %collective-permute-start = (f32[34,16,128]{2,1,0:T(8,128)S(1)}, f32[34,16,128]{2,1,0:T(8,128)S(1)}, u32[]{:S(2)}, u32[]{:S(2)}) collective-permute-start(f32[34,16,128]{2,1,0:T(8,128)S(1)} %constant_dynamic-update-slice_fusion), channel_id=1, source_target_pairs={{0,1},{1,2},{2,3},{3,4},{4,5},{5,6},{6,7},{7,8},{8,9},{9,10},{10,1... | collective-permute-start | bytes 835592 | tf_op jit(solution)/shard_map/ppermute | solution.py:414
  29.1 4.7 %collective-permute-start.2 = (f32[33,16,128]{2,1,0:T(8,128)S(1)}, f32[33,16,128]{2,1,0:T(8,128)S(1)}, u32[]{:S(2)}, u32[]{:S(2)}) collective-permute-start(f32[33,16,128]{2,1,0:T(8,128)S(1)} %pad_maximum_fusion), channel_id=1, source_target_pairs={{0,32},{32,64},{64,96},{96,128},{128,160},{160,192},{192,224},{224... | collective-permute-start | bytes 811016 | tf_op jit(solution)/shard_map/ppermute | solution.py:423
  30.4 7.2 %copy-start.4 = (bf16[128,128]{1,0:T(8,128)(2,1)S(1)}, bf16[128,128]{1,0:T(8,128)(2,1)}, u32[]{:S(2)}) copy-start(bf16[128,128]{1,0:T(8,128)(2,1)} %constant.11.clone.spread_ref) | copy-start | bytes 98308
  30.4 7.2 %collective-permute-start.3 = (f32[33,16,128]{2,1,0:T(8,128)S(1)}, f32[33,16,128]{2,1,0:T(8,128)S(1)}, u32[]{:S(2)}, u32[]{:S(2)}) collective-permute-start(f32[33,16,128]{2,1,0:T(8,128)S(1)} %pad_maximum_fusion.1), channel_id=1, source_target_pairs={{32,0},{64,32},{96,64},{128,96},{160,128},{192,160},{224,192},{256... | collective-permute-start | bytes 811016 | tf_op jit(solution)/shard_map/ppermute | solution.py:424
  31.8 103.3 %copy-start.1 = (f32[3,32,16,128]{3,2,1,0:T(8,128)S(1)}, f32[3,32,16,128]{3,2,1,0:T(8,128)}, u32[]{:S(2)}) copy-start(f32[3,32,16,128]{3,2,1,0:T(8,128)} %v_ref.1) | copy-start | bytes 2359300
  136.5 27.8 %copy-start.2 = (bf16[512,512]{1,0:T(8,128)(2,1)S(1)}, bf16[512,512]{1,0:T(8,128)(2,1)}, u32[]{:S(2)}) copy-start(bf16[512,512]{1,0:T(8,128)(2,1)} %constant.27.clone.low_ref) | copy-start | bytes 1572868
  136.5 27.8 %copy-start.3 = (bf16[512,512]{1,0:T(8,128)(2,1)S(1)}, bf16[512,512]{1,0:T(8,128)(2,1)}, u32[]{:S(2)}) copy-start(bf16[512,512]{1,0:T(8,128)(2,1)} %constant.26.clone.high_ref) | copy-start | bytes 1572868

commit v2 on v1

--- a/solution.py
+++ b/solution.py
@@ -17,12 +17,9 @@
 EY = 56
 AXIAL = 1.0 / 16.0
 COUPLING = 0.25
+GROUP, GROUP_C, GROUP_I, GROUP_P = 10, 13, 21, 16
 f32 = jnp.float32
 bf16 = jnp.bfloat16
-
-
-def rows_of_lines(table):
-    return table.reshape(CX, NZ)
 
 
 def lay_out(row):
@@ -74,18 +71,44 @@
     return 0.5 * total + (0.5 * AXIAL) * axial
 
 
-def loop(start, stop, body):
-    def step(i, carry):
-        body(i)
+def loop(start, stop, body, group=1):
+    whole = (stop - start) // group
+
+    def step(k, carry):
+        body(start + k * group, group)
         return carry
 
-    lax.fori_loop(start, stop, step, 0)
+    if whole > 1:
+        lax.fori_loop(0, whole, step, 0)
+    elif whole == 1:
+        body(start, group)
+    if start + whole * group < stop:
+        body(start + whole * group, stop - start - whole * group)
+
+
+def message_kernel(table_ref, side_ref, class_ref, out_ref):
+    out_ref[0:CX] = side_ref[...]
+    for h in range(2):
+        classes = jnp.concatenate([class_ref[:, 4 * h + m, :] for m in range(4)], axis=1)
+        cond = jnp.zeros(classes.shape, f32)
+        for k in range(CLASSES):
+            cond = jnp.where(classes == k, table_ref[k], cond)
+        out_ref[CX + h] = cond
+
+
+def message_of(table, right_side, class_map):
+    vmem = pl.BlockSpec(memory_space=pltpu.VMEM)
+    return pl.pallas_call(
+        message_kernel,
+        in_specs=[pl.BlockSpec(memory_space=pltpu.SMEM), vmem, vmem],
+        out_shape=jax.ShapeDtypeStruct((CX + 2, CY, NZ), f32),
+        name="message",
+    )(table, right_side, class_map)
 
 
 def krylov_kernel(
     copies,
     own_ref,
-    cond_ref,
     yl_ref,
     yr_ref,
     xl_ref,
@@ -113,23 +136,24 @@
     ta,
     tb,
 ):
-    sr[0, PAD : PAD + CX, :] = yl_ref[CX : CX + 2, :, :].reshape(CX, NZ)
-    sr[1, PAD : PAD + CX, :] = cond_ref[...]
-    sr[2, PAD : PAD + CX, :] = yr_ref[CX : CX + 2, :, :].reshape(CX, NZ)
-    left_rows = xl_ref[3 * REACH : 3 * REACH + 3, :, :].reshape(48, NZ)
-    right_rows = xr_ref[3 * REACH : 3 * REACH + 3, :, :].reshape(48, NZ)
+    half = PAD // 2
+    for k, ref in enumerate((yl_ref, own_ref, yr_ref)):
+        for h in range(2):
+            sr[k, h, half : half + CX // 2, :] = ref[CX + h, :, :]
     for k, src in enumerate((1, 0, 2)):
-        sr[src, 0:PAD, :] = left_rows[PAD * k : PAD * k + PAD, :]
-        sr[src, PAD + CX : WX, :] = right_rows[PAD * k : PAD * k + PAD, :]
+        for h in range(2):
+            at = slice(8 * h, 8 * h + half)
+            sr[src, h, 0:half, :] = xl_ref[3 * REACH + k, at, :]
+            sr[src, h, half + CX // 2 : WX // 2, :] = xr_ref[3 * REACH + k, at, :]
 
     sub = lax.broadcasted_iota(jnp.int32, (8, NZ), 0)
     lane8 = lax.broadcasted_iota(jnp.int32, (8, NZ), 1)
     low8 = sub < 4
     pick = lane8 // 32 == (sub // 2 + 2) % 4
 
-    def spread_rows(cx):
-        def wide_row(part, half):
-            return jnp.broadcast_to(sr[part, pl.ds(2 * cx + half, 1), :], (8, NZ))
+    def spread_row(cx):
+        def wide_row(part, h):
+            return jnp.broadcast_to(sr[part, h, pl.ds(cx, 1), :], (8, NZ))
 
         pairs = (
             (wide_row(0, 0), wide_row(0, 1)),
@@ -141,10 +165,14 @@
         for t, (a, b) in enumerate(pairs):
             sa[cx, 8 * t : 8 * t + 8, :] = jnp.where(pick, jnp.where(low8, a, b), 0.0)
 
-    loop(0, WX // 2, spread_rows)
+    def spread_rows(cx, n):
+        for i in range(n):
+            spread_row(cx + i)
+
+    loop(0, WX // 2, spread_rows, 4)
     spread = spread_ref[...]
 
-    def spread_cells(c):
+    def spread_cells(c, _):
         rest = sa[pl.ds(7 * c, 7), :, :].reshape(7 * WY, NZ)
         out = jnp.zeros((7 * WY, NZ), f32)
         for _ in range(3):
@@ -159,7 +187,7 @@
     loop(0, 4, spread_cells)
 
     rw[PAD : PAD + CX, 0:PAD, :] = yl_ref[0:CX, CY - PAD : CY, :]
-    rw[PAD : PAD + CX, PAD : PAD + CY, :] = own_ref[...]
+    rw[PAD : PAD + CX, PAD : PAD + CY, :] = own_ref[0:CX, :, :]
     rw[PAD : PAD + CX, PAD + CY : WY, :] = yr_ref[0:CX, 0:PAD, :]
     for ref, at in ((xl_ref, PAD - REACH), (xr_ref, PAD + CX)):
         rw[at : at + REACH, PAD : PAD + CY, :] = ref[0:REACH, :, :]
@@ -189,38 +217,50 @@
         inv[e] = inverse
         t0[e] = lay_out(rw[xw]) * inverse
 
-    loop(0, 13, lambda e: coefficient_row(e, e + 2))
+    def coefficient_rows(shift):
+        def rows(e, n):
+            for i in range(n):
+                coefficient_row(e + i, e + i + shift)
+
+        return rows
+
+    loop(0, 13, coefficient_rows(2), GROUP_C)
     coefficient_row(13, 15, cut_up=True)
     coefficient_row(14, 8, cut_down=True)
-    loop(15, 53, lambda e: coefficient_row(e, e - 6))
+    loop(15, 53, coefficient_rows(-6), GROUP_C)
     coefficient_row(53, 47, cut_up=True)
     coefficient_row(54, 40, cut_down=True)
-    loop(55, EX, lambda e: coefficient_row(e, e - 14))
+    loop(55, EX, coefficient_rows(-14), GROUP_C)
 
     low = lax.broadcasted_iota(jnp.int32, (8, NZ), 0) < 4
 
-    def swept(src, e):
-        t = src[e]
-        a = t0[e] + cxp[e] * src[e + 1]
-        b = cyp[e] * up_y(t) + cym[e] * down_y(t)
-        c = czp[e] * up_z(t) + czm[e] * down_z(t)
-        return (a + cxm[e] * src[e - 1]) + (b + c)
+    def swept(src, e, n):
+        rows = [src[e - 1 + i] for i in range(n + 2)]
+        out = []
+        for i in range(n):
+            t = rows[i + 1]
+            a = t0[e + i] + cxp[e + i] * rows[i + 2]
+            b = cyp[e + i] * up_y(t) + cym[e + i] * down_y(t)
+            c = czp[e + i] * up_z(t) + czm[e + i] * down_z(t)
+            out.append((a + cxm[e + i] * rows[i]) + (b + c))
+        return out
 
     def sweep(src, dst, ranges):
+        def rows(e, n):
+            for i, new in enumerate(swept(src, e, n)):
+                dst[e + i] = new
+
         for start, stop, _ in ranges:
-
-            def row(e):
-                dst[e] = swept(src, e)
-
-            loop(start, stop, row)
+            loop(start, stop, rows, GROUP)
 
     def last_sweep(src, dst, ranges):
         for start, stop, shift in ranges:
 
-            def row(e, shift=shift):
-                dst[e + shift] = gather_owned(swept(src, e), low)
-
-            loop(start, stop, row)
+            def rows(e, n, shift=shift):
+                for i, new in enumerate(swept(src, e, n)):
+                    dst[e + shift + i] = gather_owned(new, low)
+
+            loop(start, stop, rows, GROUP)
 
     def ranges(k, skip):
         return (
@@ -237,24 +277,25 @@
 
     precondition(d1w, 0)
 
-    def image_row(xw):
-        i1w[xw] = operator_row(sw, d1w, xw, 0, WY)
-
-    loop(PAD - 5, PAD + CX + 5, image_row)
+    def image_rows(xw, n):
+        for i, new in enumerate([operator_row(sw, d1w, xw + i, 0, WY) for i in range(n)]):
+            i1w[xw + i] = new
+
+    loop(PAD - 5, PAD + CX + 5, image_rows, GROUP_I)
 
     for start, stop, shift in ranges(0, 5):
 
-        def start_row(e, shift=shift):
-            t0[e] = lay_out(i1w[e + shift]) * inv[e]
-
-        loop(start, stop, start_row)
+        def start_rows(e, n, shift=shift):
+            for i in range(n):
+                t0[e + i] = lay_out(i1w[e + shift + i]) * inv[e + i]
+
+        loop(start, stop, start_rows, 4)
     precondition(ew, 5)
 
     place = lax.broadcasted_iota(jnp.int32, (24, NZ), 0)
     owned = (place >= 4) & (place < 20)
 
-    def products(i, sums):
-        xw = i + PAD
+    def products(xw, sums):
         j = jnp.where(owned, operator_row(sw, ew, xw, 8, 32), 0.0)
         i1 = jnp.where(owned, i1w[xw, 8:32, :], 0.0)
         r = rw[xw, 8:32, :]
@@ -265,11 +306,17 @@
         terms = (r * i1, i1 * i1, i1 * j, r * j, j * j)
         return tuple(acc + fold(t) for acc, t in zip(sums, terms))
 
+    def product_rows(k, sums):
+        for i in range(GROUP_P):
+            sums = products(PAD + GROUP_P * k + i, sums)
+        return sums
+
     zero = jnp.zeros((8, NZ), f32)
-    sums = lax.fori_loop(0, CX, products, (zero,) * 5)
-    block = zero
+    sums = lax.fori_loop(0, CX // GROUP_P, product_rows, (zero,) * 5)
+    block = jnp.zeros((1, NZ), f32)
     for k, acc in enumerate(sums):
-        block = jnp.where(sub == k, jnp.sum(acc, axis=0, keepdims=True), block)
+        total = jnp.sum(jnp.sum(acc, axis=0, keepdims=True), axis=1, keepdims=True)
+        block = jnp.where(lane8[0:1] == k, total, block)
     for k in range(copies):
         sums_out[k] = block
     d1_out[...] = d1w[PAD - 1 : PAD + CX + 1, 8:32, :]
@@ -277,7 +324,7 @@
     s_out[...] = sw[PAD : PAD + CX, 8:32, :]
 
 
-def krylov(copies, own, cond_rows, yl, yr, xl, xr):
+def krylov(copies, own, yl, yr, xl, xr):
     lane = np.arange(NZ)
     spread = jnp.asarray((lane[:, None] % 32 == lane[None, :] // 4).astype(np.float32), bf16)
     wide = pltpu.VMEM((WX, WY, NZ), f32)
@@ -288,10 +335,10 @@
             jax.ShapeDtypeStruct((CX + 2, 24, NZ), f32),
             jax.ShapeDtypeStruct((CX + 2, 24, NZ), f32),
             jax.ShapeDtypeStruct((CX, 24, NZ), f32),
-            jax.ShapeDtypeStruct((copies, 8, NZ), f32),
+            jax.ShapeDtypeStruct((copies, 1, NZ), f32),
         ),
         scratch_shapes=[
-            pltpu.VMEM((3, WX, NZ), f32),
+            pltpu.VMEM((3, 2, WX // 2, NZ), f32),
             pltpu.VMEM((WX // 2, WY, NZ), f32),
             wide,
             wide,
@@ -302,7 +349,7 @@
         + [laid] * 10,
         compiler_params=pltpu.CompilerParams(vmem_limit_bytes=48 << 20),
         name="krylov",
-    )(own, cond_rows, yl, yr, xl, xr, spread)
+    )(own, yl, yr, xl, xr, spread)
 
 
 def partial_kernel(copies, parts_ref, out_ref):
@@ -314,14 +361,17 @@
 def partial_sums(parts, copies):
     return pl.pallas_call(
         functools.partial(partial_kernel, copies),
-        out_shape=jax.ShapeDtypeStruct((copies, 8, NZ), f32),
+        out_shape=jax.ShapeDtypeStruct((copies, 1, NZ), f32),
         name="partial_sums",
     )(parts)
 
 
 def velocity_kernel(parts_ref, d1_ref, e_ref, s_ref, v_ref, pot_ref, moved_ref):
-    lanes = jnp.sum(jnp.sum(parts_ref[...], axis=0), axis=1, keepdims=True)
-    a, b, c, d, g = (lanes[k : k + 1, 0:1] for k in range(5))
+    totals = jnp.sum(parts_ref[...], axis=0)
+    lane = lax.broadcasted_iota(jnp.int32, (1, NZ), 1)
+    a, b, c, d, g = (
+        jnp.sum(jnp.where(lane == k, totals, 0.0), axis=1, keepdims=True) for k in range(5)
+    )
     ratio = c / b
     second = (d - ratio * a) / (g - ratio * c)
     first = a / b - ratio * second
@@ -406,23 +456,20 @@
     def down(peers):
         return [(i + 1, i) for i in range(peers - 1)]
 
-    classes = rows_of_lines(class_map)
-    cond_rows = jnp.zeros((CX, NZ), f32)
-    for k in range(CLASSES):
-        cond_rows = jnp.where(classes == k, conductivity_table[k], cond_rows)
-    message = jnp.concatenate([right_side, cond_rows.reshape(2, CY, NZ)], axis=0)
-    yl = lax.ppermute(message, "sy", up(ny))
-    yr = lax.ppermute(message, "sy", down(ny))
+    own = message_of(conductivity_table, right_side, class_map)
+    yl = lax.ppermute(own, "sy", up(ny))
+    yr = lax.ppermute(own, "sy", down(ny))
 
     def strip(at, cond_at):
-        rows = [m[at : at + REACH] for m in (right_side, yl, yr)]
-        cond = [cond_rows] + [m[CX : CX + 2].reshape(CX, NZ) for m in (yl, yr)]
-        cond = [c[cond_at : cond_at + PAD] for c in cond] + [jnp.zeros((12, NZ), f32)]
-        return jnp.concatenate(rows + [jnp.concatenate(cond, 0).reshape(3, CY, NZ)], axis=0)
-
-    xl = lax.ppermute(strip(CX - REACH, CX - PAD), "sx", up(nx))
+        parts = (own, yl, yr)
+        cond = [m[CX : CX + 2, cond_at : cond_at + PAD // 2] for m in parts]
+        cond = jnp.pad(jnp.stack(cond), ((0, 0), (0, 0), (0, 2), (0, 0)))
+        rows = [m[at : at + REACH] for m in parts]
+        return jnp.concatenate(rows + [cond.reshape(3, CY, NZ)], axis=0)
+
+    xl = lax.ppermute(strip(CX - REACH, CX // 2 - PAD // 2), "sx", up(nx))
     xr = lax.ppermute(strip(0, 0), "sx", down(nx))
-    d1, e, cond, sums = krylov(ny, right_side, cond_rows, yl, yr, xl, xr)
+    d1, e, cond, sums = krylov(ny, own, yl, yr, xl, xr)
     sums = lax.all_to_all(sums, "sy", split_axis=0, concat_axis=0, tiled=True)
     sums = partial_sums(sums, nx)
     sums = lax.all_to_all(sums, "sx", split_axis=0, concat_axis=0, tiled=True)

time: 167 us -> 123 us (0.74)
  Pallas kernels: 53.7 us -> 20.2 us
  other arithmetic: 6.02 us -> 0.06 us
  blocking collectives: 75.2 us -> 72.7 us
  local copies, waits for them, and re-layouts: 3.13 us -> 1.01 us
    pallas_call x1, Pallas kernels: 48.4 us -> 13.4 us  [krylov(): pl.pallas_call(functools.partial(krylov_kernel, copies), out_shape=(jax.S...]
    select_n x1 -> x0, other arithmetic: 5.9 us -> none  [per_device(): cond_rows = jnp.where(classes == k, conductivity_table[k], cond_rows)]
    pallas_call x0 -> x1, Pallas kernels: none -> 1.77 us  [message_of(): pl.pallas_call(message_kernel, in_specs=[pl.BlockSpec(memory_space=pltpu....]
  transfers between devices with their start and end apart: 4 -> 4, of which waited for: 3 -> 3; matrix products, arithmetic and copies ran while one was open for 0% -> 1% of each run, Pallas kernels for 0% -> 0%
where the time goes in v2:
time: 123 us; the launch traced here: 122 us
  blocking collectives  72.7 us (59%)
  Pallas kernels  20.2 us (16%)
  starting transfers between devices  17.2 us (14%)
  waiting for transfers between devices  10.5 us (9%)
    all_to_all x1, blocking collectives, per_device(): lax.all_to_all(moved.reshape(ny, CX // ny, 3, CY, NZ), 'sy', split_axis=0...  28.2 us
    all_to_all x1, blocking collectives, per_device(): sums = lax.all_to_all(sums, 'sx', split_axis=0, concat_axis=0, tiled=True)  24.5 us
    all_to_all x1, blocking collectives, per_device(): sums = lax.all_to_all(sums, 'sy', split_axis=0, concat_axis=0, tiled=True)  20 us
    pallas_call x1, Pallas kernels, krylov(): pl.pallas_call(functools.partial(krylov_kernel, copies), out_shape=(jax.S...  13.4 us
    ppermute x1, starting transfers between devices, per_device(): yr = lax.ppermute(own, 'sy', down(ny))  12.5 us
    ppermute x1, waiting for transfers between devices, per_device(): yl = lax.ppermute(own, 'sy', up(ny))  4.55 us
    ppermute x1, waiting for transfers between devices, per_device(): xr = lax.ppermute(strip(0, 0), 'sx', down(nx))  4.03 us
  transfers between devices with their start and end apart: 4, of which 3 were waited for; matrix products, arithmetic and copies ran while one was open for 1% of the time, Pallas kernels for 0%

profile of v2, /device:TPU:1, one launch (start us, length us, event | category | flops | bytes accessed | tf_op | source)
XLA Modules:
  0.0 122.4 jit_solution(1575126723451842018)
XLA Ops:
  0.6 1.8 %message.1.own_ref = f32[34,16,128]{2,1,0:T(8,128)} custom-call(f32[8]{0:T(128)} %table_ref.1, f32[32,16,128]{2,1,0:T(8,128)} %side_ref.1, s32[16,8,32]{2,1,0:T(8,128)} %class_ref.1), custom_call_target="tpu_custom_call" | custom-call | tf_op jit(solution)/shard_map/message/pallas_call | solution.py:101
  2.4 0.0 copy-start
  2.4 12.5 %collective-permute-start.1 = (f32[34,16,128]{2,1,0:T(8,128)}, f32[34,16,128]{2,1,0:T(8,128)S(1)}, u32[]{:S(2)}, u32[]{:S(2)}) collective-permute-start(f32[34,16,128]{2,1,0:T(8,128)} %message.1.own_ref), channel_id=1, source_target_pairs={{1,0},{2,1},{3,2},{4,3},{5,4},{6,5},{7,6},{8,7},{9,8},{10,9},{11,1... | collective-permute-start | bytes 835592 | tf_op jit(solution)/shard_map/ppermute | solution.py:461
  15.0 1.9 %collective-permute-start = (f32[34,16,128]{2,1,0:T(8,128)}, f32[34,16,128]{2,1,0:T(8,128)S(1)}, u32[]{:S(2)}, u32[]{:S(2)}) collective-permute-start(f32[34,16,128]{2,1,0:T(8,128)} %message.1.own_ref), channel_id=1, source_target_pairs={{0,1},{1,2},{2,3},{3,4},{4,5},{5,6},{6,7},{7,8},{8,9},{9,10},{10,1... | collective-permute-start | bytes 835592 | tf_op jit(solution)/shard_map/ppermute | solution.py:460
  16.9 0.9 fusion.2
  17.8 0.0 copy-done
  17.9 0.0 collective-permute-done.1.yr_ref
  17.9 4.5 %collective-permute-done.yl_ref = f32[34,16,128]{2,1,0:T(8,128)S(1)} collective-permute-done((f32[34,16,128]{2,1,0:T(8,128)}, f32[34,16,128]{2,1,0:T(8,128)S(1)}, u32[]{:S(2)}, u32[]{:S(2)}) %collective-permute-start) | collective-permute-done | bytes 278560 | tf_op jit(solution)/shard_map/ppermute | solution.py:460
  22.5 1.3 %collective-permute-start.2 = (f32[33,16,128]{2,1,0:T(8,128)S(1)}, f32[33,16,128]{2,1,0:T(8,128)S(1)}, u32[]{:S(2)}, u32[]{:S(2)}) collective-permute-start(f32[33,16,128]{2,1,0:T(8,128)S(1)} %pad_maximum_fusion), channel_id=1, source_target_pairs={{0,32},{32,64},{64,96},{96,128},{128,160},{160,192},{192,224},{224... | collective-permute-start | bytes 811016 | tf_op jit(solution)/shard_map/ppermute | solution.py:470
  23.9 0.0 copy-start.4
  23.9 0.0 copy-start.1
  23.9 1.4 %collective-permute-start.3 = (f32[33,16,128]{2,1,0:T(8,128)S(1)}, f32[33,16,128]{2,1,0:T(8,128)S(1)}, u32[]{:S(2)}, u32[]{:S(2)}) collective-permute-start(f32[33,16,128]{2,1,0:T(8,128)S(1)} %pad_maximum_fusion.1), channel_id=1, source_target_pairs={{32,0},{64,32},{96,64},{128,96},{160,128},{192,160},{224,192},{256... | collective-permute-start | bytes 811016 | tf_op jit(solution)/shard_map/ppermute | solution.py:471
  25.3 1.9 %collective-permute-done.2.xl_ref = f32[33,16,128]{2,1,0:T(8,128)S(1)} collective-permute-done((f32[33,16,128]{2,1,0:T(8,128)S(1)}, f32[33,16,128]{2,1,0:T(8,128)S(1)}, u32[]{:S(2)}, u32[]{:S(2)}) %collective-permute-start.2) | collective-permute-done | bytes 270368 | tf_op jit(solution)/shard_map/ppermute | solution.py:470
  27.2 4.0 %collective-permute-done.3.xr_ref = f32[33,16,128]{2,1,0:T(8,128)S(1)} collective-permute-done((f32[33,16,128]{2,1,0:T(8,128)S(1)}, f32[33,16,128]{2,1,0:T(8,128)S(1)}, u32[]{:S(2)}, u32[]{:S(2)}) %collective-permute-start.3) | collective-permute-done | bytes 270368 | tf_op jit(solution)/shard_map/ppermute | solution.py:471
  31.2 0.0 copy-done.4
  31.2 13.4 %krylov.1 = (f32[34,24,128]{2,1,0:T(8,128)S(1)}, f32[34,24,128]{2,1,0:T(8,128)S(1)}, f32[32,24,128]{2,1,0:T(8,128)S(1)}, f32[32,1,128]{2,1,0:T(1,128)S(1)}) custom-call(f32[34,16,128]{2,1,0:T(8,128)S(1)} %copy-done, f32[34,16,128]{2,1,0:T(8,128)S(1)} %collective-permute-done.yl_ref, f32[34,16,128]{2,1,0:T(8,128)S(1)} %collective-permute-done.1.yr_ref, ...), custom_call_target="tpu_custom_call" | custom-call | tf_op jit(solution)/shard_map/krylov/pallas_call | solution.py:332
  44.6 20.0 %all_to_all.15.parts_ref = f32[32,1,128]{2,1,0:T(1,128)} all-to-all(f32[32,1,128]{2,1,0:T(1,128)S(1)} %get-tuple-element.8), channel_id=1, replica_groups=mesh['sx'=24,'sy'=32] {'sy'}, dimensions={0} | all-to-all | bytes 32768 | tf_op jit(solution)/shard_map/all_to_all | solution.py:473
  64.6 1.4 %partial_sums.1 = f32[24,1,128]{2,1,0:T(1,128)} custom-call(f32[32,1,128]{2,1,0:T(1,128)} %all_to_all.15.parts_ref), custom_call_target="tpu_custom_call" | custom-call | tf_op jit(solution)/shard_map/partial_sums/pallas_call | solution.py:362
  65.9 24.5 %all_to_all.16.parts_ref = f32[24,1,128]{2,1,0:T(1,128)S(1)} all-to-all(f32[24,1,128]{2,1,0:T(1,128)} %partial_sums.1), channel_id=1, replica_groups=mesh['sx'=24,'sy'=32] {'sx'}, dimensions={0} | all-to-all | bytes 24576 | tf_op jit(solution)/shard_map/all_to_all | solution.py:475
  90.5 0.0 copy-done.1
  90.5 1.4 %velocity_step.1 = (f32[32,16,128]{2,1,0:T(8,128)}, f32[32,3,16,128]{3,2,1,0:T(8,128)S(1)}) custom-call(f32[24,1,128]{2,1,0:T(1,128)S(1)} %all_to_all.16.parts_ref, f32[34,24,128]{2,1,0:T(8,128)S(1)} %get-tuple-element.9.d1_ref, f32[34,24,128]{2,1,0:T(8,128)S(1)} %get-tuple-element.10.e_ref, f32[32,24,128]{2,1,0:T(8,128)S(1)} %get-tuple-element.11.s_ref, ...), custom_call_target="tpu_custom_call" | custom-call | tf_op jit(solution)/shard_map/velocity_step/pallas_call | solution.py:403
  91.9 0.0 copy-start.2
  91.9 0.0 copy-start.3
  91.9 28.2 %all_to_all.17.x_ref = f32[32,1,3,16,128]{4,3,2,1,0:T(8,128)S(1)} all-to-all(f32[32,1,3,16,128]{4,3,2,1,0:T(8,128)S(1)} %bitcast.17), channel_id=1, replica_groups=mesh['sx'=24,'sy'=32] {'sy'}, dimensions={0} | all-to-all | bytes 1572864 | tf_op jit(solution)/shard_map/all_to_all | solution.py:477
  120.2 0.0 copy-done.2
  120.2 0.0 copy-done.3
  120.2 2.3 %diffuse.1 = f32[3,1,512,128]{3,2,1,0:T(8,128)} custom-call(bf16[512,512]{1,0:T(8,128)(2,1)S(1)} %copy-done.3, bf16[512,512]{1,0:T(8,128)(2,1)S(1)} %copy-done.2, f32[32,1,3,16,128]{4,3,2,1,0:T(8,128)S(1)} %all_to_all.17.x_ref), custom_call_target="tpu_custom_call" | custom-call | tf_op jit(solution)/shard_map/diffuse/pallas_call | solution.py:442
  (9 shorter events, 0.1 us)
Async XLA Ops:
  2.4 15.4 %copy-start = (f32[34,16,128]{2,1,0:T(8,128)S(1)}, f32[34,16,128]{2,1,0:T(8,128)}, u32[]{:S(2)}) copy-start(f32[34,16,128]{2,1,0:T(8,128)} %message.1.own_ref) | copy-start | bytes 835588
  2.4 15.5 %collective-permute-start.1 = (f32[34,16,128]{2,1,0:T(8,128)}, f32[34,16,128]{2,1,0:T(8,128)S(1)}, u32[]{:S(2)}, u32[]{:S(2)}) collective-permute-start(f32[34,16,128]{2,1,0:T(8,128)} %message.1.own_ref), channel_id=1, source_target_pairs={{1,0},{2,1},{3,2},{4,3},{5,4},{6,5},{7,6},{8,7},{9,8},{10,9},{11,1... | collective-permute-start | bytes 835592 | tf_op jit(solution)/shard_map/ppermute | solution.py:461
  15.0 7.5 %collective-permute-start = (f32[34,16,128]{2,1,0:T(8,128)}, f32[34,16,128]{2,1,0:T(8,128)S(1)}, u32[]{:S(2)}, u32[]{:S(2)}) collective-permute-start(f32[34,16,128]{2,1,0:T(8,128)} %message.1.own_ref), channel_id=1, source_target_pairs={{0,1},{1,2},{2,3},{3,4},{4,5},{5,6},{6,7},{7,8},{8,9},{9,10},{10,1... | collective-permute-start | bytes 835592 | tf_op jit(solution)/shard_map/ppermute | solution.py:460
  22.5 4.7 %collective-permute-start.2 = (f32[33,16,128]{2,1,0:T(8,128)S(1)}, f32[33,16,128]{2,1,0:T(8,128)S(1)}, u32[]{:S(2)}, u32[]{:S(2)}) collective-permute-start(f32[33,16,128]{2,1,0:T(8,128)S(1)} %pad_maximum_fusion), channel_id=1, source_target_pairs={{0,32},{32,64},{64,96},{96,128},{128,160},{160,192},{192,224},{224... | collective-permute-start | bytes 811016 | tf_op jit(solution)/shard_map/ppermute | solution.py:470
  23.9 7.4 %copy-start.4 = (bf16[128,128]{1,0:T(8,128)(2,1)S(1)}, bf16[128,128]{1,0:T(8,128)(2,1)}, u32[]{:S(2)}) copy-start(bf16[128,128]{1,0:T(8,128)(2,1)} %constant.9.clone.spread_ref) | copy-start | bytes 98308
  23.9 66.6 %copy-start.1 = (f32[3,32,16,128]{3,2,1,0:T(8,128)S(1)}, f32[3,32,16,128]{3,2,1,0:T(8,128)}, u32[]{:S(2)}) copy-start(f32[3,32,16,128]{3,2,1,0:T(8,128)} %v_ref.1) | copy-start | bytes 2359300
  23.9 7.3 %collective-permute-start.3 = (f32[33,16,128]{2,1,0:T(8,128)S(1)}, f32[33,16,128]{2,1,0:T(8,128)S(1)}, u32[]{:S(2)}, u32[]{:S(2)}) collective-permute-start(f32[33,16,128]{2,1,0:T(8,128)S(1)} %pad_maximum_fusion.1), channel_id=1, source_target_pairs={{32,0},{64,32},{96,64},{128,96},{160,128},{192,160},{224,192},{256... | collective-permute-start | bytes 811016 | tf_op jit(solution)/shard_map/ppermute | solution.py:471
  91.9 28.2 %copy-start.2 = (bf16[512,512]{1,0:T(8,128)(2,1)S(1)}, bf16[512,512]{1,0:T(8,128)(2,1)}, u32[]{:S(2)}) copy-start(bf16[512,512]{1,0:T(8,128)(2,1)} %constant.11.clone.low_ref) | copy-start | bytes 1572868
  91.9 28.2 %copy-start.3 = (bf16[512,512]{1,0:T(8,128)(2,1)S(1)}, bf16[512,512]{1,0:T(8,128)(2,1)}, u32[]{:S(2)}) copy-start(bf16[512,512]{1,0:T(8,128)(2,1)} %constant.10.clone.high_ref) | copy-start | bytes 1572868

commit v3 on v2

--- a/solution.py
+++ b/solution.py
@@ -17,7 +17,7 @@
 EY = 56
 AXIAL = 1.0 / 16.0
 COUPLING = 0.25
-GROUP, GROUP_C, GROUP_I, GROUP_P = 10, 13, 21, 16
+GROUP, GROUP_C, GROUP_I, GROUP_P = 19, 13, 21, 16
 f32 = jnp.float32
 bf16 = jnp.bfloat16
 
@@ -26,17 +26,19 @@
     return jnp.concatenate([row[0:16], row[8:32], row[24:40]], axis=0)
 
 
-def gather_owned(row, low):
+def gather_middle(row, low):
     return jnp.concatenate(
         [
-            row[0:8],
-            jnp.where(low, row[8:16], row[16:24]),
-            row[24:32],
-            jnp.where(low, row[32:40], row[40:48]),
-            row[48:56],
+            jnp.where(low, row[0:8], row[8:16]),
+            row[16:24],
+            jnp.where(low, row[24:32], row[32:40]),
         ],
         axis=0,
     )
+
+
+def gather_owned(row, low):
+    return jnp.concatenate([row[0:8], gather_middle(row[8:48], low), row[48:56]], axis=0)
 
 
 def up_y(v):
@@ -234,31 +236,46 @@
 
     low = lax.broadcasted_iota(jnp.int32, (8, NZ), 0) < 4
 
-    def swept(src, e, n):
-        rows = [src[e - 1 + i] for i in range(n + 2)]
+    def swept(src, e, n, narrow):
+        lines = slice(8, 48) if narrow else slice(0, EY)
+        wider = narrow and src is t0
+
+        def beside(i):
+            if not wider:
+                return up_y(rows[i]), down_y(rows[i])
+            t = src[e - 1 + i]
+            return up_y(t)[8:48], down_y(t)[8:48]
+
+        rows = [src[e - 1 + i, lines, :] for i in range(n + 2)]
         out = []
         for i in range(n):
             t = rows[i + 1]
-            a = t0[e + i] + cxp[e + i] * rows[i + 2]
-            b = cyp[e + i] * up_y(t) + cym[e + i] * down_y(t)
-            c = czp[e + i] * up_z(t) + czm[e + i] * down_z(t)
-            out.append((a + cxm[e + i] * rows[i]) + (b + c))
+            above, below = beside(i + 1)
+            a = t0[e + i, lines, :] + cxp[e + i, lines, :] * rows[i + 2]
+            b = cyp[e + i, lines, :] * above + cym[e + i, lines, :] * below
+            c = czp[e + i, lines, :] * up_z(t) + czm[e + i, lines, :] * down_z(t)
+            out.append((a + cxm[e + i, lines, :] * rows[i]) + (b + c))
         return out
 
-    def sweep(src, dst, ranges):
+    def sweep(src, dst, ranges, narrow):
+        lines = slice(8, 48) if narrow else slice(0, EY)
+
         def rows(e, n):
-            for i, new in enumerate(swept(src, e, n)):
-                dst[e + i] = new
+            for i, new in enumerate(swept(src, e, n, narrow)):
+                dst[e + i, lines, :] = new
 
         for start, stop, _ in ranges:
             loop(start, stop, rows, GROUP)
 
-    def last_sweep(src, dst, ranges):
+    def last_sweep(src, dst, ranges, narrow):
         for start, stop, shift in ranges:
 
             def rows(e, n, shift=shift):
-                for i, new in enumerate(swept(src, e, n)):
-                    dst[e + shift + i] = gather_owned(new, low)
+                for i, new in enumerate(swept(src, e, n, narrow)):
+                    if narrow:
+                        dst[e + shift + i, 8:32, :] = gather_middle(new, low)
+                    else:
+                        dst[e + shift + i] = gather_owned(new, low)
 
             loop(start, stop, rows, GROUP)
 
@@ -269,13 +286,13 @@
             (54 + k, EX - skip - k, -14),
         )
 
-    def precondition(dst, skip):
-        sweep(t0, ta, ranges(1, skip))
-        sweep(ta, tb, ranges(2, skip))
-        sweep(tb, ta, ranges(3, skip))
-        last_sweep(ta, dst, ranges(4, skip))
-
-    precondition(d1w, 0)
+    def precondition(dst, skip, narrow):
+        sweep(t0, ta, ranges(1, skip), narrow)
+        sweep(ta, tb, ranges(2, skip), narrow)
+        sweep(tb, ta, ranges(3, skip), narrow)
+        last_sweep(ta, dst, ranges(4, skip), narrow)
+
+    precondition(d1w, 0, False)
 
     def image_rows(xw, n):
         for i, new in enumerate([operator_row(sw, d1w, xw + i, 0, WY) for i in range(n)]):
@@ -289,8 +306,8 @@
             for i in range(n):
                 t0[e + i] = lay_out(i1w[e + shift + i]) * inv[e + i]
 
-        loop(start, stop, start_rows, 4)
-    precondition(ew, 5)
+        loop(start, stop, start_rows, 10)
+    precondition(ew, 5, True)
 
     place = lax.broadcasted_iota(jnp.int32, (24, NZ), 0)
     owned = (place >= 4) & (place < 20)
@@ -352,20 +369,6 @@
     )(own, yl, yr, xl, xr, spread)
 
 
-def partial_kernel(copies, parts_ref, out_ref):
-    total = jnp.sum(parts_ref[...], axis=0)
-    for k in range(copies):
-        out_ref[k] = total
-
-
-def partial_sums(parts, copies):
-    return pl.pallas_call(
-        functools.partial(partial_kernel, copies),
-        out_shape=jax.ShapeDtypeStruct((copies, 1, NZ), f32),
-        name="partial_sums",
-    )(parts)
-
-
 def velocity_kernel(parts_ref, d1_ref, e_ref, s_ref, v_ref, pot_ref, moved_ref):
     totals = jnp.sum(parts_ref[...], axis=0)
     lane = lax.broadcasted_iota(jnp.int32, (1, NZ), 1)
@@ -471,7 +474,7 @@
     xr = lax.ppermute(strip(0, 0), "sx", down(nx))
     d1, e, cond, sums = krylov(ny, own, yl, yr, xl, xr)
     sums = lax.all_to_all(sums, "sy", split_axis=0, concat_axis=0, tiled=True)
-    sums = partial_sums(sums, nx)
+    sums = jnp.broadcast_to(jnp.sum(sums, axis=0, keepdims=True), (nx, 1, NZ))
     sums = lax.all_to_all(sums, "sx", split_axis=0, concat_axis=0, tiled=True)
     potential, moved = velocity_step(sums, d1, e, cond, velocity)
     lines = lax.all_to_all(

time: 123 us -> 119 us (0.967)
  Pallas kernels: 20.2 us -> 16.5 us
    pallas_call x1, Pallas kernels: 13.4 us -> 11 us  [krylov(): pl.pallas_call(functools.partial(krylov_kernel, copies), out_shape=(jax.S...]
    pallas_call x1 -> x0, Pallas kernels: 1.36 us -> none  [partial_sums(): pl.pallas_call(functools.partial(partial_kernel, copies), out_shape=jax.S...]
where the time goes in v3:
time: 119 us
  blocking collectives  72.5 us (61%)
  starting transfers between devices  17.2 us (14%)
  Pallas kernels  16.5 us (14%)
  waiting for transfers between devices  10.5 us (9%)
    all_to_all x1, blocking collectives, per_device(): lax.all_to_all(moved.reshape(ny, CX // ny, 3, CY, NZ), 'sy', split_axis=0...  28.1 us
    all_to_all x1, blocking collectives, per_device(): sums = lax.all_to_all(sums, 'sx', split_axis=0, concat_axis=0, tiled=True)  24.4 us
    all_to_all x1, blocking collectives, per_device(): sums = lax.all_to_all(sums, 'sy', split_axis=0, concat_axis=0, tiled=True)  20 us
    ppermute x1, starting transfers between devices, per_device(): yr = lax.ppermute(own, 'sy', down(ny))  12.5 us
    pallas_call x1, Pallas kernels, krylov(): pl.pallas_call(functools.partial(krylov_kernel, copies), out_shape=(jax.S...  11 us
    ppermute x1, waiting for transfers between devices, per_device(): yl = lax.ppermute(own, 'sy', up(ny))  4.55 us
    ppermute x1, waiting for transfers between devices, per_device(): xr = lax.ppermute(strip(0, 0), 'sx', down(nx))  4.03 us
  transfers between devices with their start and end apart: 4, of which 3 were waited for; matrix products, arithmetic and copies ran while one was open for 1% of the time, Pallas kernels for 0%

profile of v3, /device:TPU:1, one launch (start us, length us, event | category | flops | bytes accessed | tf_op | source)
XLA Modules:
  0.0 118.6 jit_solution(9808637669799374334)
XLA Ops:
  0.6 1.8 %message.1.own_ref = f32[34,16,128]{2,1,0:T(8,128)} custom-call(f32[8]{0:T(128)} %table_ref.1, f32[32,16,128]{2,1,0:T(8,128)} %side_ref.1, s32[16,8,32]{2,1,0:T(8,128)} %class_ref.1), custom_call_target="tpu_custom_call" | custom-call | tf_op jit(solution)/shard_map/message/pallas_call | solution.py:103
  2.4 0.0 copy-start
  2.4 12.5 %collective-permute-start.1 = (f32[34,16,128]{2,1,0:T(8,128)}, f32[34,16,128]{2,1,0:T(8,128)S(1)}, u32[]{:S(2)}, u32[]{:S(2)}) collective-permute-start(f32[34,16,128]{2,1,0:T(8,128)} %message.1.own_ref), channel_id=1, source_target_pairs={{1,0},{2,1},{3,2},{4,3},{5,4},{6,5},{7,6},{8,7},{9,8},{10,9},{11,1... | collective-permute-start | bytes 835592 | tf_op jit(solution)/shard_map/ppermute | solution.py:464
  15.0 1.9 %collective-permute-start = (f32[34,16,128]{2,1,0:T(8,128)}, f32[34,16,128]{2,1,0:T(8,128)S(1)}, u32[]{:S(2)}, u32[]{:S(2)}) collective-permute-start(f32[34,16,128]{2,1,0:T(8,128)} %message.1.own_ref), channel_id=1, source_target_pairs={{0,1},{1,2},{2,3},{3,4},{4,5},{5,6},{6,7},{7,8},{8,9},{9,10},{10,1... | collective-permute-start | bytes 835592 | tf_op jit(solution)/shard_map/ppermute | solution.py:463
  16.9 0.9 fusion.2
  17.8 0.0 copy-done
  17.9 0.0 collective-permute-done.1.yr_ref
  17.9 4.5 %collective-permute-done.yl_ref = f32[34,16,128]{2,1,0:T(8,128)S(1)} collective-permute-done((f32[34,16,128]{2,1,0:T(8,128)}, f32[34,16,128]{2,1,0:T(8,128)S(1)}, u32[]{:S(2)}, u32[]{:S(2)}) %collective-permute-start) | collective-permute-done | bytes 278560 | tf_op jit(solution)/shard_map/ppermute | solution.py:463
  22.5 1.3 %collective-permute-start.2 = (f32[33,16,128]{2,1,0:T(8,128)S(1)}, f32[33,16,128]{2,1,0:T(8,128)S(1)}, u32[]{:S(2)}, u32[]{:S(2)}) collective-permute-start(f32[33,16,128]{2,1,0:T(8,128)S(1)} %pad_maximum_fusion), channel_id=1, source_target_pairs={{0,32},{32,64},{64,96},{96,128},{128,160},{160,192},{192,224},{224... | collective-permute-start | bytes 811016 | tf_op jit(solution)/shard_map/ppermute | solution.py:473
  23.9 0.0 copy-start.4
  23.9 0.0 copy-start.1
  23.9 1.4 %collective-permute-start.3 = (f32[33,16,128]{2,1,0:T(8,128)S(1)}, f32[33,16,128]{2,1,0:T(8,128)S(1)}, u32[]{:S(2)}, u32[]{:S(2)}) collective-permute-start(f32[33,16,128]{2,1,0:T(8,128)S(1)} %pad_maximum_fusion.1), channel_id=1, source_target_pairs={{32,0},{64,32},{96,64},{128,96},{160,128},{192,160},{224,192},{256... | collective-permute-start | bytes 811016 | tf_op jit(solution)/shard_map/ppermute | solution.py:474
  25.3 1.9 %collective-permute-done.2.xl_ref = f32[33,16,128]{2,1,0:T(8,128)S(1)} collective-permute-done((f32[33,16,128]{2,1,0:T(8,128)S(1)}, f32[33,16,128]{2,1,0:T(8,128)S(1)}, u32[]{:S(2)}, u32[]{:S(2)}) %collective-permute-start.2) | collective-permute-done | bytes 270368 | tf_op jit(solution)/shard_map/ppermute | solution.py:473
  27.2 4.0 %collective-permute-done.3.xr_ref = f32[33,16,128]{2,1,0:T(8,128)S(1)} collective-permute-done((f32[33,16,128]{2,1,0:T(8,128)S(1)}, f32[33,16,128]{2,1,0:T(8,128)S(1)}, u32[]{:S(2)}, u32[]{:S(2)}) %collective-permute-start.3) | collective-permute-done | bytes 270368 | tf_op jit(solution)/shard_map/ppermute | solution.py:474
  31.2 0.0 copy-done.4
  31.2 11.0 %krylov.1 = (f32[34,24,128]{2,1,0:T(8,128)S(1)}, f32[34,24,128]{2,1,0:T(8,128)S(1)}, f32[32,24,128]{2,1,0:T(8,128)S(1)}, f32[32,1,128]{2,1,0:T(1,128)S(1)}) custom-call(f32[34,16,128]{2,1,0:T(8,128)S(1)} %copy-done, f32[34,16,128]{2,1,0:T(8,128)S(1)} %collective-permute-done.yl_ref, f32[34,16,128]{2,1,0:T(8,128)S(1)} %collective-permute-done.1.yr_ref, ...), custom_call_target="tpu_custom_call" | custom-call | tf_op jit(solution)/shard_map/krylov/pallas_call | solution.py:349
  42.3 20.0 %all_to_all.15 = f32[32,1,128]{2,1,0:T(1,128)S(1)} all-to-all(f32[32,1,128]{2,1,0:T(1,128)S(1)} %get-tuple-element.8), channel_id=1, replica_groups=mesh['sx'=24,'sy'=32] {'sy'}, dimensions={0} | all-to-all | bytes 32768 | tf_op jit(solution)/shard_map/all_to_all | solution.py:476
  62.3 0.1 reduce_sum.9
  62.3 24.4 %all_to_all.16.parts_ref = f32[24,1,128]{2,1,0:T(1,128)S(1)} all-to-all(f32[24,1,128]{2,1,0:T(1,128)S(1)} %broadcast_in_dim.2), channel_id=1, replica_groups=mesh['sx'=24,'sy'=32] {'sx'}, dimensions={0} | all-to-all | bytes 24576 | tf_op jit(solution)/shard_map/all_to_all | solution.py:478
  86.8 0.0 copy-done.1
  86.8 1.4 %velocity_step.1 = (f32[32,16,128]{2,1,0:T(8,128)}, f32[32,3,16,128]{3,2,1,0:T(8,128)S(1)}) custom-call(f32[24,1,128]{2,1,0:T(1,128)S(1)} %all_to_all.16.parts_ref, f32[34,24,128]{2,1,0:T(8,128)S(1)} %get-tuple-element.9.d1_ref, f32[34,24,128]{2,1,0:T(8,128)S(1)} %get-tuple-element.10.e_ref, f32[32,24,128]{2,1,0:T(8,128)S(1)} %get-tuple-element.11.s_ref, ...), custom_call_target="tpu_custom_call" | custom-call | tf_op jit(solution)/shard_map/velocity_step/pallas_call | solution.py:406
  88.2 0.0 copy-start.2
  88.2 0.0 copy-start.3
  88.2 28.1 %all_to_all.17.x_ref = f32[32,1,3,16,128]{4,3,2,1,0:T(8,128)S(1)} all-to-all(f32[32,1,3,16,128]{4,3,2,1,0:T(8,128)S(1)} %bitcast.17), channel_id=1, replica_groups=mesh['sx'=24,'sy'=32] {'sy'}, dimensions={0} | all-to-all | bytes 1572864 | tf_op jit(solution)/shard_map/all_to_all | solution.py:480
  116.3 0.0 copy-done.2
  116.3 0.0 copy-done.3
  116.3 2.3 %diffuse.1 = f32[3,1,512,128]{3,2,1,0:T(8,128)} custom-call(bf16[512,512]{1,0:T(8,128)(2,1)S(1)} %copy-done.3, bf16[512,512]{1,0:T(8,128)(2,1)S(1)} %copy-done.2, f32[32,1,3,16,128]{4,3,2,1,0:T(8,128)S(1)} %all_to_all.17.x_ref), custom_call_target="tpu_custom_call" | custom-call | tf_op jit(solution)/shard_map/diffuse/pallas_call | solution.py:445
  (10 shorter events, 0.1 us)
Async XLA Ops:
  2.4 15.4 %copy-start = (f32[34,16,128]{2,1,0:T(8,128)S(1)}, f32[34,16,128]{2,1,0:T(8,128)}, u32[]{:S(2)}) copy-start(f32[34,16,128]{2,1,0:T(8,128)} %message.1.own_ref) | copy-start | bytes 835588
  2.4 15.5 %collective-permute-start.1 = (f32[34,16,128]{2,1,0:T(8,128)}, f32[34,16,128]{2,1,0:T(8,128)S(1)}, u32[]{:S(2)}, u32[]{:S(2)}) collective-permute-start(f32[34,16,128]{2,1,0:T(8,128)} %message.1.own_ref), channel_id=1, source_target_pairs={{1,0},{2,1},{3,2},{4,3},{5,4},{6,5},{7,6},{8,7},{9,8},{10,9},{11,1... | collective-permute-start | bytes 835592 | tf_op jit(solution)/shard_map/ppermute | solution.py:464
  15.0 7.5 %collective-permute-start = (f32[34,16,128]{2,1,0:T(8,128)}, f32[34,16,128]{2,1,0:T(8,128)S(1)}, u32[]{:S(2)}, u32[]{:S(2)}) collective-permute-start(f32[34,16,128]{2,1,0:T(8,128)} %message.1.own_ref), channel_id=1, source_target_pairs={{0,1},{1,2},{2,3},{3,4},{4,5},{5,6},{6,7},{7,8},{8,9},{9,10},{10,1... | collective-permute-start | bytes 835592 | tf_op jit(solution)/shard_map/ppermute | solution.py:463
  22.5 4.7 %collective-permute-start.2 = (f32[33,16,128]{2,1,0:T(8,128)S(1)}, f32[33,16,128]{2,1,0:T(8,128)S(1)}, u32[]{:S(2)}, u32[]{:S(2)}) collective-permute-start(f32[33,16,128]{2,1,0:T(8,128)S(1)} %pad_maximum_fusion), channel_id=1, source_target_pairs={{0,32},{32,64},{64,96},{96,128},{128,160},{160,192},{192,224},{224... | collective-permute-start | bytes 811016 | tf_op jit(solution)/shard_map/ppermute | solution.py:473
  23.9 7.4 %copy-start.4 = (bf16[128,128]{1,0:T(8,128)(2,1)S(1)}, bf16[128,128]{1,0:T(8,128)(2,1)}, u32[]{:S(2)}) copy-start(bf16[128,128]{1,0:T(8,128)(2,1)} %constant.10.clone.spread_ref) | copy-start | bytes 98308
  23.9 62.9 %copy-start.1 = (f32[3,32,16,128]{3,2,1,0:T(8,128)S(1)}, f32[3,32,16,128]{3,2,1,0:T(8,128)}, u32[]{:S(2)}) copy-start(f32[3,32,16,128]{3,2,1,0:T(8,128)} %v_ref.1) | copy-start | bytes 2359300
  23.9 7.3 %collective-permute-start.3 = (f32[33,16,128]{2,1,0:T(8,128)S(1)}, f32[33,16,128]{2,1,0:T(8,128)S(1)}, u32[]{:S(2)}, u32[]{:S(2)}) collective-permute-start(f32[33,16,128]{2,1,0:T(8,128)S(1)} %pad_maximum_fusion.1), channel_id=1, source_target_pairs={{32,0},{64,32},{96,64},{128,96},{160,128},{192,160},{224,192},{256... | collective-permute-start | bytes 811016 | tf_op jit(solution)/shard_map/ppermute | solution.py:474
  88.2 28.1 %copy-start.2 = (bf16[512,512]{1,0:T(8,128)(2,1)S(1)}, bf16[512,512]{1,0:T(8,128)(2,1)}, u32[]{:S(2)}) copy-start(bf16[512,512]{1,0:T(8,128)(2,1)} %constant.12.clone.low_ref) | copy-start | bytes 1572868
  88.2 28.1 %copy-start.3 = (bf16[512,512]{1,0:T(8,128)(2,1)S(1)}, bf16[512,512]{1,0:T(8,128)(2,1)}, u32[]{:S(2)}) copy-start(bf16[512,512]{1,0:T(8,128)(2,1)} %constant.11.clone.high_ref) | copy-start | bytes 1572868

commit v4 on v3

--- a/solution.py
+++ b/solution.py
@@ -88,22 +88,29 @@
         body(start + whole * group, stop - start - whole * group)
 
 
-def message_kernel(table_ref, side_ref, class_ref, out_ref):
-    out_ref[0:CX] = side_ref[...]
+def message_kernel(table_ref, side_ref, class_ref, own_ref, low_ref, high_ref):
+    own_ref[0:CX] = side_ref[...]
+    low_ref[0:REACH] = side_ref[0:REACH]
+    high_ref[0:REACH] = side_ref[CX - REACH : CX]
+    half = PAD // 2
     for h in range(2):
         classes = jnp.concatenate([class_ref[:, 4 * h + m, :] for m in range(4)], axis=1)
         cond = jnp.zeros(classes.shape, f32)
         for k in range(CLASSES):
             cond = jnp.where(classes == k, table_ref[k], cond)
-        out_ref[CX + h] = cond
+        own_ref[CX + h] = cond
+        low_ref[REACH, 8 * h : 8 * h + 8, :] = cond[0:8]
+        high_ref[REACH, 8 * h : 8 * h + half, :] = cond[CX // 2 - half : CX // 2]
+        high_ref[REACH, 8 * h + half : 8 * h + 8, :] = cond[0 : 8 - half]
 
 
 def message_of(table, right_side, class_map):
     vmem = pl.BlockSpec(memory_space=pltpu.VMEM)
+    strip = jax.ShapeDtypeStruct((REACH + 1, CY, NZ), f32)
     return pl.pallas_call(
         message_kernel,
         in_specs=[pl.BlockSpec(memory_space=pltpu.SMEM), vmem, vmem],
-        out_shape=jax.ShapeDtypeStruct((CX + 2, CY, NZ), f32),
+        out_shape=(jax.ShapeDtypeStruct((CX + 2, CY, NZ), f32), strip, strip),
         name="message",
     )(table, right_side, class_map)
 
@@ -113,8 +120,12 @@
     own_ref,
     yl_ref,
     yr_ref,
-    xl_ref,
-    xr_ref,
+    ll_ref,
+    lo_ref,
+    lr_ref,
+    rl_ref,
+    ro_ref,
+    rr_ref,
     spread_ref,
     d1_out,
     e_out,
@@ -138,15 +149,17 @@
     ta,
     tb,
 ):
+    xl, xr = (ll_ref, lo_ref, lr_ref), (rl_ref, ro_ref, rr_ref)
+
     half = PAD // 2
     for k, ref in enumerate((yl_ref, own_ref, yr_ref)):
         for h in range(2):
             sr[k, h, half : half + CX // 2, :] = ref[CX + h, :, :]
-    for k, src in enumerate((1, 0, 2)):
+    for k in range(3):
         for h in range(2):
             at = slice(8 * h, 8 * h + half)
-            sr[src, h, 0:half, :] = xl_ref[3 * REACH + k, at, :]
-            sr[src, h, half + CX // 2 : WX // 2, :] = xr_ref[3 * REACH + k, at, :]
+            sr[k, h, 0:half, :] = xl[k][REACH, at, :]
+            sr[k, h, half + CX // 2 : WX // 2, :] = xr[k][REACH, at, :]
 
     sub = lax.broadcasted_iota(jnp.int32, (8, NZ), 0)
     lane8 = lax.broadcasted_iota(jnp.int32, (8, NZ), 1)
@@ -191,10 +204,10 @@
     rw[PAD : PAD + CX, 0:PAD, :] = yl_ref[0:CX, CY - PAD : CY, :]
     rw[PAD : PAD + CX, PAD : PAD + CY, :] = own_ref[0:CX, :, :]
     rw[PAD : PAD + CX, PAD + CY : WY, :] = yr_ref[0:CX, 0:PAD, :]
-    for ref, at in ((xl_ref, PAD - REACH), (xr_ref, PAD + CX)):
-        rw[at : at + REACH, PAD : PAD + CY, :] = ref[0:REACH, :, :]
-        rw[at : at + REACH, 0:PAD, :] = ref[REACH : 2 * REACH, CY - PAD : CY, :]
-        rw[at : at + REACH, PAD + CY : WY, :] = ref[2 * REACH : 3 * REACH, 0:PAD, :]
+    for refs, at in ((xl, PAD - REACH), (xr, PAD + CX)):
+        rw[at : at + REACH, 0:PAD, :] = refs[0][0:REACH, CY - PAD : CY, :]
+        rw[at : at + REACH, PAD : PAD + CY, :] = refs[1][0:REACH, :, :]
+        rw[at : at + REACH, PAD + CY : WY, :] = refs[2][0:REACH, 0:PAD, :]
 
     def coefficient_row(e, xw, cut_up=False, cut_down=False):
         s5 = sw[xw]
@@ -341,7 +354,7 @@
     s_out[...] = sw[PAD : PAD + CX, 8:32, :]
 
 
-def krylov(copies, own, yl, yr, xl, xr):
+def krylov(copies, own, yl, yr, strips):
     lane = np.arange(NZ)
     spread = jnp.asarray((lane[:, None] % 32 == lane[None, :] // 4).astype(np.float32), bf16)
     wide = pltpu.VMEM((WX, WY, NZ), f32)
@@ -366,7 +379,7 @@
         + [laid] * 10,
         compiler_params=pltpu.CompilerParams(vmem_limit_bytes=48 << 20),
         name="krylov",
-    )(own, yl, yr, xl, xr, spread)
+    )(own, yl, yr, *strips, spread)
 
 
 def velocity_kernel(parts_ref, d1_ref, e_ref, s_ref, v_ref, pot_ref, moved_ref):
@@ -453,26 +466,21 @@
 def per_device(right_side, class_map, conductivity_table, velocity):
     nx, ny = lax.axis_size("sx"), lax.axis_size("sy")
 
-    def up(peers):
-        return [(i, i + 1) for i in range(peers - 1)]
-
-    def down(peers):
-        return [(i + 1, i) for i in range(peers - 1)]
-
-    own = message_of(conductivity_table, right_side, class_map)
-    yl = lax.ppermute(own, "sy", up(ny))
-    yr = lax.ppermute(own, "sy", down(ny))
-
-    def strip(at, cond_at):
-        parts = (own, yl, yr)
-        cond = [m[CX : CX + 2, cond_at : cond_at + PAD // 2] for m in parts]
-        cond = jnp.pad(jnp.stack(cond), ((0, 0), (0, 0), (0, 2), (0, 0)))
-        rows = [m[at : at + REACH] for m in parts]
-        return jnp.concatenate(rows + [cond.reshape(3, CY, NZ)], axis=0)
-
-    xl = lax.ppermute(strip(CX - REACH, CX // 2 - PAD // 2), "sx", up(nx))
-    xr = lax.ppermute(strip(0, 0), "sx", down(nx))
-    d1, e, cond, sums = krylov(ny, own, yl, yr, xl, xr)
+    def shifted(message, along_x, along_y):
+        moves = [
+            (p * ny + q, (p + along_x) * ny + q + along_y)
+            for p in range(nx)
+            for q in range(ny)
+            if 0 <= p + along_x < nx and 0 <= q + along_y < ny
+        ]
+        return lax.ppermute(message, ("sx", "sy"), moves)
+
+    own, low, high = message_of(conductivity_table, right_side, class_map)
+    yl = shifted(own, 0, 1)
+    yr = shifted(own, 0, -1)
+    strips = [shifted(high, 1, along_y) for along_y in (1, 0, -1)]
+    strips += [shifted(low, -1, along_y) for along_y in (1, 0, -1)]
+    d1, e, cond, sums = krylov(ny, own, yl, yr, strips)
     sums = lax.all_to_all(sums, "sy", split_axis=0, concat_axis=0, tiled=True)
     sums = jnp.broadcast_to(jnp.sum(sums, axis=0, keepdims=True), (nx, 1, NZ))
     sums = lax.all_to_all(sums, "sx", split_axis=0, concat_axis=0, tiled=True)

time: 119 us -> 129 us (1.084)
  starting transfers between devices: 17.2 us -> 25.9 us
  blocking collectives: 72.5 us -> 78.2 us
  waiting for transfers between devices: 10.5 us -> 5.74 us
    ppermute x4 -> x8, starting transfers between devices: 17.2 us -> 25.9 us  [shifted(): return lax.ppermute(message, ('sx', 'sy'), moves)]
    ppermute x4 -> x8, waiting for transfers between devices: 10.5 us -> 5.74 us  [shifted(): return lax.ppermute(message, ('sx', 'sy'), moves)]
    all_to_all x1, blocking collectives: 20 us -> 23.5 us  [per_device(): sums = lax.all_to_all(sums, 'sy', split_axis=0, concat_axis=0, tiled=True)]
    all_to_all x1, blocking collectives: 24.4 us -> 26.6 us  [per_device(): sums = lax.all_to_all(sums, 'sx', split_axis=0, concat_axis=0, tiled=True)]
  transfers between devices with their start and end apart: 4 -> 8, of which waited for: 3 -> 2; matrix products, arithmetic and copies ran while one was open for 1% -> 0% of each run, Pallas kernels for 0% -> 0%
where the time goes in v4:
time: 129 us; the launch traced here: 128 us
  blocking collectives  78.2 us (61%)
  starting transfers between devices  25.9 us (20%)
  Pallas kernels  16.5 us (13%)
  waiting for transfers between devices  5.74 us (4%)
    all_to_all x1, blocking collectives, per_device(): lax.all_to_all(moved.reshape(ny, CX // ny, 3, CY, NZ), 'sy', split_axis=0...  28.1 us
    all_to_all x1, blocking collectives, per_device(): sums = lax.all_to_all(sums, 'sx', split_axis=0, concat_axis=0, tiled=True)  26.6 us
    ppermute x8, starting transfers between devices, shifted(): return lax.ppermute(message, ('sx', 'sy'), moves)  25.9 us
    all_to_all x1, blocking collectives, per_device(): sums = lax.all_to_all(sums, 'sy', split_axis=0, concat_axis=0, tiled=True)  23.5 us
    pallas_call x1, Pallas kernels, krylov(): pl.pallas_call(functools.partial(krylov_kernel, copies), out_shape=(jax.S...  11 us
    ppermute x8, waiting for transfers between devices, shifted(): return lax.ppermute(message, ('sx', 'sy'), moves)  5.74 us
  transfers between devices with their start and end apart: 8, of which 2 were waited for; matrix products, arithmetic and copies ran while one was open for 0% of the time, Pallas kernels for 0%

profile of v4, /device:TPU:1, one launch (start us, length us, event | category | flops | bytes accessed | tf_op | source)
XLA Modules:
  0.0 128.2 jit_solution(11381620416185494227)
XLA Ops:
  0.6 0.0 copy-start.4
  0.6 1.8 %message.1 = (f32[34,16,128]{2,1,0:T(8,128)}, f32[11,16,128]{2,1,0:T(8,128)}, f32[11,16,128]{2,1,0:T(8,128)}) custom-call(f32[8]{0:T(128)} %table_ref.1, f32[32,16,128]{2,1,0:T(8,128)} %side_ref.1, s32[16,8,32]{2,1,0:T(8,128)} %class_ref.1), custom_call_target="tpu_custom_call" | custom-call | tf_op jit(solution)/shard_map/message/pallas_call | solution.py:110
  2.4 0.0 copy-start
  2.5 12.5 %collective-permute-start.1 = (f32[34,16,128]{2,1,0:T(8,128)}, f32[34,16,128]{2,1,0:T(8,128)S(1)}, u32[]{:S(2)}, u32[]{:S(2)}) collective-permute-start(f32[34,16,128]{2,1,0:T(8,128)} %get-tuple-element.11.own_ref), channel_id=1, source_target_pairs={{1,0},{2,1},{3,2},{4,3},{5,4},{6,5},{7,6},{8,7},{9,8},{10,9},{11,1... | collective-permute-start | bytes 835592 | tf_op jit(solution)/shard_map/ppermute | solution.py:476
  15.0 1.9 %collective-permute-start = (f32[34,16,128]{2,1,0:T(8,128)}, f32[34,16,128]{2,1,0:T(8,128)S(1)}, u32[]{:S(2)}, u32[]{:S(2)}) collective-permute-start(f32[34,16,128]{2,1,0:T(8,128)} %get-tuple-element.11.own_ref), channel_id=1, source_target_pairs={{0,1},{1,2},{2,3},{3,4},{4,5},{5,6},{6,7},{7,8},{8,9},{9,10},{10,1... | collective-permute-start | bytes 835592 | tf_op jit(solution)/shard_map/ppermute | solution.py:476
  16.9 1.3 %collective-permute-start.4 = (f32[11,16,128]{2,1,0:T(8,128)}, f32[11,16,128]{2,1,0:T(8,128)S(1)}, u32[]{:S(2)}, u32[]{:S(2)}) collective-permute-start(f32[11,16,128]{2,1,0:T(8,128)} %get-tuple-element.12), channel_id=1, source_target_pairs={{1,32},{2,33},{3,34},{4,35},{5,36},{6,37},{7,38},{8,39},{9,40},{10... | collective-permute-start | bytes 270344 | tf_op jit(solution)/shard_map/ppermute | solution.py:476
  18.2 1.3 %collective-permute-start.3 = (f32[11,16,128]{2,1,0:T(8,128)}, f32[11,16,128]{2,1,0:T(8,128)S(1)}, u32[]{:S(2)}, u32[]{:S(2)}) collective-permute-start(f32[11,16,128]{2,1,0:T(8,128)} %get-tuple-element.12), channel_id=1, source_target_pairs={{0,32},{1,33},{2,34},{3,35},{4,36},{5,37},{6,38},{7,39},{8,40},{9,... | collective-permute-start | bytes 270344 | tf_op jit(solution)/shard_map/ppermute | solution.py:476
  19.5 5.0 %collective-permute-start.2 = (f32[11,16,128]{2,1,0:T(8,128)}, f32[11,16,128]{2,1,0:T(8,128)S(1)}, u32[]{:S(2)}, u32[]{:S(2)}) collective-permute-start(f32[11,16,128]{2,1,0:T(8,128)} %get-tuple-element.12), channel_id=1, source_target_pairs={{0,33},{1,34},{2,35},{3,36},{4,37},{5,38},{6,39},{7,40},{8,41},{9,... | collective-permute-start | bytes 270344 | tf_op jit(solution)/shard_map/ppermute | solution.py:476
  24.5 0.0 collective-permute-done.4.lr_ref
  24.5 1.3 %collective-permute-start.7 = (f32[11,16,128]{2,1,0:T(8,128)}, f32[11,16,128]{2,1,0:T(8,128)S(1)}, u32[]{:S(2)}, u32[]{:S(2)}) collective-permute-start(f32[11,16,128]{2,1,0:T(8,128)} %get-tuple-element.13), channel_id=1, source_target_pairs={{33,0},{34,1},{35,2},{36,3},{37,4},{38,5},{39,6},{40,7},{41,8},{42... | collective-permute-start | bytes 270344 | tf_op jit(solution)/shard_map/ppermute | solution.py:476
  25.8 0.0 collective-permute-done.3.lo_ref
  25.8 1.3 %collective-permute-start.6 = (f32[11,16,128]{2,1,0:T(8,128)}, f32[11,16,128]{2,1,0:T(8,128)S(1)}, u32[]{:S(2)}, u32[]{:S(2)}) collective-permute-start(f32[11,16,128]{2,1,0:T(8,128)} %get-tuple-element.13), channel_id=1, source_target_pairs={{32,0},{33,1},{34,2},{35,3},{36,4},{37,5},{38,6},{39,7},{40,8},{41... | collective-permute-start | bytes 270344 | tf_op jit(solution)/shard_map/ppermute | solution.py:476
  27.1 0.0 collective-permute-done.2.ll_ref
  27.1 1.3 %collective-permute-start.5 = (f32[11,16,128]{2,1,0:T(8,128)}, f32[11,16,128]{2,1,0:T(8,128)S(1)}, u32[]{:S(2)}, u32[]{:S(2)}) collective-permute-start(f32[11,16,128]{2,1,0:T(8,128)} %get-tuple-element.13), channel_id=1, source_target_pairs={{32,1},{33,2},{34,3},{35,4},{36,5},{37,6},{38,7},{39,8},{40,9},{41... | collective-permute-start | bytes 270344 | tf_op jit(solution)/shard_map/ppermute | solution.py:476
  28.4 3.9 %collective-permute-done.7.rr_ref = f32[11,16,128]{2,1,0:T(8,128)S(1)} collective-permute-done((f32[11,16,128]{2,1,0:T(8,128)}, f32[11,16,128]{2,1,0:T(8,128)S(1)}, u32[]{:S(2)}, u32[]{:S(2)}) %collective-permute-start.7) | collective-permute-done | bytes 90144 | tf_op jit(solution)/shard_map/ppermute | solution.py:476
  32.4 1.8 %collective-permute-done.6.ro_ref = f32[11,16,128]{2,1,0:T(8,128)S(1)} collective-permute-done((f32[11,16,128]{2,1,0:T(8,128)}, f32[11,16,128]{2,1,0:T(8,128)S(1)}, u32[]{:S(2)}, u32[]{:S(2)}) %collective-permute-start.6) | collective-permute-done | bytes 90144 | tf_op jit(solution)/shard_map/ppermute | solution.py:476
  34.2 0.0 collective-permute-done.5.rl_ref
  34.2 0.0 collective-permute-done.1.yr_ref
  34.2 0.0 collective-permute-done.yl_ref
  34.2 0.0 copy-done.4
  34.2 0.0 copy-start.3
  34.2 0.9 copy-done.3
  35.1 11.0 %krylov.1 = (f32[34,24,128]{2,1,0:T(8,128)S(1)}, f32[34,24,128]{2,1,0:T(8,128)S(1)}, f32[32,24,128]{2,1,0:T(8,128)S(1)}, f32[32,1,128]{2,1,0:T(1,128)S(1)}) custom-call(f32[34,16,128]{2,1,0:T(8,128)S(1)} %copy-done.3, f32[34,16,128]{2,1,0:T(8,128)S(1)} %collective-permute-done.yl_ref, f32[34,16,128]{2,1,0:T(8,128)S(1)} %collective-permute-done.1.yr_ref, ...), custom_call_target="tpu_custom_call" | custom-call | tf_op jit(solution)/shard_map/krylov/pallas_call | solution.py:362
  46.2 23.5 %all_to_all.15 = f32[32,1,128]{2,1,0:T(1,128)S(1)} all-to-all(f32[32,1,128]{2,1,0:T(1,128)S(1)} %get-tuple-element.14), channel_id=1, replica_groups=mesh['sx'=24,'sy'=32] {'sy'}, dimensions={0} | all-to-all | bytes 32768 | tf_op jit(solution)/shard_map/all_to_all | solution.py:484
  69.7 0.1 reduce_sum.9
  69.8 26.6 %all_to_all.16.parts_ref = f32[24,1,128]{2,1,0:T(1,128)S(1)} all-to-all(f32[24,1,128]{2,1,0:T(1,128)S(1)} %broadcast_in_dim.2), channel_id=1, replica_groups=mesh['sx'=24,'sy'=32] {'sx'}, dimensions={0} | all-to-all | bytes 24576 | tf_op jit(solution)/shard_map/all_to_all | solution.py:486
  96.4 0.0 copy-done
  96.4 1.4 %velocity_step.1 = (f32[32,16,128]{2,1,0:T(8,128)}, f32[32,3,16,128]{3,2,1,0:T(8,128)S(1)}) custom-call(f32[24,1,128]{2,1,0:T(1,128)S(1)} %all_to_all.16.parts_ref, f32[34,24,128]{2,1,0:T(8,128)S(1)} %get-tuple-element.15.d1_ref, f32[34,24,128]{2,1,0:T(8,128)S(1)} %get-tuple-element.16.e_ref, f32[32,24,128]{2,1,0:T(8,128)S(1)} %get-tuple-element.17.s_ref, ...), custom_call_target="tpu_custom_call" | custom-call | tf_op jit(solution)/shard_map/velocity_step/pallas_call | solution.py:419
  97.8 0.0 copy-start.1
  97.8 0.0 copy-start.2
  97.8 28.1 %all_to_all.17.x_ref = f32[32,1,3,16,128]{4,3,2,1,0:T(8,128)S(1)} all-to-all(f32[32,1,3,16,128]{4,3,2,1,0:T(8,128)S(1)} %bitcast.1), channel_id=1, replica_groups=mesh['sx'=24,'sy'=32] {'sy'}, dimensions={0} | all-to-all | bytes 1572864 | tf_op jit(solution)/shard_map/all_to_all | solution.py:488
  125.9 0.0 copy-done.1
  125.9 0.0 copy-done.2
  125.9 2.3 %diffuse.1 = f32[3,1,512,128]{3,2,1,0:T(8,128)} custom-call(bf16[512,512]{1,0:T(8,128)(2,1)S(1)} %copy-done.2, bf16[512,512]{1,0:T(8,128)(2,1)S(1)} %copy-done.1, f32[32,1,3,16,128]{4,3,2,1,0:T(8,128)S(1)} %all_to_all.17.x_ref), custom_call_target="tpu_custom_call" | custom-call | tf_op jit(solution)/shard_map/diffuse/pallas_call | solution.py:458
  (1 shorter events, 0.0 us)
Async XLA Ops:
  0.6 33.5 %copy-start.4 = (bf16[128,128]{1,0:T(8,128)(2,1)S(1)}, bf16[128,128]{1,0:T(8,128)(2,1)}, u32[]{:S(2)}) copy-start(bf16[128,128]{1,0:T(8,128)(2,1)} %constant.8.clone.spread_ref) | copy-start | bytes 98308
  2.4 93.9 %copy-start = (f32[3,32,16,128]{3,2,1,0:T(8,128)S(1)}, f32[3,32,16,128]{3,2,1,0:T(8,128)}, u32[]{:S(2)}) copy-start(f32[3,32,16,128]{3,2,1,0:T(8,128)} %v_ref.1) | copy-start | bytes 2359300
  2.5 31.7 %collective-permute-start.1 = (f32[34,16,128]{2,1,0:T(8,128)}, f32[34,16,128]{2,1,0:T(8,128)S(1)}, u32[]{:S(2)}, u32[]{:S(2)}) collective-permute-start(f32[34,16,128]{2,1,0:T(8,128)} %get-tuple-element.11.own_ref), channel_id=1, source_target_pairs={{1,0},{2,1},{3,2},{4,3},{5,4},{6,5},{7,6},{8,7},{9,8},{10,9},{11,1... | collective-permute-start | bytes 835592 | tf_op jit(solution)/shard_map/ppermute | solution.py:476
  15.0 19.2 %collective-permute-start = (f32[34,16,128]{2,1,0:T(8,128)}, f32[34,16,128]{2,1,0:T(8,128)S(1)}, u32[]{:S(2)}, u32[]{:S(2)}) collective-permute-start(f32[34,16,128]{2,1,0:T(8,128)} %get-tuple-element.11.own_ref), channel_id=1, source_target_pairs={{0,1},{1,2},{2,3},{3,4},{4,5},{5,6},{6,7},{7,8},{8,9},{9,10},{10,1... | collective-permute-start | bytes 835592 | tf_op jit(solution)/shard_map/ppermute | solution.py:476
  16.9 7.6 %collective-permute-start.4 = (f32[11,16,128]{2,1,0:T(8,128)}, f32[11,16,128]{2,1,0:T(8,128)S(1)}, u32[]{:S(2)}, u32[]{:S(2)}) collective-permute-start(f32[11,16,128]{2,1,0:T(8,128)} %get-tuple-element.12), channel_id=1, source_target_pairs={{1,32},{2,33},{3,34},{4,35},{5,36},{6,37},{7,38},{8,39},{9,40},{10... | collective-permute-start | bytes 270344 | tf_op jit(solution)/shard_map/ppermute | solution.py:476
  18.2 7.6 %collective-permute-start.3 = (f32[11,16,128]{2,1,0:T(8,128)}, f32[11,16,128]{2,1,0:T(8,128)S(1)}, u32[]{:S(2)}, u32[]{:S(2)}) collective-permute-start(f32[11,16,128]{2,1,0:T(8,128)} %get-tuple-element.12), channel_id=1, source_target_pairs={{0,32},{1,33},{2,34},{3,35},{4,36},{5,37},{6,38},{7,39},{8,40},{9,... | collective-permute-start | bytes 270344 | tf_op jit(solution)/shard_map/ppermute | solution.py:476
  19.5 7.6 %collective-permute-start.2 = (f32[11,16,128]{2,1,0:T(8,128)}, f32[11,16,128]{2,1,0:T(8,128)S(1)}, u32[]{:S(2)}, u32[]{:S(2)}) collective-permute-start(f32[11,16,128]{2,1,0:T(8,128)} %get-tuple-element.12), channel_id=1, source_target_pairs={{0,33},{1,34},{2,35},{3,36},{4,37},{5,38},{6,39},{7,40},{8,41},{9,... | collective-permute-start | bytes 270344 | tf_op jit(solution)/shard_map/ppermute | solution.py:476
  24.5 7.9 %collective-permute-start.7 = (f32[11,16,128]{2,1,0:T(8,128)}, f32[11,16,128]{2,1,0:T(8,128)S(1)}, u32[]{:S(2)}, u32[]{:S(2)}) collective-permute-start(f32[11,16,128]{2,1,0:T(8,128)} %get-tuple-element.13), channel_id=1, source_target_pairs={{33,0},{34,1},{35,2},{36,3},{37,4},{38,5},{39,6},{40,7},{41,8},{42... | collective-permute-start | bytes 270344 | tf_op jit(solution)/shard_map/ppermute | solution.py:476
  25.8 8.3 %collective-permute-start.6 = (f32[11,16,128]{2,1,0:T(8,128)}, f32[11,16,128]{2,1,0:T(8,128)S(1)}, u32[]{:S(2)}, u32[]{:S(2)}) collective-permute-start(f32[11,16,128]{2,1,0:T(8,128)} %get-tuple-element.13), channel_id=1, source_target_pairs={{32,0},{33,1},{34,2},{35,3},{36,4},{37,5},{38,6},{39,7},{40,8},{41... | collective-permute-start | bytes 270344 | tf_op jit(solution)/shard_map/ppermute | solution.py:476
  27.1 7.0 %collective-permute-start.5 = (f32[11,16,128]{2,1,0:T(8,128)}, f32[11,16,128]{2,1,0:T(8,128)S(1)}, u32[]{:S(2)}, u32[]{:S(2)}) collective-permute-start(f32[11,16,128]{2,1,0:T(8,128)} %get-tuple-element.13), channel_id=1, source_target_pairs={{32,1},{33,2},{34,3},{35,4},{36,5},{37,6},{38,7},{39,8},{40,9},{41... | collective-permute-start | bytes 270344 | tf_op jit(solution)/shard_map/ppermute | solution.py:476
  34.2 1.0 copy-start.3
  97.8 28.1 %copy-start.1 = (bf16[512,512]{1,0:T(8,128)(2,1)S(1)}, bf16[512,512]{1,0:T(8,128)(2,1)}, u32[]{:S(2)}) copy-start(bf16[512,512]{1,0:T(8,128)(2,1)} %constant.10.clone.low_ref) | copy-start | bytes 1572868
  97.8 28.1 %copy-start.2 = (bf16[512,512]{1,0:T(8,128)(2,1)S(1)}, bf16[512,512]{1,0:T(8,128)(2,1)}, u32[]{:S(2)}) copy-start(bf16[512,512]{1,0:T(8,128)(2,1)} %constant.9.clone.high_ref) | copy-start | bytes 1572868

commit v5 on v3

--- a/solution.py
+++ b/solution.py
@@ -88,22 +88,39 @@
         body(start + whole * group, stop - start - whole * group)
 
 
-def message_kernel(table_ref, side_ref, class_ref, out_ref):
-    out_ref[0:CX] = side_ref[...]
+NEAR, NEXT, COND = 32, 8, 4
+ALONG_Y = NEAR + NEXT + COND
+
+
+def message_kernel(table_ref, side_ref, class_ref, up_ref, down_ref, low_ref, high_ref):
+    up_ref[0:CX] = side_ref[:, 8:16, :]
+    down_ref[0:CX] = side_ref[:, 0:8, :]
+    for x in range(CX):
+        at = slice(2 * (x % 4), 2 * (x % 4) + 2)
+        up_ref[NEAR + x // 4, at, :] = side_ref[x, 6:8, :]
+        down_ref[NEAR + x // 4, at, :] = side_ref[x, 8:10, :]
+    low_ref[0 : 2 * REACH] = side_ref[0:REACH].reshape(2 * REACH, 8, NZ)
+    high_ref[0 : 2 * REACH] = side_ref[CX - REACH : CX].reshape(2 * REACH, 8, NZ)
     for h in range(2):
         classes = jnp.concatenate([class_ref[:, 4 * h + m, :] for m in range(4)], axis=1)
         cond = jnp.zeros(classes.shape, f32)
         for k in range(CLASSES):
             cond = jnp.where(classes == k, table_ref[k], cond)
-        out_ref[CX + h] = cond
+        for k in range(2):
+            tile = cond[8 * k : 8 * k + 8]
+            up_ref[NEAR + NEXT + 2 * h + k] = tile
+            down_ref[NEAR + NEXT + 2 * h + k] = tile
+            (low_ref, high_ref)[k][2 * REACH + h] = tile
 
 
 def message_of(table, right_side, class_map):
     vmem = pl.BlockSpec(memory_space=pltpu.VMEM)
+    along_y = jax.ShapeDtypeStruct((ALONG_Y, 8, NZ), f32)
+    along_x = jax.ShapeDtypeStruct((2 * REACH + 2, 8, NZ), f32)
     return pl.pallas_call(
         message_kernel,
         in_specs=[pl.BlockSpec(memory_space=pltpu.SMEM), vmem, vmem],
-        out_shape=jax.ShapeDtypeStruct((CX + 2, CY, NZ), f32),
+        out_shape=(along_y, along_y, along_x, along_x),
         name="message",
     )(table, right_side, class_map)
 
@@ -111,6 +128,7 @@
 def krylov_kernel(
     copies,
     own_ref,
+    up_ref,
     yl_ref,
     yr_ref,
     xl_ref,
@@ -139,14 +157,14 @@
     tb,
 ):
     half = PAD // 2
-    for k, ref in enumerate((yl_ref, own_ref, yr_ref)):
-        for h in range(2):
-            sr[k, h, half : half + CX // 2, :] = ref[CX + h, :, :]
-    for k, src in enumerate((1, 0, 2)):
-        for h in range(2):
-            at = slice(8 * h, 8 * h + half)
-            sr[src, h, 0:half, :] = xl_ref[3 * REACH + k, at, :]
-            sr[src, h, half + CX // 2 : WX // 2, :] = xr_ref[3 * REACH + k, at, :]
+    for h in range(2):
+        for k, ref in enumerate((yl_ref, up_ref, yr_ref)):
+            at = NEAR + NEXT + 2 * h
+            sr[k, h, half : half + 8, :] = ref[at]
+            sr[k, h, half + 8 : half + 16, :] = ref[at + 1]
+        for k, at in enumerate((48, 20, 50)):
+            sr[k, h, 0:half, :] = xl_ref[at + h, 8 - half : 8, :]
+            sr[k, h, half + 16 : 2 * half + 16, :] = xr_ref[at + h, 0:half, :]
 
     sub = lax.broadcasted_iota(jnp.int32, (8, NZ), 0)
     lane8 = lax.broadcasted_iota(jnp.int32, (8, NZ), 1)
@@ -188,13 +206,25 @@
 
     loop(0, 4, spread_cells)
 
-    rw[PAD : PAD + CX, 0:PAD, :] = yl_ref[0:CX, CY - PAD : CY, :]
-    rw[PAD : PAD + CX, PAD : PAD + CY, :] = own_ref[0:CX, :, :]
-    rw[PAD : PAD + CX, PAD + CY : WY, :] = yr_ref[0:CX, 0:PAD, :]
-    for ref, at in ((xl_ref, PAD - REACH), (xr_ref, PAD + CX)):
-        rw[at : at + REACH, PAD : PAD + CY, :] = ref[0:REACH, :, :]
-        rw[at : at + REACH, 0:PAD, :] = ref[REACH : 2 * REACH, CY - PAD : CY, :]
-        rw[at : at + REACH, PAD + CY : WY, :] = ref[2 * REACH : 3 * REACH, 0:PAD, :]
+    def place(at, rows, own, first, near_l, near_r, next_l, next_r):
+        rw[at : at + rows, PAD : PAD + CY, :] = own
+        rw[at : at + rows, PAD - 8 : PAD, :] = near_l
+        rw[at : at + rows, PAD + CY : PAD + CY + 8, :] = near_r
+        rw[at : at + rows, 0:2, :] = jnp.zeros((rows, 2, NZ), f32)
+        rw[at : at + rows, WY - 2 : WY, :] = jnp.zeros((rows, 2, NZ), f32)
+        for i in range(rows):
+            x = first + i
+            tile, lines = x // 4 - first // 4, slice(2 * (x % 4), 2 * (x % 4) + 2)
+            for (ref, start), to in ((next_l, PAD - 10), (next_r, PAD + CY + 8)):
+                rw[at + i, to : to + 2, :] = ref[start + tile, lines, :]
+
+    place(
+        PAD, CX, own_ref[...], 0, yl_ref[0:CX], yr_ref[0:CX], (yl_ref, NEAR), (yr_ref, NEAR)
+    )
+    for ref, at, first in ((xl_ref, PAD - REACH, CX - REACH), (xr_ref, PAD + CX, 0)):
+        own = ref[0 : 2 * REACH].reshape(REACH, CY, NZ)
+        near_l, near_r = ref[22:32], ref[32:42]
+        place(at, REACH, own, first, near_l, near_r, (ref, 42), (ref, 45))
 
     def coefficient_row(e, xw, cut_up=False, cut_down=False):
         s5 = sw[xw]
@@ -341,7 +371,7 @@
     s_out[...] = sw[PAD : PAD + CX, 8:32, :]
 
 
-def krylov(copies, own, yl, yr, xl, xr):
+def krylov(copies, own, up, yl, yr, xl, xr):
     lane = np.arange(NZ)
     spread = jnp.asarray((lane[:, None] % 32 == lane[None, :] // 4).astype(np.float32), bf16)
     wide = pltpu.VMEM((WX, WY, NZ), f32)
@@ -366,7 +396,7 @@
         + [laid] * 10,
         compiler_params=pltpu.CompilerParams(vmem_limit_bytes=48 << 20),
         name="krylov",
-    )(own, yl, yr, xl, xr, spread)
+    )(own, up, yl, yr, xl, xr, spread)
 
 
 def velocity_kernel(parts_ref, d1_ref, e_ref, s_ref, v_ref, pot_ref, moved_ref):
@@ -459,20 +489,21 @@
     def down(peers):
         return [(i + 1, i) for i in range(peers - 1)]
 
-    own = message_of(conductivity_table, right_side, class_map)
-    yl = lax.ppermute(own, "sy", up(ny))
-    yr = lax.ppermute(own, "sy", down(ny))
-
-    def strip(at, cond_at):
-        parts = (own, yl, yr)
-        cond = [m[CX : CX + 2, cond_at : cond_at + PAD // 2] for m in parts]
-        cond = jnp.pad(jnp.stack(cond), ((0, 0), (0, 0), (0, 2), (0, 0)))
-        rows = [m[at : at + REACH] for m in parts]
-        return jnp.concatenate(rows + [cond.reshape(3, CY, NZ)], axis=0)
-
-    xl = lax.ppermute(strip(CX - REACH, CX // 2 - PAD // 2), "sx", up(nx))
-    xr = lax.ppermute(strip(0, 0), "sx", down(nx))
-    d1, e, cond, sums = krylov(ny, own, yl, yr, xl, xr)
+    to_up, to_down, low, high = message_of(conductivity_table, right_side, class_map)
+    yl = lax.ppermute(to_up, "sy", up(ny))
+    yr = lax.ppermute(to_down, "sy", down(ny))
+
+    def strip(own, at, next_at, k):
+        pieces = [own]
+        pieces += [m[at : at + REACH] for m in (yl, yr)]
+        pieces += [m[NEAR + next_at : NEAR + next_at + 3] for m in (yl, yr)]
+        for m in (yl, yr):
+            pieces += [m[NEAR + NEXT + 2 * h + k :][:1] for h in range(2)]
+        return jnp.concatenate(pieces, axis=0)
+
+    xl = lax.ppermute(strip(high, CX - REACH, 5, 1), "sx", up(nx))
+    xr = lax.ppermute(strip(low, 0, 0, 0), "sx", down(nx))
+    d1, e, cond, sums = krylov(ny, right_side, to_up, yl, yr, xl, xr)
     sums = lax.all_to_all(sums, "sy", split_axis=0, concat_axis=0, tiled=True)
     sums = jnp.broadcast_to(jnp.sum(sums, axis=0, keepdims=True), (nx, 1, NZ))
     sums = lax.all_to_all(sums, "sx", split_axis=0, concat_axis=0, tiled=True)

time: 119 us -> 117 us (0.983)
  waiting for transfers between devices: 10.5 us -> 5.77 us
  starting transfers between devices: 17.2 us -> 19.8 us
    ppermute x4, waiting for transfers between devices: 10.5 us -> 5.77 us  [the longest x1 3.26 us: per_device(): xr = lax.ppermute(strip(low, 0, 0, 0), 'sx', down(nx))]
    ppermute x4, starting transfers between devices: 17.2 us -> 19.8 us  [the longest x1 8.12 us: per_device(): yr = lax.ppermute(to_down, 'sy', down(ny))]
    all_to_all x1, blocking collectives: 20 us -> 17.6 us  [per_device(): sums = lax.all_to_all(sums, 'sy', split_axis=0, concat_axis=0, tiled=True)]
    all_to_all x1, blocking collectives: 24.4 us -> 26.7 us  [per_device(): sums = lax.all_to_all(sums, 'sx', split_axis=0, concat_axis=0, tiled=True)]
where the time goes in v5:
time: 117 us; the launch traced here: 116 us
  blocking collectives  72.4 us (62%)
  starting transfers between devices  19.8 us (17%)
  Pallas kernels  16.6 us (14%)
  waiting for transfers between devices  5.77 us (5%)
    all_to_all x1, blocking collectives, per_device(): lax.all_to_all(moved.reshape(ny, CX // ny, 3, CY, NZ), 'sy', split_axis=0...  28 us
    all_to_all x1, blocking collectives, per_device(): sums = lax.all_to_all(sums, 'sx', split_axis=0, concat_axis=0, tiled=True)  26.7 us
    all_to_all x1, blocking collectives, per_device(): sums = lax.all_to_all(sums, 'sy', split_axis=0, concat_axis=0, tiled=True)  17.6 us
    pallas_call x1, Pallas kernels, krylov(): pl.pallas_call(functools.partial(krylov_kernel, copies), out_shape=(jax.S...  11 us
    ppermute x1, starting transfers between devices, per_device(): yr = lax.ppermute(to_down, 'sy', down(ny))  8.12 us
    ppermute x1, starting transfers between devices, per_device(): yl = lax.ppermute(to_up, 'sy', up(ny))  5.6 us
    ppermute x1, starting transfers between devices, per_device(): xl = lax.ppermute(strip(high, CX - REACH, 5, 1), 'sx', up(nx))  4.64 us
    ppermute x1, waiting for transfers between devices, per_device(): xr = lax.ppermute(strip(low, 0, 0, 0), 'sx', down(nx))  3.26 us
  transfers between devices with their start and end apart: 4, of which 3 were waited for; matrix products, arithmetic and copies ran while one was open for 1% of the time, Pallas kernels for 0%

profile of v5, /device:TPU:1, one launch (start us, length us, event | category | flops | bytes accessed | tf_op | source)
XLA Modules:
  0.0 116.4 jit_solution(13116888722166430087)
XLA Ops:
  0.6 1.8 %message.1 = (f32[44,8,128]{2,1,0:T(8,128)}, f32[44,8,128]{2,1,0:T(8,128)}, f32[22,8,128]{2,1,0:T(8,128)}, f32[22,8,128]{2,1,0:T(8,128)}) custom-call(f32[8]{0:T(128)} %table_ref.1, f32[32,16,128]{2,1,0:T(8,128)} %own_ref.1, s32[16,8,32]{2,1,0:T(8,128)} %class_ref.1), custom_call_target="tpu_custom_call" | custom-call | tf_op jit(solution)/shard_map/message/pallas_call | solution.py:120
  2.5 5.6 %collective-permute-start = (f32[44,8,128]{2,1,0:T(8,128)}, f32[44,8,128]{2,1,0:T(8,128)S(1)}, u32[]{:S(2)}, u32[]{:S(2)}) collective-permute-start(f32[44,8,128]{2,1,0:T(8,128)} %get-tuple-element.12.up_ref), channel_id=1, source_target_pairs={{0,1},{1,2},{2,3},{3,4},{4,5},{5,6},{6,7},{7,8},{8,9},{9,10},{10,1... | collective-permute-start | bytes 540680 | tf_op jit(solution)/shard_map/ppermute | solution.py:493
  8.1 8.1 %collective-permute-start.1 = (f32[44,8,128]{2,1,0:T(8,128)}, f32[44,8,128]{2,1,0:T(8,128)S(1)}, u32[]{:S(2)}, u32[]{:S(2)}) collective-permute-start(f32[44,8,128]{2,1,0:T(8,128)} %get-tuple-element.13), channel_id=1, source_target_pairs={{1,0},{2,1},{3,2},{4,3},{5,4},{6,5},{7,6},{8,7},{9,8},{10,9},{11,1... | collective-permute-start | bytes 540680 | tf_op jit(solution)/shard_map/ppermute | solution.py:494
  16.2 0.9 constant_dynamic-update-slice_fusion.6
  17.2 0.0 collective-permute-done.yl_ref
  17.2 0.0 copy-start
  17.2 0.0 copy-start.4
  17.2 0.7 collective-permute-done.1.yr_ref
  17.9 0.0 copy-start.5
  17.9 0.0 copy-start.1
  18.0 1.4 %collective-permute-start.3 = (f32[52,8,128]{2,1,0:T(8,128)S(1)}, f32[52,8,128]{2,1,0:T(8,128)S(1)}, u32[]{:S(2)}, u32[]{:S(2)}) collective-permute-start(f32[52,8,128]{2,1,0:T(8,128)S(1)} %get-tuple-element.22), channel_id=1, source_target_pairs={{32,0},{64,32},{96,64},{128,96},{160,128},{192,160},{224,192},{256... | collective-permute-start | bytes 638984 | tf_op jit(solution)/shard_map/ppermute | solution.py:505
  19.5 4.6 %collective-permute-start.2 = (f32[52,8,128]{2,1,0:T(8,128)S(1)}, f32[52,8,128]{2,1,0:T(8,128)S(1)}, u32[]{:S(2)}, u32[]{:S(2)}) collective-permute-start(f32[52,8,128]{2,1,0:T(8,128)S(1)} %get-tuple-element.23), channel_id=1, source_target_pairs={{0,32},{32,64},{64,96},{96,128},{128,160},{160,192},{192,224},{224... | collective-permute-start | bytes 638984 | tf_op jit(solution)/shard_map/ppermute | solution.py:504
  24.1 3.3 %collective-permute-done.3.xr_ref = f32[52,8,128]{2,1,0:T(8,128)S(1)} collective-permute-done((f32[52,8,128]{2,1,0:T(8,128)S(1)}, f32[52,8,128]{2,1,0:T(8,128)S(1)}, u32[]{:S(2)}, u32[]{:S(2)}) %collective-permute-start.3) | collective-permute-done | bytes 213024 | tf_op jit(solution)/shard_map/ppermute | solution.py:505
  27.4 1.8 %collective-permute-done.2.xl_ref = f32[52,8,128]{2,1,0:T(8,128)S(1)} collective-permute-done((f32[52,8,128]{2,1,0:T(8,128)S(1)}, f32[52,8,128]{2,1,0:T(8,128)S(1)}, u32[]{:S(2)}, u32[]{:S(2)}) %collective-permute-start.2) | collective-permute-done | bytes 213024 | tf_op jit(solution)/shard_map/ppermute | solution.py:504
  29.1 0.0 copy-done
  29.1 0.0 copy-done.4
  29.1 0.0 copy-done.5
  29.2 11.0 %krylov.1 = (f32[34,24,128]{2,1,0:T(8,128)S(1)}, f32[34,24,128]{2,1,0:T(8,128)S(1)}, f32[32,24,128]{2,1,0:T(8,128)S(1)}, f32[32,1,128]{2,1,0:T(1,128)S(1)}) custom-call(f32[32,16,128]{2,1,0:T(8,128)S(1)} %copy-done, f32[44,8,128]{2,1,0:T(8,128)S(1)} %copy-done.4, f32[44,8,128]{2,1,0:T(8,128)S(1)} %collective-permute-done.yl_ref, ...), custom_call_target="tpu_custom_call" | custom-call | tf_op jit(solution)/shard_map/krylov/pallas_call | solution.py:379
  40.2 17.6 %all_to_all.15 = f32[32,1,128]{2,1,0:T(1,128)S(1)} all-to-all(f32[32,1,128]{2,1,0:T(1,128)S(1)} %get-tuple-element.16), channel_id=1, replica_groups=mesh['sx'=24,'sy'=32] {'sy'}, dimensions={0} | all-to-all | bytes 32768 | tf_op jit(solution)/shard_map/all_to_all | solution.py:507
  57.8 0.1 reduce_sum.9
  57.9 26.7 %all_to_all.16.parts_ref = f32[24,1,128]{2,1,0:T(1,128)S(1)} all-to-all(f32[24,1,128]{2,1,0:T(1,128)S(1)} %broadcast_in_dim.2), channel_id=1, replica_groups=mesh['sx'=24,'sy'=32] {'sx'}, dimensions={0} | all-to-all | bytes 24576 | tf_op jit(solution)/shard_map/all_to_all | solution.py:509
  84.6 0.0 copy-done.1
  84.6 1.4 %velocity_step.1 = (f32[32,16,128]{2,1,0:T(8,128)}, f32[32,3,16,128]{3,2,1,0:T(8,128)S(1)}) custom-call(f32[24,1,128]{2,1,0:T(1,128)S(1)} %all_to_all.16.parts_ref, f32[34,24,128]{2,1,0:T(8,128)S(1)} %get-tuple-element.17.d1_ref, f32[34,24,128]{2,1,0:T(8,128)S(1)} %get-tuple-element.18.e_ref, f32[32,24,128]{2,1,0:T(8,128)S(1)} %get-tuple-element.19.s_ref, ...), custom_call_target="tpu_custom_call" | custom-call | tf_op jit(solution)/shard_map/velocity_step/pallas_call | solution.py:436
  86.1 0.0 copy-start.2
  86.1 0.0 copy-start.3
  86.1 28.0 %all_to_all.17.x_ref = f32[32,1,3,16,128]{4,3,2,1,0:T(8,128)S(1)} all-to-all(f32[32,1,3,16,128]{4,3,2,1,0:T(8,128)S(1)} %bitcast.1), channel_id=1, replica_groups=mesh['sx'=24,'sy'=32] {'sy'}, dimensions={0} | all-to-all | bytes 1572864 | tf_op jit(solution)/shard_map/all_to_all | solution.py:511
  114.1 0.0 copy-done.2
  114.1 0.0 copy-done.3
  114.1 2.3 %diffuse.1 = f32[3,1,512,128]{3,2,1,0:T(8,128)} custom-call(bf16[512,512]{1,0:T(8,128)(2,1)S(1)} %copy-done.3, bf16[512,512]{1,0:T(8,128)(2,1)S(1)} %copy-done.2, f32[32,1,3,16,128]{4,3,2,1,0:T(8,128)S(1)} %all_to_all.17.x_ref), custom_call_target="tpu_custom_call" | custom-call | tf_op jit(solution)/shard_map/diffuse/pallas_call | solution.py:475
  (9 shorter events, 0.1 us)
Async XLA Ops:
  2.5 14.7 %collective-permute-start = (f32[44,8,128]{2,1,0:T(8,128)}, f32[44,8,128]{2,1,0:T(8,128)S(1)}, u32[]{:S(2)}, u32[]{:S(2)}) collective-permute-start(f32[44,8,128]{2,1,0:T(8,128)} %get-tuple-element.12.up_ref), channel_id=1, source_target_pairs={{0,1},{1,2},{2,3},{3,4},{4,5},{5,6},{6,7},{7,8},{8,9},{9,10},{10,1... | collective-permute-start | bytes 540680 | tf_op jit(solution)/shard_map/ppermute | solution.py:493
  8.1 9.9 %collective-permute-start.1 = (f32[44,8,128]{2,1,0:T(8,128)}, f32[44,8,128]{2,1,0:T(8,128)S(1)}, u32[]{:S(2)}, u32[]{:S(2)}) collective-permute-start(f32[44,8,128]{2,1,0:T(8,128)} %get-tuple-element.13), channel_id=1, source_target_pairs={{1,0},{2,1},{3,2},{4,3},{5,4},{6,5},{7,6},{8,7},{9,8},{10,9},{11,1... | collective-permute-start | bytes 540680 | tf_op jit(solution)/shard_map/ppermute | solution.py:494
  17.2 12.0 %copy-start = (f32[32,16,128]{2,1,0:T(8,128)S(1)}, f32[32,16,128]{2,1,0:T(8,128)}, u32[]{:S(2)}) copy-start(f32[32,16,128]{2,1,0:T(8,128)} %own_ref.1) | copy-start | bytes 786436
  17.2 12.0 %copy-start.4 = (f32[44,8,128]{2,1,0:T(8,128)S(1)}, f32[44,8,128]{2,1,0:T(8,128)}, u32[]{:S(2)}) copy-start(f32[44,8,128]{2,1,0:T(8,128)} %get-tuple-element.12.up_ref) | copy-start | bytes 540676
  17.9 11.2 %copy-start.5 = (bf16[128,128]{1,0:T(8,128)(2,1)S(1)}, bf16[128,128]{1,0:T(8,128)(2,1)}, u32[]{:S(2)}) copy-start(bf16[128,128]{1,0:T(8,128)(2,1)} %constant.8.clone.spread_ref) | copy-start | bytes 98308
  17.9 66.7 %copy-start.1 = (f32[3,32,16,128]{3,2,1,0:T(8,128)S(1)}, f32[3,32,16,128]{3,2,1,0:T(8,128)}, u32[]{:S(2)}) copy-start(f32[3,32,16,128]{3,2,1,0:T(8,128)} %v_ref.1) | copy-start | bytes 2359300
  18.0 9.3 %collective-permute-start.3 = (f32[52,8,128]{2,1,0:T(8,128)S(1)}, f32[52,8,128]{2,1,0:T(8,128)S(1)}, u32[]{:S(2)}, u32[]{:S(2)}) collective-permute-start(f32[52,8,128]{2,1,0:T(8,128)S(1)} %get-tuple-element.22), channel_id=1, source_target_pairs={{32,0},{64,32},{96,64},{128,96},{160,128},{192,160},{224,192},{256... | collective-permute-start | bytes 638984 | tf_op jit(solution)/shard_map/ppermute | solution.py:505
  19.5 9.7 %collective-permute-start.2 = (f32[52,8,128]{2,1,0:T(8,128)S(1)}, f32[52,8,128]{2,1,0:T(8,128)S(1)}, u32[]{:S(2)}, u32[]{:S(2)}) collective-permute-start(f32[52,8,128]{2,1,0:T(8,128)S(1)} %get-tuple-element.23), channel_id=1, source_target_pairs={{0,32},{32,64},{64,96},{96,128},{128,160},{160,192},{192,224},{224... | collective-permute-start | bytes 638984 | tf_op jit(solution)/shard_map/ppermute | solution.py:504
  86.1 28.1 %copy-start.2 = (bf16[512,512]{1,0:T(8,128)(2,1)S(1)}, bf16[512,512]{1,0:T(8,128)(2,1)}, u32[]{:S(2)}) copy-start(bf16[512,512]{1,0:T(8,128)(2,1)} %constant.10.clone.low_ref) | copy-start | bytes 1572868
  86.1 28.1 %copy-start.3 = (bf16[512,512]{1,0:T(8,128)(2,1)S(1)}, bf16[512,512]{1,0:T(8,128)(2,1)}, u32[]{:S(2)}) copy-start(bf16[512,512]{1,0:T(8,128)(2,1)} %constant.9.clone.high_ref) | copy-start | bytes 1572868

commit v6 on v5

--- a/solution.py
+++ b/solution.py
@@ -92,13 +92,25 @@
 ALONG_Y = NEAR + NEXT + COND
 
 
-def message_kernel(table_ref, side_ref, class_ref, up_ref, down_ref, low_ref, high_ref):
-    up_ref[0:CX] = side_ref[:, 8:16, :]
-    down_ref[0:CX] = side_ref[:, 0:8, :]
-    for x in range(CX):
-        at = slice(2 * (x % 4), 2 * (x % 4) + 2)
-        up_ref[NEAR + x // 4, at, :] = side_ref[x, 6:8, :]
-        down_ref[NEAR + x // 4, at, :] = side_ref[x, 8:10, :]
+def message_kernel(
+    odd_ref, table_ref, side_ref, class_ref, first_ref, second_ref, low_ref, high_ref
+):
+    def sides(up_ref, down_ref):
+        up_ref[0:CX] = side_ref[:, 8:16, :]
+        down_ref[0:CX] = side_ref[:, 0:8, :]
+        for x in range(CX):
+            at = slice(2 * (x % 4), 2 * (x % 4) + 2)
+            up_ref[NEAR + x // 4, at, :] = side_ref[x, 6:8, :]
+            down_ref[NEAR + x // 4, at, :] = side_ref[x, 8:10, :]
+
+    @pl.when(odd_ref[0] == 0)
+    def _():
+        sides(first_ref, second_ref)
+
+    @pl.when(odd_ref[0] == 1)
+    def _():
+        sides(second_ref, first_ref)
+
     low_ref[0 : 2 * REACH] = side_ref[0:REACH].reshape(2 * REACH, 8, NZ)
     high_ref[0 : 2 * REACH] = side_ref[CX - REACH : CX].reshape(2 * REACH, 8, NZ)
     for h in range(2):
@@ -108,29 +120,31 @@
             cond = jnp.where(classes == k, table_ref[k], cond)
         for k in range(2):
             tile = cond[8 * k : 8 * k + 8]
-            up_ref[NEAR + NEXT + 2 * h + k] = tile
-            down_ref[NEAR + NEXT + 2 * h + k] = tile
+            first_ref[NEAR + NEXT + 2 * h + k] = tile
+            second_ref[NEAR + NEXT + 2 * h + k] = tile
             (low_ref, high_ref)[k][2 * REACH + h] = tile
 
 
-def message_of(table, right_side, class_map):
+def message_of(odd, table, right_side, class_map):
     vmem = pl.BlockSpec(memory_space=pltpu.VMEM)
+    smem = pl.BlockSpec(memory_space=pltpu.SMEM)
     along_y = jax.ShapeDtypeStruct((ALONG_Y, 8, NZ), f32)
     along_x = jax.ShapeDtypeStruct((2 * REACH + 2, 8, NZ), f32)
     return pl.pallas_call(
         message_kernel,
-        in_specs=[pl.BlockSpec(memory_space=pltpu.SMEM), vmem, vmem],
+        in_specs=[smem, smem, vmem, vmem],
         out_shape=(along_y, along_y, along_x, along_x),
         name="message",
-    )(table, right_side, class_map)
+    )(odd, table, right_side, class_map)
 
 
 def krylov_kernel(
     copies,
+    odd_ref,
     own_ref,
-    up_ref,
-    yl_ref,
-    yr_ref,
+    mine_ref,
+    ya_ref,
+    yb_ref,
     xl_ref,
     xr_ref,
     spread_ref,
@@ -157,14 +171,42 @@
     tb,
 ):
     half = PAD // 2
-    for h in range(2):
-        for k, ref in enumerate((yl_ref, up_ref, yr_ref)):
-            at = NEAR + NEXT + 2 * h
-            sr[k, h, half : half + 8, :] = ref[at]
-            sr[k, h, half + 8 : half + 16, :] = ref[at + 1]
-        for k, at in enumerate((48, 20, 50)):
-            sr[k, h, 0:half, :] = xl_ref[at + h, 8 - half : 8, :]
-            sr[k, h, half + 16 : 2 * half + 16, :] = xr_ref[at + h, 0:half, :]
+
+    def place(at, rows, own, first, near_l, near_r, next_l, next_r):
+        rw[at : at + rows, PAD : PAD + CY, :] = own
+        rw[at : at + rows, PAD - 8 : PAD, :] = near_l
+        rw[at : at + rows, PAD + CY : PAD + CY + 8, :] = near_r
+        rw[at : at + rows, 0:2, :] = jnp.zeros((rows, 2, NZ), f32)
+        rw[at : at + rows, WY - 2 : WY, :] = jnp.zeros((rows, 2, NZ), f32)
+        for i in range(rows):
+            x = first + i
+            tile, lines = x // 4 - first // 4, slice(2 * (x % 4), 2 * (x % 4) + 2)
+            for (ref, start), to in ((next_l, PAD - 10), (next_r, PAD + CY + 8)):
+                rw[at + i, to : to + 2, :] = ref[start + tile, lines, :]
+
+    def unpack(yl_ref, yr_ref, l, r):
+        for h in range(2):
+            for k, ref in enumerate((yl_ref, mine_ref, yr_ref)):
+                at = NEAR + NEXT + 2 * h
+                sr[k, h, half : half + 8, :] = ref[at]
+                sr[k, h, half + 8 : half + 16, :] = ref[at + 1]
+            for k, at in enumerate((48 + 2 * l, 20, 48 + 2 * r)):
+                sr[k, h, 0:half, :] = xl_ref[at + h, 8 - half : 8, :]
+                sr[k, h, half + 16 : 2 * half + 16, :] = xr_ref[at + h, 0:half, :]
+        next_y = (yl_ref, NEAR), (yr_ref, NEAR)
+        place(PAD, CX, own_ref[...], 0, yl_ref[0:CX], yr_ref[0:CX], *next_y)
+        for ref, at, first in ((xl_ref, PAD - REACH, CX - REACH), (xr_ref, PAD + CX, 0)):
+            own = ref[0 : 2 * REACH].reshape(REACH, CY, NZ)
+            near_l, near_r = (ref[22 + 10 * k : 32 + 10 * k] for k in (l, r))
+            place(at, REACH, own, first, near_l, near_r, (ref, 42 + 3 * l), (ref, 42 + 3 * r))
+
+    @pl.when(odd_ref[0] == 0)
+    def _():
+        unpack(yb_ref, ya_ref, 1, 0)
+
+    @pl.when(odd_ref[0] == 1)
+    def _():
+        unpack(ya_ref, yb_ref, 0, 1)
 
     sub = lax.broadcasted_iota(jnp.int32, (8, NZ), 0)
     lane8 = lax.broadcasted_iota(jnp.int32, (8, NZ), 1)
@@ -205,26 +247,6 @@
             sw[14 * c + 2 * k + 1, :, :] = out[k]
 
     loop(0, 4, spread_cells)
-
-    def place(at, rows, own, first, near_l, near_r, next_l, next_r):
-        rw[at : at + rows, PAD : PAD + CY, :] = own
-        rw[at : at + rows, PAD - 8 : PAD, :] = near_l
-        rw[at : at + rows, PAD + CY : PAD + CY + 8, :] = near_r
-        rw[at : at + rows, 0:2, :] = jnp.zeros((rows, 2, NZ), f32)
-        rw[at : at + rows, WY - 2 : WY, :] = jnp.zeros((rows, 2, NZ), f32)
-        for i in range(rows):
-            x = first + i
-            tile, lines = x // 4 - first // 4, slice(2 * (x % 4), 2 * (x % 4) + 2)
-            for (ref, start), to in ((next_l, PAD - 10), (next_r, PAD + CY + 8)):
-                rw[at + i, to : to + 2, :] = ref[start + tile, lines, :]
-
-    place(
-        PAD, CX, own_ref[...], 0, yl_ref[0:CX], yr_ref[0:CX], (yl_ref, NEAR), (yr_ref, NEAR)
-    )
-    for ref, at, first in ((xl_ref, PAD - REACH, CX - REACH), (xr_ref, PAD + CX, 0)):
-        own = ref[0 : 2 * REACH].reshape(REACH, CY, NZ)
-        near_l, near_r = ref[22:32], ref[32:42]
-        place(at, REACH, own, first, near_l, near_r, (ref, 42), (ref, 45))
 
     def coefficient_row(e, xw, cut_up=False, cut_down=False):
         s5 = sw[xw]
@@ -371,13 +393,15 @@
     s_out[...] = sw[PAD : PAD + CX, 8:32, :]
 
 
-def krylov(copies, own, up, yl, yr, xl, xr):
+def krylov(copies, odd, own, mine, ya, yb, xl, xr):
+    smem, vmem = (pl.BlockSpec(memory_space=m) for m in (pltpu.SMEM, pltpu.VMEM))
     lane = np.arange(NZ)
     spread = jnp.asarray((lane[:, None] % 32 == lane[None, :] // 4).astype(np.float32), bf16)
     wide = pltpu.VMEM((WX, WY, NZ), f32)
     laid = pltpu.VMEM((EX, EY, NZ), f32)
     return pl.pallas_call(
         functools.partial(krylov_kernel, copies),
+        in_specs=[smem] + [vmem] * 7,
         out_shape=(
             jax.ShapeDtypeStruct((CX + 2, 24, NZ), f32),
             jax.ShapeDtypeStruct((CX + 2, 24, NZ), f32),
@@ -396,7 +420,7 @@
         + [laid] * 10,
         compiler_params=pltpu.CompilerParams(vmem_limit_bytes=48 << 20),
         name="krylov",
-    )(own, up, yl, yr, xl, xr, spread)
+    )(odd, own, mine, ya, yb, xl, xr, spread)
 
 
 def velocity_kernel(parts_ref, d1_ref, e_ref, s_ref, v_ref, pot_ref, moved_ref):
@@ -489,21 +513,27 @@
     def down(peers):
         return [(i + 1, i) for i in range(peers - 1)]
 
-    to_up, to_down, low, high = message_of(conductivity_table, right_side, class_map)
-    yl = lax.ppermute(to_up, "sy", up(ny))
-    yr = lax.ppermute(to_down, "sy", down(ny))
+    odd = (lax.axis_index("sy") % 2).astype(jnp.int32).reshape(1)
+    first, second, low, high = message_of(odd, conductivity_table, right_side, class_map)
+
+    def pairs(start):
+        firsts = range(start, ny - 1, 2)
+        return [(i, i + 1) for i in firsts] + [(i + 1, i) for i in firsts]
+
+    ya = lax.ppermute(first, "sy", pairs(0))
+    yb = lax.ppermute(second, "sy", pairs(1))
 
     def strip(own, at, next_at, k):
         pieces = [own]
-        pieces += [m[at : at + REACH] for m in (yl, yr)]
-        pieces += [m[NEAR + next_at : NEAR + next_at + 3] for m in (yl, yr)]
-        for m in (yl, yr):
+        pieces += [m[at : at + REACH] for m in (ya, yb)]
+        pieces += [m[NEAR + next_at : NEAR + next_at + 3] for m in (ya, yb)]
+        for m in (ya, yb):
             pieces += [m[NEAR + NEXT + 2 * h + k :][:1] for h in range(2)]
         return jnp.concatenate(pieces, axis=0)
 
     xl = lax.ppermute(strip(high, CX - REACH, 5, 1), "sx", up(nx))
     xr = lax.ppermute(strip(low, 0, 0, 0), "sx", down(nx))
-    d1, e, cond, sums = krylov(ny, right_side, to_up, yl, yr, xl, xr)
+    d1, e, cond, sums = krylov(ny, odd, right_side, first, ya, yb, xl, xr)
     sums = lax.all_to_all(sums, "sy", split_axis=0, concat_axis=0, tiled=True)
     sums = jnp.broadcast_to(jnp.sum(sums, axis=0, keepdims=True), (nx, 1, NZ))
     sums = lax.all_to_all(sums, "sx", split_axis=0, concat_axis=0, tiled=True)

time: 117 us -> 117 us (level)
  blocking collectives: 72.4 us -> 70.2 us
  waiting for transfers between devices: 5.77 us -> 7.75 us
    ppermute x2, waiting for transfers between devices: 0.73 us -> 5 us  [the longest x1 4.99 us: per_device(): yb = lax.ppermute(second, 'sy', pairs(1))]
    all_to_all x1, blocking collectives: 17.6 us -> 15.4 us  [per_device(): sums = lax.all_to_all(sums, 'sy', split_axis=0, concat_axis=0, tiled=True)]
    ppermute x1, waiting for transfers between devices: 3.26 us -> 1.28 us  [per_device(): xr = lax.ppermute(strip(low, 0, 0, 0), 'sx', down(nx))]
where the time goes in v6:
time: 117 us; the launch traced here: 116 us
  blocking collectives  70.2 us (60%)
  starting transfers between devices  19.8 us (17%)
  Pallas kernels  16.7 us (14%)
  waiting for transfers between devices  7.75 us (7%)
    all_to_all x1, blocking collectives, per_device(): lax.all_to_all(moved.reshape(ny, CX // ny, 3, CY, NZ), 'sy', split_axis=0...  28 us
    all_to_all x1, blocking collectives, per_device(): sums = lax.all_to_all(sums, 'sx', split_axis=0, concat_axis=0, tiled=True)  26.7 us
    all_to_all x1, blocking collectives, per_device(): sums = lax.all_to_all(sums, 'sy', split_axis=0, concat_axis=0, tiled=True)  15.4 us
    ppermute x1, starting transfers between devices, per_device(): ya = lax.ppermute(first, 'sy', pairs(0))  12.4 us
    pallas_call x1, Pallas kernels, krylov(): pl.pallas_call(functools.partial(krylov_kernel, copies), in_specs=[smem]...  11.1 us
    ppermute x1, waiting for transfers between devices, per_device(): yb = lax.ppermute(second, 'sy', pairs(1))  4.99 us
    ppermute x1, starting transfers between devices, per_device(): xl = lax.ppermute(strip(high, CX - REACH, 5, 1), 'sx', up(nx))  4 us
  transfers between devices with their start and end apart: 4, of which 3 were waited for; matrix products, arithmetic and copies ran while one was open for 1% of the time, Pallas kernels for 0%

profile of v6, /device:TPU:1, one launch (start us, length us, event | category | flops | bytes accessed | tf_op | source)
XLA Modules:
  0.0 116.3 jit_solution(3067562677578484989)
XLA Ops:
  0.6 1.9 %message.1 = (f32[44,8,128]{2,1,0:T(8,128)}, f32[44,8,128]{2,1,0:T(8,128)}, f32[22,8,128]{2,1,0:T(8,128)}, f32[22,8,128]{2,1,0:T(8,128)}) custom-call(s32[1]{0:T(128)} %bitcast.odd_ref, f32[8]{0:T(128)} %table_ref.1, f32[32,16,128]{2,1,0:T(8,128)} %own_ref.1, s32[16,8,32]{2,1,0:T(8,128)} %class_ref.1), custom_call_target="tpu_custom_call" | custom-call | tf_op jit(solution)/shard_map/message/pallas_call | solution.py:133
  2.5 12.4 %collective-permute-start = (f32[44,8,128]{2,1,0:T(8,128)}, f32[44,8,128]{2,1,0:T(8,128)S(1)}, u32[]{:S(2)}, u32[]{:S(2)}) collective-permute-start(f32[44,8,128]{2,1,0:T(8,128)} %get-tuple-element.12.mine_ref), channel_id=1, source_target_pairs={{0,1},{2,3},{4,5},{6,7},{8,9},{10,11},{12,13},{14,15},{16,17},{18,... | collective-permute-start | bytes 540680 | tf_op jit(solution)/shard_map/ppermute | solution.py:523
  15.0 1.9 %collective-permute-start.1 = (f32[44,8,128]{2,1,0:T(8,128)}, f32[44,8,128]{2,1,0:T(8,128)S(1)}, u32[]{:S(2)}, u32[]{:S(2)}) collective-permute-start(f32[44,8,128]{2,1,0:T(8,128)} %get-tuple-element.13), channel_id=1, source_target_pairs={{1,2},{3,4},{5,6},{7,8},{9,10},{11,12},{13,14},{15,16},{17,18},{19... | collective-permute-start | bytes 540680 | tf_op jit(solution)/shard_map/ppermute | solution.py:524
  16.9 0.9 constant_dynamic-update-slice_fusion.6
  17.8 0.0 collective-permute-done.ya_ref
  17.8 0.0 copy-start
  17.9 0.0 copy-start.4
  17.9 5.0 %collective-permute-done.1.yb_ref = f32[44,8,128]{2,1,0:T(8,128)S(1)} collective-permute-done((f32[44,8,128]{2,1,0:T(8,128)}, f32[44,8,128]{2,1,0:T(8,128)S(1)}, u32[]{:S(2)}, u32[]{:S(2)}) %collective-permute-start.1) | collective-permute-done | bytes 180256 | tf_op jit(solution)/shard_map/ppermute | solution.py:524
  22.9 0.0 copy-start.5
  22.9 0.0 copy-start.1
  23.0 1.4 %collective-permute-start.3 = (f32[52,8,128]{2,1,0:T(8,128)S(1)}, f32[52,8,128]{2,1,0:T(8,128)S(1)}, u32[]{:S(2)}, u32[]{:S(2)}) collective-permute-start(f32[52,8,128]{2,1,0:T(8,128)S(1)} %get-tuple-element.22), channel_id=1, source_target_pairs={{32,0},{64,32},{96,64},{128,96},{160,128},{192,160},{224,192},{256... | collective-permute-start | bytes 638984 | tf_op jit(solution)/shard_map/ppermute | solution.py:535
  24.4 4.0 %collective-permute-start.2 = (f32[52,8,128]{2,1,0:T(8,128)S(1)}, f32[52,8,128]{2,1,0:T(8,128)S(1)}, u32[]{:S(2)}, u32[]{:S(2)}) collective-permute-start(f32[52,8,128]{2,1,0:T(8,128)S(1)} %get-tuple-element.23), channel_id=1, source_target_pairs={{0,32},{32,64},{64,96},{96,128},{128,160},{160,192},{192,224},{224... | collective-permute-start | bytes 638984 | tf_op jit(solution)/shard_map/ppermute | solution.py:534
  28.4 1.3 %collective-permute-done.3.xr_ref = f32[52,8,128]{2,1,0:T(8,128)S(1)} collective-permute-done((f32[52,8,128]{2,1,0:T(8,128)S(1)}, f32[52,8,128]{2,1,0:T(8,128)S(1)}, u32[]{:S(2)}, u32[]{:S(2)}) %collective-permute-start.3) | collective-permute-done | bytes 213024 | tf_op jit(solution)/shard_map/ppermute | solution.py:535
  29.7 1.5 %collective-permute-done.2.xl_ref = f32[52,8,128]{2,1,0:T(8,128)S(1)} collective-permute-done((f32[52,8,128]{2,1,0:T(8,128)S(1)}, f32[52,8,128]{2,1,0:T(8,128)S(1)}, u32[]{:S(2)}, u32[]{:S(2)}) %collective-permute-start.2) | collective-permute-done | bytes 213024 | tf_op jit(solution)/shard_map/ppermute | solution.py:534
  31.2 0.0 copy-done
  31.2 0.0 copy-done.4
  31.2 0.0 copy-done.5
  31.2 11.1 %krylov.1 = (f32[34,24,128]{2,1,0:T(8,128)S(1)}, f32[34,24,128]{2,1,0:T(8,128)S(1)}, f32[32,24,128]{2,1,0:T(8,128)S(1)}, f32[32,1,128]{2,1,0:T(1,128)S(1)}) custom-call(s32[1]{0:T(128)} %bitcast.odd_ref, f32[32,16,128]{2,1,0:T(8,128)S(1)} %copy-done, f32[44,8,128]{2,1,0:T(8,128)S(1)} %copy-done.4, f32[44,8,128]{2,1,0:T(8,128)S(1)} %collective-permute-done.ya_ref, ...), custom_call_target="tpu_custom_call" | custom-call | tf_op jit(solution)/shard_map/krylov/pallas_call | solution.py:402
  42.3 15.4 %all_to_all.15 = f32[32,1,128]{2,1,0:T(1,128)S(1)} all-to-all(f32[32,1,128]{2,1,0:T(1,128)S(1)} %get-tuple-element.16), channel_id=1, replica_groups=mesh['sx'=24,'sy'=32] {'sy'}, dimensions={0} | all-to-all | bytes 32768 | tf_op jit(solution)/shard_map/all_to_all | solution.py:537
  57.7 0.1 reduce_sum.9
  57.7 26.7 %all_to_all.16.parts_ref = f32[24,1,128]{2,1,0:T(1,128)S(1)} all-to-all(f32[24,1,128]{2,1,0:T(1,128)S(1)} %broadcast_in_dim.2), channel_id=1, replica_groups=mesh['sx'=24,'sy'=32] {'sx'}, dimensions={0} | all-to-all | bytes 24576 | tf_op jit(solution)/shard_map/all_to_all | solution.py:539
  84.5 0.0 copy-done.1
  84.5 1.4 %velocity_step.1 = (f32[32,16,128]{2,1,0:T(8,128)}, f32[32,3,16,128]{3,2,1,0:T(8,128)S(1)}) custom-call(f32[24,1,128]{2,1,0:T(1,128)S(1)} %all_to_all.16.parts_ref, f32[34,24,128]{2,1,0:T(8,128)S(1)} %get-tuple-element.17.d1_ref, f32[34,24,128]{2,1,0:T(8,128)S(1)} %get-tuple-element.18.e_ref, f32[32,24,128]{2,1,0:T(8,128)S(1)} %get-tuple-element.19.s_ref, ...), custom_call_target="tpu_custom_call" | custom-call | tf_op jit(solution)/shard_map/velocity_step/pallas_call | solution.py:460
  85.9 0.0 copy-start.2
  85.9 0.0 copy-start.3
  85.9 28.0 %all_to_all.17.x_ref = f32[32,1,3,16,128]{4,3,2,1,0:T(8,128)S(1)} all-to-all(f32[32,1,3,16,128]{4,3,2,1,0:T(8,128)S(1)} %bitcast.2), channel_id=1, replica_groups=mesh['sx'=24,'sy'=32] {'sy'}, dimensions={0} | all-to-all | bytes 1572864 | tf_op jit(solution)/shard_map/all_to_all | solution.py:541
  114.0 0.0 copy-done.2
  114.0 0.0 copy-done.3
  114.0 2.3 %diffuse.1 = f32[3,1,512,128]{3,2,1,0:T(8,128)} custom-call(bf16[512,512]{1,0:T(8,128)(2,1)S(1)} %copy-done.3, bf16[512,512]{1,0:T(8,128)(2,1)S(1)} %copy-done.2, f32[32,1,3,16,128]{4,3,2,1,0:T(8,128)S(1)} %all_to_all.17.x_ref), custom_call_target="tpu_custom_call" | custom-call | tf_op jit(solution)/shard_map/diffuse/pallas_call | solution.py:499
  (9 shorter events, 0.1 us)
Async XLA Ops:
  2.5 15.3 %collective-permute-start = (f32[44,8,128]{2,1,0:T(8,128)}, f32[44,8,128]{2,1,0:T(8,128)S(1)}, u32[]{:S(2)}, u32[]{:S(2)}) collective-permute-start(f32[44,8,128]{2,1,0:T(8,128)} %get-tuple-element.12.mine_ref), channel_id=1, source_target_pairs={{0,1},{2,3},{4,5},{6,7},{8,9},{10,11},{12,13},{14,15},{16,17},{18,... | collective-permute-start | bytes 540680 | tf_op jit(solution)/shard_map/ppermute | solution.py:523
  15.0 7.9 %collective-permute-start.1 = (f32[44,8,128]{2,1,0:T(8,128)}, f32[44,8,128]{2,1,0:T(8,128)S(1)}, u32[]{:S(2)}, u32[]{:S(2)}) collective-permute-start(f32[44,8,128]{2,1,0:T(8,128)} %get-tuple-element.13), channel_id=1, source_target_pairs={{1,2},{3,4},{5,6},{7,8},{9,10},{11,12},{13,14},{15,16},{17,18},{19... | collective-permute-start | bytes 540680 | tf_op jit(solution)/shard_map/ppermute | solution.py:524
  17.8 13.3 %copy-start = (f32[32,16,128]{2,1,0:T(8,128)S(1)}, f32[32,16,128]{2,1,0:T(8,128)}, u32[]{:S(2)}) copy-start(f32[32,16,128]{2,1,0:T(8,128)} %own_ref.1) | copy-start | bytes 786436
  17.9 13.3 %copy-start.4 = (f32[44,8,128]{2,1,0:T(8,128)S(1)}, f32[44,8,128]{2,1,0:T(8,128)}, u32[]{:S(2)}) copy-start(f32[44,8,128]{2,1,0:T(8,128)} %get-tuple-element.12.mine_ref) | copy-start | bytes 540676
  22.9 8.3 %copy-start.5 = (bf16[128,128]{1,0:T(8,128)(2,1)S(1)}, bf16[128,128]{1,0:T(8,128)(2,1)}, u32[]{:S(2)}) copy-start(bf16[128,128]{1,0:T(8,128)(2,1)} %constant.25.clone.spread_ref) | copy-start | bytes 98308
  22.9 61.6 %copy-start.1 = (f32[3,32,16,128]{3,2,1,0:T(8,128)S(1)}, f32[3,32,16,128]{3,2,1,0:T(8,128)}, u32[]{:S(2)}) copy-start(f32[3,32,16,128]{3,2,1,0:T(8,128)} %v_ref.1) | copy-start | bytes 2359300
  23.0 6.7 %collective-permute-start.3 = (f32[52,8,128]{2,1,0:T(8,128)S(1)}, f32[52,8,128]{2,1,0:T(8,128)S(1)}, u32[]{:S(2)}, u32[]{:S(2)}) collective-permute-start(f32[52,8,128]{2,1,0:T(8,128)S(1)} %get-tuple-element.22), channel_id=1, source_target_pairs={{32,0},{64,32},{96,64},{128,96},{160,128},{192,160},{224,192},{256... | collective-permute-start | bytes 638984 | tf_op jit(solution)/shard_map/ppermute | solution.py:535
  24.4 6.8 %collective-permute-start.2 = (f32[52,8,128]{2,1,0:T(8,128)S(1)}, f32[52,8,128]{2,1,0:T(8,128)S(1)}, u32[]{:S(2)}, u32[]{:S(2)}) collective-permute-start(f32[52,8,128]{2,1,0:T(8,128)S(1)} %get-tuple-element.23), channel_id=1, source_target_pairs={{0,32},{32,64},{64,96},{96,128},{128,160},{160,192},{192,224},{224... | collective-permute-start | bytes 638984 | tf_op jit(solution)/shard_map/ppermute | solution.py:534
  85.9 28.1 %copy-start.2 = (bf16[512,512]{1,0:T(8,128)(2,1)S(1)}, bf16[512,512]{1,0:T(8,128)(2,1)}, u32[]{:S(2)}) copy-start(bf16[512,512]{1,0:T(8,128)(2,1)} %constant.27.clone.low_ref) | copy-start | bytes 1572868
  85.9 28.1 %copy-start.3 = (bf16[512,512]{1,0:T(8,128)(2,1)S(1)}, bf16[512,512]{1,0:T(8,128)(2,1)}, u32[]{:S(2)}) copy-start(bf16[512,512]{1,0:T(8,128)(2,1)} %constant.26.clone.high_ref) | copy-start | bytes 1572868

commit v7 on v6

--- a/solution.py
+++ b/solution.py
@@ -17,7 +17,7 @@
 EY = 56
 AXIAL = 1.0 / 16.0
 COUPLING = 0.25
-GROUP, GROUP_C, GROUP_I, GROUP_P = 19, 13, 21, 16
+GROUP, GROUP_C, GROUP_I, GROUP_P = 40, 13, 21, 16
 f32 = jnp.float32
 bf16 = jnp.bfloat16
 
@@ -480,14 +480,15 @@
 def diffusion_kernel(high_ref, low_ref, x_ref, out_ref):
     high, low = high_ref[...], low_ref[...]
     for i in range(x_ref.shape[1]):
+        parts = [x_ref[:, i, c, :, :].reshape(high.shape[0], NZ) for c in range(3)]
+        x = jnp.concatenate(parts, axis=1)
+        big = x.astype(bf16)
+        small = (x - big.astype(f32)).astype(bf16)
+        total = jnp.dot(high, small, preferred_element_type=f32)
+        total = total + jnp.dot(low, big, preferred_element_type=f32)
+        total = total + jnp.dot(high, big, preferred_element_type=f32)
         for c in range(3):
-            x = x_ref[:, i, c, :, :].reshape(high.shape[0], NZ)
-            big = x.astype(bf16)
-            small = (x - big.astype(f32)).astype(bf16)
-            total = jnp.dot(high, small, preferred_element_type=f32)
-            total = total + jnp.dot(low, big, preferred_element_type=f32)
-            total = total + jnp.dot(high, big, preferred_element_type=f32)
-            out_ref[c, i] = total - x
+            out_ref[c, i] = total[:, NZ * c : NZ * (c + 1)] - parts[c]
 
 
 def diffuse(lines, cells_side):

time: 117 us -> 116 us (level)
  no operation moved by 1% of the time
where the time goes in v7:
time: 116 us
  blocking collectives  70.2 us (61%)
  starting transfers between devices  19.8 us (17%)
  Pallas kernels  15.9 us (14%)
  waiting for transfers between devices  7.75 us (7%)
    all_to_all x1, blocking collectives, per_device(): lax.all_to_all(moved.reshape(ny, CX // ny, 3, CY, NZ), 'sy', split_axis=0...  28 us
    all_to_all x1, blocking collectives, per_device(): sums = lax.all_to_all(sums, 'sx', split_axis=0, concat_axis=0, tiled=True)  26.7 us
    all_to_all x1, blocking collectives, per_device(): sums = lax.all_to_all(sums, 'sy', split_axis=0, concat_axis=0, tiled=True)  15.4 us
    ppermute x1, starting transfers between devices, per_device(): ya = lax.ppermute(first, 'sy', pairs(0))  12.4 us
    pallas_call x1, Pallas kernels, krylov(): pl.pallas_call(functools.partial(krylov_kernel, copies), in_specs=[smem]...  10.7 us
    ppermute x1, waiting for transfers between devices, per_device(): yb = lax.ppermute(second, 'sy', pairs(1))  4.99 us
    ppermute x1, starting transfers between devices, per_device(): xl = lax.ppermute(strip(high, CX - REACH, 5, 1), 'sx', up(nx))  4 us
  transfers between devices with their start and end apart: 4, of which 3 were waited for; matrix products, arithmetic and copies ran while one was open for 1% of the time, Pallas kernels for 0%

profile of v7, /device:TPU:1, one launch (start us, length us, event | category | flops | bytes accessed | tf_op | source)
XLA Modules:
  0.0 115.5 jit_solution(17358678011595461343)
XLA Ops:
  0.6 1.9 %message.1 = (f32[44,8,128]{2,1,0:T(8,128)}, f32[44,8,128]{2,1,0:T(8,128)}, f32[22,8,128]{2,1,0:T(8,128)}, f32[22,8,128]{2,1,0:T(8,128)}) custom-call(s32[1]{0:T(128)} %bitcast.odd_ref, f32[8]{0:T(128)} %table_ref.1, f32[32,16,128]{2,1,0:T(8,128)} %own_ref.1, s32[16,8,32]{2,1,0:T(8,128)} %class_ref.1), custom_call_target="tpu_custom_call" | custom-call | tf_op jit(solution)/shard_map/message/pallas_call | solution.py:133
  2.5 12.4 %collective-permute-start = (f32[44,8,128]{2,1,0:T(8,128)}, f32[44,8,128]{2,1,0:T(8,128)S(1)}, u32[]{:S(2)}, u32[]{:S(2)}) collective-permute-start(f32[44,8,128]{2,1,0:T(8,128)} %get-tuple-element.12.mine_ref), channel_id=1, source_target_pairs={{0,1},{2,3},{4,5},{6,7},{8,9},{10,11},{12,13},{14,15},{16,17},{18,... | collective-permute-start | bytes 540680 | tf_op jit(solution)/shard_map/ppermute | solution.py:524
  15.0 1.9 %collective-permute-start.1 = (f32[44,8,128]{2,1,0:T(8,128)}, f32[44,8,128]{2,1,0:T(8,128)S(1)}, u32[]{:S(2)}, u32[]{:S(2)}) collective-permute-start(f32[44,8,128]{2,1,0:T(8,128)} %get-tuple-element.13), channel_id=1, source_target_pairs={{1,2},{3,4},{5,6},{7,8},{9,10},{11,12},{13,14},{15,16},{17,18},{19... | collective-permute-start | bytes 540680 | tf_op jit(solution)/shard_map/ppermute | solution.py:525
  16.9 0.9 constant_dynamic-update-slice_fusion.6
  17.8 0.0 collective-permute-done.ya_ref
  17.8 0.0 copy-start
  17.9 0.0 copy-start.4
  17.9 5.0 %collective-permute-done.1.yb_ref = f32[44,8,128]{2,1,0:T(8,128)S(1)} collective-permute-done((f32[44,8,128]{2,1,0:T(8,128)}, f32[44,8,128]{2,1,0:T(8,128)S(1)}, u32[]{:S(2)}, u32[]{:S(2)}) %collective-permute-start.1) | collective-permute-done | bytes 180256 | tf_op jit(solution)/shard_map/ppermute | solution.py:525
  22.9 0.0 copy-start.5
  22.9 0.0 copy-start.1
  23.0 1.4 %collective-permute-start.3 = (f32[52,8,128]{2,1,0:T(8,128)S(1)}, f32[52,8,128]{2,1,0:T(8,128)S(1)}, u32[]{:S(2)}, u32[]{:S(2)}) collective-permute-start(f32[52,8,128]{2,1,0:T(8,128)S(1)} %get-tuple-element.22), channel_id=1, source_target_pairs={{32,0},{64,32},{96,64},{128,96},{160,128},{192,160},{224,192},{256... | collective-permute-start | bytes 638984 | tf_op jit(solution)/shard_map/ppermute | solution.py:536
  24.4 4.0 %collective-permute-start.2 = (f32[52,8,128]{2,1,0:T(8,128)S(1)}, f32[52,8,128]{2,1,0:T(8,128)S(1)}, u32[]{:S(2)}, u32[]{:S(2)}) collective-permute-start(f32[52,8,128]{2,1,0:T(8,128)S(1)} %get-tuple-element.23), channel_id=1, source_target_pairs={{0,32},{32,64},{64,96},{96,128},{128,160},{160,192},{192,224},{224... | collective-permute-start | bytes 638984 | tf_op jit(solution)/shard_map/ppermute | solution.py:535
  28.4 1.3 %collective-permute-done.3.xr_ref = f32[52,8,128]{2,1,0:T(8,128)S(1)} collective-permute-done((f32[52,8,128]{2,1,0:T(8,128)S(1)}, f32[52,8,128]{2,1,0:T(8,128)S(1)}, u32[]{:S(2)}, u32[]{:S(2)}) %collective-permute-start.3) | collective-permute-done | bytes 213024 | tf_op jit(solution)/shard_map/ppermute | solution.py:536
  29.7 1.5 %collective-permute-done.2.xl_ref = f32[52,8,128]{2,1,0:T(8,128)S(1)} collective-permute-done((f32[52,8,128]{2,1,0:T(8,128)S(1)}, f32[52,8,128]{2,1,0:T(8,128)S(1)}, u32[]{:S(2)}, u32[]{:S(2)}) %collective-permute-start.2) | collective-permute-done | bytes 213024 | tf_op jit(solution)/shard_map/ppermute | solution.py:535
  31.2 0.0 copy-done
  31.2 0.0 copy-done.4
  31.2 0.0 copy-done.5
  31.2 10.7 %krylov.1 = (f32[34,24,128]{2,1,0:T(8,128)S(1)}, f32[34,24,128]{2,1,0:T(8,128)S(1)}, f32[32,24,128]{2,1,0:T(8,128)S(1)}, f32[32,1,128]{2,1,0:T(1,128)S(1)}) custom-call(s32[1]{0:T(128)} %bitcast.odd_ref, f32[32,16,128]{2,1,0:T(8,128)S(1)} %copy-done, f32[44,8,128]{2,1,0:T(8,128)S(1)} %copy-done.4, f32[44,8,128]{2,1,0:T(8,128)S(1)} %collective-permute-done.ya_ref, ...), custom_call_target="tpu_custom_call" | custom-call | tf_op jit(solution)/shard_map/krylov/pallas_call | solution.py:402
  41.9 15.4 %all_to_all.15 = f32[32,1,128]{2,1,0:T(1,128)S(1)} all-to-all(f32[32,1,128]{2,1,0:T(1,128)S(1)} %get-tuple-element.16), channel_id=1, replica_groups=mesh['sx'=24,'sy'=32] {'sy'}, dimensions={0} | all-to-all | bytes 32768 | tf_op jit(solution)/shard_map/all_to_all | solution.py:538
  57.3 0.1 reduce_sum.9
  57.4 26.7 %all_to_all.16.parts_ref = f32[24,1,128]{2,1,0:T(1,128)S(1)} all-to-all(f32[24,1,128]{2,1,0:T(1,128)S(1)} %broadcast_in_dim.2), channel_id=1, replica_groups=mesh['sx'=24,'sy'=32] {'sx'}, dimensions={0} | all-to-all | bytes 24576 | tf_op jit(solution)/shard_map/all_to_all | solution.py:540
  84.2 0.0 copy-done.1
  84.2 1.4 %velocity_step.1 = (f32[32,16,128]{2,1,0:T(8,128)}, f32[32,3,16,128]{3,2,1,0:T(8,128)S(1)}) custom-call(f32[24,1,128]{2,1,0:T(1,128)S(1)} %all_to_all.16.parts_ref, f32[34,24,128]{2,1,0:T(8,128)S(1)} %get-tuple-element.17.d1_ref, f32[34,24,128]{2,1,0:T(8,128)S(1)} %get-tuple-element.18.e_ref, f32[32,24,128]{2,1,0:T(8,128)S(1)} %get-tuple-element.19.s_ref, ...), custom_call_target="tpu_custom_call" | custom-call | tf_op jit(solution)/shard_map/velocity_step/pallas_call | solution.py:460
  85.6 0.0 copy-start.2
  85.6 0.0 copy-start.3
  85.6 28.0 %all_to_all.17.x_ref = f32[32,1,3,16,128]{4,3,2,1,0:T(8,128)S(1)} all-to-all(f32[32,1,3,16,128]{4,3,2,1,0:T(8,128)S(1)} %bitcast.2), channel_id=1, replica_groups=mesh['sx'=24,'sy'=32] {'sy'}, dimensions={0} | all-to-all | bytes 1572864 | tf_op jit(solution)/shard_map/all_to_all | solution.py:542
  113.6 0.0 copy-done.2
  113.6 0.0 copy-done.3
  113.6 1.9 %diffuse.1 = f32[3,1,512,128]{3,2,1,0:T(8,128)} custom-call(bf16[512,512]{1,0:T(8,128)(2,1)S(1)} %copy-done.3, bf16[512,512]{1,0:T(8,128)(2,1)S(1)} %copy-done.2, f32[32,1,3,16,128]{4,3,2,1,0:T(8,128)S(1)} %all_to_all.17.x_ref), custom_call_target="tpu_custom_call" | custom-call | tf_op jit(solution)/shard_map/diffuse/pallas_call | solution.py:500
  (9 shorter events, 0.1 us)
Async XLA Ops:
  2.5 15.3 %collective-permute-start = (f32[44,8,128]{2,1,0:T(8,128)}, f32[44,8,128]{2,1,0:T(8,128)S(1)}, u32[]{:S(2)}, u32[]{:S(2)}) collective-permute-start(f32[44,8,128]{2,1,0:T(8,128)} %get-tuple-element.12.mine_ref), channel_id=1, source_target_pairs={{0,1},{2,3},{4,5},{6,7},{8,9},{10,11},{12,13},{14,15},{16,17},{18,... | collective-permute-start | bytes 540680 | tf_op jit(solution)/shard_map/ppermute | solution.py:524
  15.0 7.9 %collective-permute-start.1 = (f32[44,8,128]{2,1,0:T(8,128)}, f32[44,8,128]{2,1,0:T(8,128)S(1)}, u32[]{:S(2)}, u32[]{:S(2)}) collective-permute-start(f32[44,8,128]{2,1,0:T(8,128)} %get-tuple-element.13), channel_id=1, source_target_pairs={{1,2},{3,4},{5,6},{7,8},{9,10},{11,12},{13,14},{15,16},{17,18},{19... | collective-permute-start | bytes 540680 | tf_op jit(solution)/shard_map/ppermute | solution.py:525
  17.8 13.3 %copy-start = (f32[32,16,128]{2,1,0:T(8,128)S(1)}, f32[32,16,128]{2,1,0:T(8,128)}, u32[]{:S(2)}) copy-start(f32[32,16,128]{2,1,0:T(8,128)} %own_ref.1) | copy-start | bytes 786436
  17.9 13.3 %copy-start.4 = (f32[44,8,128]{2,1,0:T(8,128)S(1)}, f32[44,8,128]{2,1,0:T(8,128)}, u32[]{:S(2)}) copy-start(f32[44,8,128]{2,1,0:T(8,128)} %get-tuple-element.12.mine_ref) | copy-start | bytes 540676
  22.9 8.3 %copy-start.5 = (bf16[128,128]{1,0:T(8,128)(2,1)S(1)}, bf16[128,128]{1,0:T(8,128)(2,1)}, u32[]{:S(2)}) copy-start(bf16[128,128]{1,0:T(8,128)(2,1)} %constant.25.clone.spread_ref) | copy-start | bytes 98308
  22.9 61.3 %copy-start.1 = (f32[3,32,16,128]{3,2,1,0:T(8,128)S(1)}, f32[3,32,16,128]{3,2,1,0:T(8,128)}, u32[]{:S(2)}) copy-start(f32[3,32,16,128]{3,2,1,0:T(8,128)} %v_ref.1) | copy-start | bytes 2359300
  23.0 6.7 %collective-permute-start.3 = (f32[52,8,128]{2,1,0:T(8,128)S(1)}, f32[52,8,128]{2,1,0:T(8,128)S(1)}, u32[]{:S(2)}, u32[]{:S(2)}) collective-permute-start(f32[52,8,128]{2,1,0:T(8,128)S(1)} %get-tuple-element.22), channel_id=1, source_target_pairs={{32,0},{64,32},{96,64},{128,96},{160,128},{192,160},{224,192},{256... | collective-permute-start | bytes 638984 | tf_op jit(solution)/shard_map/ppermute | solution.py:536
  24.4 6.8 %collective-permute-start.2 = (f32[52,8,128]{2,1,0:T(8,128)S(1)}, f32[52,8,128]{2,1,0:T(8,128)S(1)}, u32[]{:S(2)}, u32[]{:S(2)}) collective-permute-start(f32[52,8,128]{2,1,0:T(8,128)S(1)} %get-tuple-element.23), channel_id=1, source_target_pairs={{0,32},{32,64},{64,96},{96,128},{128,160},{160,192},{192,224},{224... | collective-permute-start | bytes 638984 | tf_op jit(solution)/shard_map/ppermute | solution.py:535
  85.6 28.1 %copy-start.2 = (bf16[512,512]{1,0:T(8,128)(2,1)S(1)}, bf16[512,512]{1,0:T(8,128)(2,1)}, u32[]{:S(2)}) copy-start(bf16[512,512]{1,0:T(8,128)(2,1)} %constant.27.clone.low_ref) | copy-start | bytes 1572868
  85.6 28.1 %copy-start.3 = (bf16[512,512]{1,0:T(8,128)(2,1)S(1)}, bf16[512,512]{1,0:T(8,128)(2,1)}, u32[]{:S(2)}) copy-start(bf16[512,512]{1,0:T(8,128)(2,1)} %constant.26.clone.high_ref) | copy-start | bytes 1572868

commit v8 on v7

--- a/solution.py
+++ b/solution.py
@@ -451,8 +451,13 @@
         moved_ref[i, 2] = v_ref[2, i]
         return here, after
 
+    def rows(k, before_here):
+        for i in range(8):
+            before_here = row(8 * k + i, before_here)
+        return before_here
+
     lax.fori_loop(
-        0, CX, row, (p1 * d1_ref[0] + p2 * e_ref[0], p1 * d1_ref[1] + p2 * e_ref[1])
+        0, CX // 8, rows, (p1 * d1_ref[0] + p2 * e_ref[0], p1 * d1_ref[1] + p2 * e_ref[1])
     )
 
 

time: 116 us -> 116 us (level)
  no operation moved by 1% of the time
where the time goes in v8:
time: 116 us; the launch traced here: 115 us
  blocking collectives  70.2 us (61%)
  starting transfers between devices  19.8 us (17%)
  Pallas kernels  15.7 us (14%)
  waiting for transfers between devices  7.75 us (7%)
    all_to_all x1, blocking collectives, per_device(): lax.all_to_all(moved.reshape(ny, CX // ny, 3, CY, NZ), 'sy', split_axis=0...  28 us
    all_to_all x1, blocking collectives, per_device(): sums = lax.all_to_all(sums, 'sx', split_axis=0, concat_axis=0, tiled=True)  26.7 us
    all_to_all x1, blocking collectives, per_device(): sums = lax.all_to_all(sums, 'sy', split_axis=0, concat_axis=0, tiled=True)  15.4 us
    ppermute x1, starting transfers between devices, per_device(): ya = lax.ppermute(first, 'sy', pairs(0))  12.4 us
    pallas_call x1, Pallas kernels, krylov(): pl.pallas_call(functools.partial(krylov_kernel, copies), in_specs=[smem]...  10.7 us
    ppermute x1, waiting for transfers between devices, per_device(): yb = lax.ppermute(second, 'sy', pairs(1))  4.99 us
    ppermute x1, starting transfers between devices, per_device(): xl = lax.ppermute(strip(high, CX - REACH, 5, 1), 'sx', up(nx))  4 us
  transfers between devices with their start and end apart: 4, of which 3 were waited for; matrix products, arithmetic and copies ran while one was open for 1% of the time, Pallas kernels for 0%

profile of v8, /device:TPU:1, one launch (start us, length us, event | category | flops | bytes accessed | tf_op | source)
XLA Modules:
  0.0 115.3 jit_solution(13634334712743518881)
XLA Ops:
  0.6 1.9 %message.1 = (f32[44,8,128]{2,1,0:T(8,128)}, f32[44,8,128]{2,1,0:T(8,128)}, f32[22,8,128]{2,1,0:T(8,128)}, f32[22,8,128]{2,1,0:T(8,128)}) custom-call(s32[1]{0:T(128)} %bitcast.odd_ref, f32[8]{0:T(128)} %table_ref.1, f32[32,16,128]{2,1,0:T(8,128)} %own_ref.1, s32[16,8,32]{2,1,0:T(8,128)} %class_ref.1), custom_call_target="tpu_custom_call" | custom-call | tf_op jit(solution)/shard_map/message/pallas_call | solution.py:133
  2.5 12.4 %collective-permute-start = (f32[44,8,128]{2,1,0:T(8,128)}, f32[44,8,128]{2,1,0:T(8,128)S(1)}, u32[]{:S(2)}, u32[]{:S(2)}) collective-permute-start(f32[44,8,128]{2,1,0:T(8,128)} %get-tuple-element.12.mine_ref), channel_id=1, source_target_pairs={{0,1},{2,3},{4,5},{6,7},{8,9},{10,11},{12,13},{14,15},{16,17},{18,... | collective-permute-start | bytes 540680 | tf_op jit(solution)/shard_map/ppermute | solution.py:529
  15.0 1.9 %collective-permute-start.1 = (f32[44,8,128]{2,1,0:T(8,128)}, f32[44,8,128]{2,1,0:T(8,128)S(1)}, u32[]{:S(2)}, u32[]{:S(2)}) collective-permute-start(f32[44,8,128]{2,1,0:T(8,128)} %get-tuple-element.13), channel_id=1, source_target_pairs={{1,2},{3,4},{5,6},{7,8},{9,10},{11,12},{13,14},{15,16},{17,18},{19... | collective-permute-start | bytes 540680 | tf_op jit(solution)/shard_map/ppermute | solution.py:530
  16.9 0.9 constant_dynamic-update-slice_fusion.6
  17.8 0.0 collective-permute-done.ya_ref
  17.8 0.0 copy-start
  17.9 0.0 copy-start.4
  17.9 5.0 %collective-permute-done.1.yb_ref = f32[44,8,128]{2,1,0:T(8,128)S(1)} collective-permute-done((f32[44,8,128]{2,1,0:T(8,128)}, f32[44,8,128]{2,1,0:T(8,128)S(1)}, u32[]{:S(2)}, u32[]{:S(2)}) %collective-permute-start.1) | collective-permute-done | bytes 180256 | tf_op jit(solution)/shard_map/ppermute | solution.py:530
  22.9 0.0 copy-start.5
  22.9 0.0 copy-start.1
  23.0 1.4 %collective-permute-start.3 = (f32[52,8,128]{2,1,0:T(8,128)S(1)}, f32[52,8,128]{2,1,0:T(8,128)S(1)}, u32[]{:S(2)}, u32[]{:S(2)}) collective-permute-start(f32[52,8,128]{2,1,0:T(8,128)S(1)} %get-tuple-element.22), channel_id=1, source_target_pairs={{32,0},{64,32},{96,64},{128,96},{160,128},{192,160},{224,192},{256... | collective-permute-start | bytes 638984 | tf_op jit(solution)/shard_map/ppermute | solution.py:541
  24.4 4.0 %collective-permute-start.2 = (f32[52,8,128]{2,1,0:T(8,128)S(1)}, f32[52,8,128]{2,1,0:T(8,128)S(1)}, u32[]{:S(2)}, u32[]{:S(2)}) collective-permute-start(f32[52,8,128]{2,1,0:T(8,128)S(1)} %get-tuple-element.23), channel_id=1, source_target_pairs={{0,32},{32,64},{64,96},{96,128},{128,160},{160,192},{192,224},{224... | collective-permute-start | bytes 638984 | tf_op jit(solution)/shard_map/ppermute | solution.py:540
  28.4 1.3 %collective-permute-done.3.xr_ref = f32[52,8,128]{2,1,0:T(8,128)S(1)} collective-permute-done((f32[52,8,128]{2,1,0:T(8,128)S(1)}, f32[52,8,128]{2,1,0:T(8,128)S(1)}, u32[]{:S(2)}, u32[]{:S(2)}) %collective-permute-start.3) | collective-permute-done | bytes 213024 | tf_op jit(solution)/shard_map/ppermute | solution.py:541
  29.7 1.5 %collective-permute-done.2.xl_ref = f32[52,8,128]{2,1,0:T(8,128)S(1)} collective-permute-done((f32[52,8,128]{2,1,0:T(8,128)S(1)}, f32[52,8,128]{2,1,0:T(8,128)S(1)}, u32[]{:S(2)}, u32[]{:S(2)}) %collective-permute-start.2) | collective-permute-done | bytes 213024 | tf_op jit(solution)/shard_map/ppermute | solution.py:540
  31.2 0.0 copy-done
  31.2 0.0 copy-done.4
  31.2 0.0 copy-done.5
  31.2 10.7 %krylov.1 = (f32[34,24,128]{2,1,0:T(8,128)S(1)}, f32[34,24,128]{2,1,0:T(8,128)S(1)}, f32[32,24,128]{2,1,0:T(8,128)S(1)}, f32[32,1,128]{2,1,0:T(1,128)S(1)}) custom-call(s32[1]{0:T(128)} %bitcast.odd_ref, f32[32,16,128]{2,1,0:T(8,128)S(1)} %copy-done, f32[44,8,128]{2,1,0:T(8,128)S(1)} %copy-done.4, f32[44,8,128]{2,1,0:T(8,128)S(1)} %collective-permute-done.ya_ref, ...), custom_call_target="tpu_custom_call" | custom-call | tf_op jit(solution)/shard_map/krylov/pallas_call | solution.py:402
  41.9 15.4 %all_to_all.15 = f32[32,1,128]{2,1,0:T(1,128)S(1)} all-to-all(f32[32,1,128]{2,1,0:T(1,128)S(1)} %get-tuple-element.16), channel_id=1, replica_groups=mesh['sx'=24,'sy'=32] {'sy'}, dimensions={0} | all-to-all | bytes 32768 | tf_op jit(solution)/shard_map/all_to_all | solution.py:543
  57.3 0.1 reduce_sum.9
  57.4 26.7 %all_to_all.16.parts_ref = f32[24,1,128]{2,1,0:T(1,128)S(1)} all-to-all(f32[24,1,128]{2,1,0:T(1,128)S(1)} %broadcast_in_dim.2), channel_id=1, replica_groups=mesh['sx'=24,'sy'=32] {'sx'}, dimensions={0} | all-to-all | bytes 24576 | tf_op jit(solution)/shard_map/all_to_all | solution.py:545
  84.2 0.0 copy-done.1
  84.2 1.2 %velocity_step.1 = (f32[32,16,128]{2,1,0:T(8,128)}, f32[32,3,16,128]{3,2,1,0:T(8,128)S(1)}) custom-call(f32[24,1,128]{2,1,0:T(1,128)S(1)} %all_to_all.16.parts_ref, f32[34,24,128]{2,1,0:T(8,128)S(1)} %get-tuple-element.17.d1_ref, f32[34,24,128]{2,1,0:T(8,128)S(1)} %get-tuple-element.18.e_ref, f32[32,24,128]{2,1,0:T(8,128)S(1)} %get-tuple-element.19.s_ref, ...), custom_call_target="tpu_custom_call" | custom-call | tf_op jit(solution)/shard_map/velocity_step/pallas_call | solution.py:465
  85.3 0.0 copy-start.2
  85.3 0.0 copy-start.3
  85.3 28.0 %all_to_all.17.x_ref = f32[32,1,3,16,128]{4,3,2,1,0:T(8,128)S(1)} all-to-all(f32[32,1,3,16,128]{4,3,2,1,0:T(8,128)S(1)} %bitcast.2), channel_id=1, replica_groups=mesh['sx'=24,'sy'=32] {'sy'}, dimensions={0} | all-to-all | bytes 1572864 | tf_op jit(solution)/shard_map/all_to_all | solution.py:547
  113.4 0.0 copy-done.2
  113.4 0.0 copy-done.3
  113.4 1.9 %diffuse.1 = f32[3,1,512,128]{3,2,1,0:T(8,128)} custom-call(bf16[512,512]{1,0:T(8,128)(2,1)S(1)} %copy-done.3, bf16[512,512]{1,0:T(8,128)(2,1)S(1)} %copy-done.2, f32[32,1,3,16,128]{4,3,2,1,0:T(8,128)S(1)} %all_to_all.17.x_ref), custom_call_target="tpu_custom_call" | custom-call | tf_op jit(solution)/shard_map/diffuse/pallas_call | solution.py:505
  (9 shorter events, 0.1 us)
Async XLA Ops:
  2.5 15.3 %collective-permute-start = (f32[44,8,128]{2,1,0:T(8,128)}, f32[44,8,128]{2,1,0:T(8,128)S(1)}, u32[]{:S(2)}, u32[]{:S(2)}) collective-permute-start(f32[44,8,128]{2,1,0:T(8,128)} %get-tuple-element.12.mine_ref), channel_id=1, source_target_pairs={{0,1},{2,3},{4,5},{6,7},{8,9},{10,11},{12,13},{14,15},{16,17},{18,... | collective-permute-start | bytes 540680 | tf_op jit(solution)/shard_map/ppermute | solution.py:529
  15.0 7.9 %collective-permute-start.1 = (f32[44,8,128]{2,1,0:T(8,128)}, f32[44,8,128]{2,1,0:T(8,128)S(1)}, u32[]{:S(2)}, u32[]{:S(2)}) collective-permute-start(f32[44,8,128]{2,1,0:T(8,128)} %get-tuple-element.13), channel_id=1, source_target_pairs={{1,2},{3,4},{5,6},{7,8},{9,10},{11,12},{13,14},{15,16},{17,18},{19... | collective-permute-start | bytes 540680 | tf_op jit(solution)/shard_map/ppermute | solution.py:530
  17.8 13.3 %copy-start = (f32[32,16,128]{2,1,0:T(8,128)S(1)}, f32[32,16,128]{2,1,0:T(8,128)}, u32[]{:S(2)}) copy-start(f32[32,16,128]{2,1,0:T(8,128)} %own_ref.1) | copy-start | bytes 786436
  17.9 13.3 %copy-start.4 = (f32[44,8,128]{2,1,0:T(8,128)S(1)}, f32[44,8,128]{2,1,0:T(8,128)}, u32[]{:S(2)}) copy-start(f32[44,8,128]{2,1,0:T(8,128)} %get-tuple-element.12.mine_ref) | copy-start | bytes 540676
  22.9 8.3 %copy-start.5 = (bf16[128,128]{1,0:T(8,128)(2,1)S(1)}, bf16[128,128]{1,0:T(8,128)(2,1)}, u32[]{:S(2)}) copy-start(bf16[128,128]{1,0:T(8,128)(2,1)} %constant.25.clone.spread_ref) | copy-start | bytes 98308
  22.9 61.3 %copy-start.1 = (f32[3,32,16,128]{3,2,1,0:T(8,128)S(1)}, f32[3,32,16,128]{3,2,1,0:T(8,128)}, u32[]{:S(2)}) copy-start(f32[3,32,16,128]{3,2,1,0:T(8,128)} %v_ref.1) | copy-start | bytes 2359300
  23.0 6.7 %collective-permute-start.3 = (f32[52,8,128]{2,1,0:T(8,128)S(1)}, f32[52,8,128]{2,1,0:T(8,128)S(1)}, u32[]{:S(2)}, u32[]{:S(2)}) collective-permute-start(f32[52,8,128]{2,1,0:T(8,128)S(1)} %get-tuple-element.22), channel_id=1, source_target_pairs={{32,0},{64,32},{96,64},{128,96},{160,128},{192,160},{224,192},{256... | collective-permute-start | bytes 638984 | tf_op jit(solution)/shard_map/ppermute | solution.py:541
  24.4 6.8 %collective-permute-start.2 = (f32[52,8,128]{2,1,0:T(8,128)S(1)}, f32[52,8,128]{2,1,0:T(8,128)S(1)}, u32[]{:S(2)}, u32[]{:S(2)}) collective-permute-start(f32[52,8,128]{2,1,0:T(8,128)S(1)} %get-tuple-element.23), channel_id=1, source_target_pairs={{0,32},{32,64},{64,96},{96,128},{128,160},{160,192},{192,224},{224... | collective-permute-start | bytes 638984 | tf_op jit(solution)/shard_map/ppermute | solution.py:540
  85.3 28.1 %copy-start.2 = (bf16[512,512]{1,0:T(8,128)(2,1)S(1)}, bf16[512,512]{1,0:T(8,128)(2,1)}, u32[]{:S(2)}) copy-start(bf16[512,512]{1,0:T(8,128)(2,1)} %constant.27.clone.low_ref) | copy-start | bytes 1572868
  85.3 28.1 %copy-start.3 = (bf16[512,512]{1,0:T(8,128)(2,1)S(1)}, bf16[512,512]{1,0:T(8,128)(2,1)}, u32[]{:S(2)}) copy-start(bf16[512,512]{1,0:T(8,128)(2,1)} %constant.26.clone.high_ref) | copy-start | bytes 1572868
